TPU v7x, 128 devices: a whole 4x4x4 slice. The times are simulated.
128 devices in a mesh: stream: 32 (over z, y, x_lo), span: 4 (over x_hi, core).
Axes of the slice: x: 4 (x_hi: 2, x_lo: 2; x = x_hi * 2 + x_lo), y: 4, z: 4, core: 2. Of those that a mesh axis runs over, the one named last changes fastest.
Arguments:
- rhs: float32 [128, 4, 64, 4096], P('stream', None, None, 'span'), may hold values from -0.15625 to 0.15625
- lagged: float32 [128, 4, 64, 4096], P('stream', None, None, 'span'), may hold values from -6 to 6
- face_types: int32 [3, 128, 4096], P(None, 'stream', 'span'), may hold values from 0 to 5
- stream_scale: float32 [128, 4096], P('stream', 'span'), may hold values from 1 to 4
- span_scale: float32 [2, 128, 4096], P(None, 'stream', 'span'), may hold values from 0.004 to 0.016
- absorb: float32 [128, 4096], P('stream', 'span'), may hold values from 0.002 to 0.008
- up_blocks: float32 [6, 64, 64], replicated, may hold values from -1 to 0.03
- down_blocks: float32 [6, 64, 64], replicated, may hold values from -1 to 0.03
- diag_inverse: float32 [64, 64], replicated, may hold values from -0.012 to 1
Outputs:
- increment: float32 [128, 4, 64, 4096], P('stream', None, None, 'span')
All inputs are finite; a program needn't handle non-finite values.
Results may differ from a plain program's by a relative error of at most 0.00023.
Values sent between devices are 32-bit elements; how exact they have to be, the bound alone decides.
A program may use at most 64 MiB of HBM per device.

v0:
```python
import jax
import jax.numpy as jnp
from jax import lax
from jax.sharding import PartitionSpec as P

precise = lax.Precision.HIGHEST


def padded_2(block, sides, width):
    for axis, dim in sides:
        count = lax.axis_size(axis)
        forward = [(i, i + 1) for i in range(count - 1)]
        backward = [(target, source) for source, target in forward]
        low = lax.ppermute(
            lax.slice_in_dim(block, block.shape[dim] - width, None, axis=dim), axis, forward
        )
        high = lax.ppermute(lax.slice_in_dim(block, 0, width, axis=dim), axis, backward)
        block = jnp.concatenate([low, block, high], axis=dim)
    return block


def passed_along(block, axis, distance):
    devices = range(lax.axis_size(axis))
    route = [(i - distance, i) for i in devices if i - distance in devices]
    return lax.ppermute(block, axis, route)


def typed_product(blocks_table, type_ids, state_in):
    products = jnp.einsum("tpq,rqw->trpw", blocks_table, state_in, precision=precise)
    kinds = jnp.arange(blocks_table.shape[0], dtype=jnp.int32)
    selector = (type_ids[None, :] == kinds[:, None]).astype(jnp.float32)
    return jnp.sum(products * selector[:, None, None, :], axis=0)


def inverse_product(diag_inverse, balance, denom_row):
    return jnp.einsum("pq,rqw->rpw", diag_inverse, balance, precision=precise) / denom_row


def span_block(padded, face_types, span_scale, up_blocks, offset, breadth):
    lower_side = lax.dynamic_slice_in_dim(padded, offset, breadth, 3)
    upper_side = lax.dynamic_slice_in_dim(padded, offset + 2, breadth, 3)
    lower_types = face_types[1]
    upper_types = face_types[2]
    lower_scale = span_scale[0]
    upper_scale = span_scale[1]
    results = []
    for row_index in range(padded.shape[0]):
        lower_term = lower_scale[row_index] * typed_product(
            up_blocks, lower_types[row_index], lower_side[row_index]
        )
        upper_term = upper_scale[row_index] * typed_product(
            up_blocks, upper_types[row_index], upper_side[row_index]
        )
        results.append(lower_term + upper_term)
    return jnp.stack(results)


def per_device(
    rhs, lagged, face_types, stream_scale, span_scale, absorb, up_blocks, down_blocks, diag_inverse
):
    height = rhs.shape[0]
    columns = rhs.shape[3]
    padded = padded_2(lagged, (("span", 3),), 1)
    denominator = stream_scale + span_scale[0] + span_scale[1] + absorb
    blocks = 4
    breadth = columns // blocks
    length = lax.axis_size("stream")
    position = lax.axis_index("stream")
    whole_span = span_block(padded, face_types, span_scale, up_blocks, 0, columns)

    def span_part(offset):
        return lax.dynamic_slice_in_dim(whole_span, offset, breadth, 3)

    def forward_block(forward_part, inflow, offset):
        rhs_block = lax.dynamic_slice_in_dim(rhs, offset, breadth, 3)
        type_block = lax.dynamic_slice_in_dim(face_types[0], offset, breadth, 1)
        scale_block = lax.dynamic_slice_in_dim(stream_scale, offset, breadth, 1)
        denom_block = lax.dynamic_slice_in_dim(denominator, offset, breadth, 1)
        span_terms = span_part(offset)
        previous = inflow
        results = []
        for row_index in range(height):
            balance = (
                rhs_block[row_index]
                - span_terms[row_index]
                - scale_block[row_index] * typed_product(up_blocks, type_block[row_index], previous)
            )
            previous = inverse_product(diag_inverse, balance, denom_block[row_index])
            results.append(previous)
        forward_part = lax.dynamic_update_slice_in_dim(forward_part, jnp.stack(results), offset, 3)
        return (forward_part, previous)

    def forward_step(wave_step, state):
        forward_part, inflow = state
        block_index = wave_step - position
        active = (block_index >= 0) & (block_index < blocks)
        offset = jnp.clip(block_index, 0, blocks - 1) * breadth

        def forward_working(forward_part, inflow):
            return forward_block(forward_part, inflow, offset)

        def forward_waiting(forward_part, inflow):
            return (forward_part, jnp.zeros_like(inflow))

        forward_part, outflow = lax.cond(
            active, forward_working, forward_waiting, forward_part, inflow
        )
        inflow = passed_along(outflow, "stream", 1)
        return (forward_part, inflow)

    front_zero = jnp.zeros((rhs.shape[1], rhs.shape[2], breadth), jnp.float32)
    forward_part, unused = lax.fori_loop(
        0, length + blocks - 1, forward_step, (jnp.zeros_like(rhs), front_zero)
    )

    def backward_block(increment, inflow, offset):
        part_block = lax.dynamic_slice_in_dim(forward_part, offset, breadth, 3)
        type_block = lax.dynamic_slice_in_dim(face_types[0], offset, breadth, 1)
        scale_block = lax.dynamic_slice_in_dim(stream_scale, offset, breadth, 1)
        denom_block = lax.dynamic_slice_in_dim(denominator, offset, breadth, 1)
        carried = inflow
        results = []
        for row_index in reversed(range(height)):
            solved = part_block[row_index] - inverse_product(
                diag_inverse, carried, denom_block[row_index]
            )
            carried = scale_block[row_index] * typed_product(
                down_blocks, type_block[row_index], solved
            )
            results.append(solved)
        ordered = results[::-1]
        increment = lax.dynamic_update_slice_in_dim(increment, jnp.stack(ordered), offset, 3)
        return (increment, carried)

    def backward_step(wave_step, state):
        increment, inflow = state
        block_index = wave_step - (length - 1 - position)
        active = (block_index >= 0) & (block_index < blocks)
        offset = jnp.clip(block_index, 0, blocks - 1) * breadth

        def backward_working(increment, inflow):
            return backward_block(increment, inflow, offset)

        def backward_waiting(increment, inflow):
            return (increment, jnp.zeros_like(inflow))

        increment, outflow = lax.cond(active, backward_working, backward_waiting, increment, inflow)
        inflow = passed_along(outflow, "stream", -1)
        return (increment, inflow)

    increment, unused_two = lax.fori_loop(
        0, length + blocks - 1, backward_step, (jnp.zeros_like(rhs), front_zero)
    )
    return increment


def solution(mesh):
    return jax.shard_map(
        per_device,
        mesh=mesh,
        in_specs=(
            P("stream", None, None, "span"),
            P("stream", None, None, "span"),
            P(None, "stream", "span"),
            P("stream", "span"),
            P(None, "stream", "span"),
            P("stream", "span"),
            P(),
            P(),
            P(),
        ),
        out_specs=P("stream", None, None, "span"),
        check_vma=False,
    )
```

profile of v0, /device:TPU:0, one launch (start us, length us, event | category | flops | bytes accessed | tf_op | source)
XLA Modules:
  0.0 1602.6 jit_solution(13361241880145761488)
XLA Ops:
  72.1 588.2 %while.38 = (s32[]{:T(128)}, f32[4,4,64,1024]{3,2,1,0:T(8,128)}, f32[4,64,256]{2,1,0:T(8,128)S(1)}, s32[]{:T(128)}, f32[4,4,64,1024]{3,2,1,0:T(8,128)}, /*index=...) while((s32[]{:T(128)}, f32[4,4,64,1024]{3,2,1,0:T(8,128)}, ...), condition=%wide.region_15.16_spmd, body=%wide.region_8.15_spmd.sunk | while | flops 1414017024 | bytes 10015197 | solution.py:112
  72.1 14.5 conditional.4
  92.8 14.4 conditional.4
  117.6 14.3 conditional.4
  143.1 14.4 conditional.4
  168.3 17.9 %collective-permute-start = (f32[4,64,256]{2,1,0:T(8,128)}, f32[4,64,256]{2,1,0:T(8,128)S(1)}, u32[]{:S(2)}, u32[]{:S(2)}) collective-permute-start(f32[4,64,256]{2,1,0:T(8,128)} %get-tuple-element.766), channel_id=1, source_target_pairs={{0,4},{4,8},{8,12},{12,16},{16,20},{20,24},{24,28},{28,32},{32,36}... | collective-permute-start | bytes 786440 | tf_op jit(solution)/shard_map/while/body/eval_jaxpr/ppermute | solution.py:25
  202.1 18.8 %collective-permute-start = (f32[4,64,256]{2,1,0:T(8,128)}, f32[4,64,256]{2,1,0:T(8,128)S(1)}, u32[]{:S(2)}, u32[]{:S(2)}) collective-permute-start(f32[4,64,256]{2,1,0:T(8,128)} %get-tuple-element.766), channel_id=1, source_target_pairs={{0,4},{4,8},{8,12},{12,16},{16,20},{20,24},{24,28},{28,32},{32,36}... | collective-permute-start | bytes 786440 | tf_op jit(solution)/shard_map/while/body/eval_jaxpr/ppermute | solution.py:25
  236.0 15.0 collective-permute-start
  265.9 17.0 %collective-permute-start = (f32[4,64,256]{2,1,0:T(8,128)}, f32[4,64,256]{2,1,0:T(8,128)S(1)}, u32[]{:S(2)}, u32[]{:S(2)}) collective-permute-start(f32[4,64,256]{2,1,0:T(8,128)} %get-tuple-element.766), channel_id=1, source_target_pairs={{0,4},{4,8},{8,12},{12,16},{16,20},{20,24},{24,28},{28,32},{32,36}... | collective-permute-start | bytes 786440 | tf_op jit(solution)/shard_map/while/body/eval_jaxpr/ppermute | solution.py:25
  297.8 16.3 %collective-permute-start = (f32[4,64,256]{2,1,0:T(8,128)}, f32[4,64,256]{2,1,0:T(8,128)S(1)}, u32[]{:S(2)}, u32[]{:S(2)}) collective-permute-start(f32[4,64,256]{2,1,0:T(8,128)} %get-tuple-element.766), channel_id=1, source_target_pairs={{0,4},{4,8},{8,12},{12,16},{16,20},{20,24},{24,28},{28,32},{32,36}... | collective-permute-start | bytes 786440 | tf_op jit(solution)/shard_map/while/body/eval_jaxpr/ppermute | solution.py:25
  330.3 19.8 %collective-permute-start = (f32[4,64,256]{2,1,0:T(8,128)}, f32[4,64,256]{2,1,0:T(8,128)S(1)}, u32[]{:S(2)}, u32[]{:S(2)}) collective-permute-start(f32[4,64,256]{2,1,0:T(8,128)} %get-tuple-element.766), channel_id=1, source_target_pairs={{0,4},{4,8},{8,12},{12,16},{16,20},{20,24},{24,28},{28,32},{32,36}... | collective-permute-start | bytes 786440 | tf_op jit(solution)/shard_map/while/body/eval_jaxpr/ppermute | solution.py:25
  366.5 11.4 collective-permute-start
  394.7 26.6 %collective-permute-start = (f32[4,64,256]{2,1,0:T(8,128)}, f32[4,64,256]{2,1,0:T(8,128)S(1)}, u32[]{:S(2)}, u32[]{:S(2)}) collective-permute-start(f32[4,64,256]{2,1,0:T(8,128)} %get-tuple-element.766), channel_id=1, source_target_pairs={{0,4},{4,8},{8,12},{12,16},{16,20},{20,24},{24,28},{28,32},{32,36}... | collective-permute-start | bytes 786440 | tf_op jit(solution)/shard_map/while/body/eval_jaxpr/ppermute | solution.py:25
  453.7 14.5 collective-permute-start
  483.2 12.0 collective-permute-start
  512.3 12.8 collective-permute-start
  567.7 14.6 collective-permute-start
  598.3 14.5 collective-permute-start
  627.9 12.7 collective-permute-start
  645.5 10.6 collective-permute-start
  662.8 939.5 %while.39 = (s32[]{:T(128)}, f32[4,4,64,1024]{3,2,1,0:T(8,128)}, f32[4,64,256]{2,1,0:T(8,128)S(1)}, s32[]{:T(128)}, f32[4,4,64,1024]{3,2,1,0:T(8,128)}, /*index=...) while((s32[]{:T(128)}, f32[4,4,64,1024]{3,2,1,0:T(8,128)}, ...), condition=%wide.region_23.24_spmd, body=%wide.region_16.23_spmd.sunk | while | flops 1413754880 | bytes 9490893 | solution.py:151
  664.4 23.0 %collective-permute-done.1 = f32[4,64,256]{2,1,0:T(8,128)S(1)} collective-permute-done((f32[4,64,256]{2,1,0:T(8,128)S(1)}, f32[4,64,256]{2,1,0:T(8,128)S(1)}, u32[]{:S(2)}, u32[]{:S(2)}) %collective-permute-start.1) | collective-permute-done | bytes 262176 | tf_op jit(solution)/shard_map/while/body/eval_jaxpr/ppermute | solution.py:25
  698.2 18.5 %collective-permute-done.1 = f32[4,64,256]{2,1,0:T(8,128)S(1)} collective-permute-done((f32[4,64,256]{2,1,0:T(8,128)S(1)}, f32[4,64,256]{2,1,0:T(8,128)S(1)}, u32[]{:S(2)}, u32[]{:S(2)}) %collective-permute-start.1) | collective-permute-done | bytes 262176 | tf_op jit(solution)/shard_map/while/body/eval_jaxpr/ppermute | solution.py:25
  726.8 27.1 %collective-permute-done.1 = f32[4,64,256]{2,1,0:T(8,128)S(1)} collective-permute-done((f32[4,64,256]{2,1,0:T(8,128)S(1)}, f32[4,64,256]{2,1,0:T(8,128)S(1)}, u32[]{:S(2)}, u32[]{:S(2)}) %collective-permute-start.1) | collective-permute-done | bytes 262176 | tf_op jit(solution)/shard_map/while/body/eval_jaxpr/ppermute | solution.py:25
  755.2 10.5 collective-permute-done.1
  767.0 13.1 collective-permute-done.1
  781.5 14.8 collective-permute-done.1
  806.7 17.8 %collective-permute-done.1 = f32[4,64,256]{2,1,0:T(8,128)S(1)} collective-permute-done((f32[4,64,256]{2,1,0:T(8,128)S(1)}, f32[4,64,256]{2,1,0:T(8,128)S(1)}, u32[]{:S(2)}, u32[]{:S(2)}) %collective-permute-start.1) | collective-permute-done | bytes 262176 | tf_op jit(solution)/shard_map/while/body/eval_jaxpr/ppermute | solution.py:25
  825.9 12.5 collective-permute-done.1
  839.8 12.4 collective-permute-done.1
  864.4 10.6 collective-permute-done.1
  876.3 18.1 %collective-permute-done.1 = f32[4,64,256]{2,1,0:T(8,128)S(1)} collective-permute-done((f32[4,64,256]{2,1,0:T(8,128)S(1)}, f32[4,64,256]{2,1,0:T(8,128)S(1)}, u32[]{:S(2)}, u32[]{:S(2)}) %collective-permute-start.1) | collective-permute-done | bytes 262176 | tf_op jit(solution)/shard_map/while/body/eval_jaxpr/ppermute | solution.py:25
  895.8 21.1 %collective-permute-done.1 = f32[4,64,256]{2,1,0:T(8,128)S(1)} collective-permute-done((f32[4,64,256]{2,1,0:T(8,128)S(1)}, f32[4,64,256]{2,1,0:T(8,128)S(1)}, u32[]{:S(2)}, u32[]{:S(2)}) %collective-permute-start.1) | collective-permute-done | bytes 262176 | tf_op jit(solution)/shard_map/while/body/eval_jaxpr/ppermute | solution.py:25
  928.9 19.1 %collective-permute-done.1 = f32[4,64,256]{2,1,0:T(8,128)S(1)} collective-permute-done((f32[4,64,256]{2,1,0:T(8,128)S(1)}, f32[4,64,256]{2,1,0:T(8,128)S(1)}, u32[]{:S(2)}, u32[]{:S(2)}) %collective-permute-start.1) | collective-permute-done | bytes 262176 | tf_op jit(solution)/shard_map/while/body/eval_jaxpr/ppermute | solution.py:25
  958.3 20.2 %collective-permute-done.1 = f32[4,64,256]{2,1,0:T(8,128)S(1)} collective-permute-done((f32[4,64,256]{2,1,0:T(8,128)S(1)}, f32[4,64,256]{2,1,0:T(8,128)S(1)}, u32[]{:S(2)}, u32[]{:S(2)}) %collective-permute-start.1) | collective-permute-done | bytes 262176 | tf_op jit(solution)/shard_map/while/body/eval_jaxpr/ppermute | solution.py:25
  979.8 10.9 collective-permute-done.1
  992.0 13.2 collective-permute-done.1
  1006.5 13.7 collective-permute-done.1
  1021.6 13.5 collective-permute-done.1
  1036.4 17.4 %collective-permute-done.1 = f32[4,64,256]{2,1,0:T(8,128)S(1)} collective-permute-done((f32[4,64,256]{2,1,0:T(8,128)S(1)}, f32[4,64,256]{2,1,0:T(8,128)S(1)}, u32[]{:S(2)}, u32[]{:S(2)}) %collective-permute-start.1) | collective-permute-done | bytes 262176 | tf_op jit(solution)/shard_map/while/body/eval_jaxpr/ppermute | solution.py:25
  1055.2 12.9 collective-permute-done.1
  1113.9 393.4 %collective-permute-done.1 = f32[4,64,256]{2,1,0:T(8,128)S(1)} collective-permute-done((f32[4,64,256]{2,1,0:T(8,128)S(1)}, f32[4,64,256]{2,1,0:T(8,128)S(1)}, u32[]{:S(2)}, u32[]{:S(2)}) %collective-permute-start.1) | collective-permute-done | bytes 262176 | tf_op jit(solution)/shard_map/while/body/eval_jaxpr/ppermute | solution.py:25
  1507.2 12.3 conditional.5
  1530.3 12.3 conditional.5
  1544.0 13.8 collective-permute-done.1
  1557.8 12.3 conditional.5
  1571.5 10.3 collective-permute-done.1
  1581.8 12.3 conditional.5
  (403 shorter events, 649.8 us)
Async XLA Ops:
  1.4 12.0 collective-permute-start.3
  2.7 39.7 %collective-permute-start.2 = (f32[4,4,64,1]{3,2,1,0:T(8,128)S(1)}, f32[4,4,64,1]{3,2,1,0:T(8,128)S(1)}, u32[]{:S(2)}, u32[]{:S(2)}) collective-permute-start(f32[4,4,64,1]{3,2,1,0:T(8,128)S(1)} %get-tuple-element.621), channel_id=1, source_target_pairs={{0,1},{1,2},{2,3},{4,5},{5,6},{6,7},{8,9},{9,10},{10,11},{12,13},{... | collective-permute-start | bytes 12296 | tf_op jit(solution)/shard_map/ppermute | solution.py:14
  131.9 11.1 collective-permute-start
  168.3 23.0 %collective-permute-start = (f32[4,64,256]{2,1,0:T(8,128)}, f32[4,64,256]{2,1,0:T(8,128)S(1)}, u32[]{:S(2)}, u32[]{:S(2)}) collective-permute-start(f32[4,64,256]{2,1,0:T(8,128)} %get-tuple-element.766), channel_id=1, source_target_pairs={{0,4},{4,8},{8,12},{12,16},{16,20},{20,24},{24,28},{28,32},{32,36}... | collective-permute-start | bytes 786440 | tf_op jit(solution)/shard_map/while/body/eval_jaxpr/ppermute | solution.py:25
  202.1 23.0 %collective-permute-start = (f32[4,64,256]{2,1,0:T(8,128)}, f32[4,64,256]{2,1,0:T(8,128)S(1)}, u32[]{:S(2)}, u32[]{:S(2)}) collective-permute-start(f32[4,64,256]{2,1,0:T(8,128)} %get-tuple-element.766), channel_id=1, source_target_pairs={{0,4},{4,8},{8,12},{12,16},{16,20},{20,24},{24,28},{28,32},{32,36}... | collective-permute-start | bytes 786440 | tf_op jit(solution)/shard_map/while/body/eval_jaxpr/ppermute | solution.py:25
  236.0 19.2 %collective-permute-start = (f32[4,64,256]{2,1,0:T(8,128)}, f32[4,64,256]{2,1,0:T(8,128)S(1)}, u32[]{:S(2)}, u32[]{:S(2)}) collective-permute-start(f32[4,64,256]{2,1,0:T(8,128)} %get-tuple-element.766), channel_id=1, source_target_pairs={{0,4},{4,8},{8,12},{12,16},{16,20},{20,24},{24,28},{28,32},{32,36}... | collective-permute-start | bytes 786440 | tf_op jit(solution)/shard_map/while/body/eval_jaxpr/ppermute | solution.py:25
  265.9 21.6 %collective-permute-start = (f32[4,64,256]{2,1,0:T(8,128)}, f32[4,64,256]{2,1,0:T(8,128)S(1)}, u32[]{:S(2)}, u32[]{:S(2)}) collective-permute-start(f32[4,64,256]{2,1,0:T(8,128)} %get-tuple-element.766), channel_id=1, source_target_pairs={{0,4},{4,8},{8,12},{12,16},{16,20},{20,24},{24,28},{28,32},{32,36}... | collective-permute-start | bytes 786440 | tf_op jit(solution)/shard_map/while/body/eval_jaxpr/ppermute | solution.py:25
  297.8 22.5 %collective-permute-start = (f32[4,64,256]{2,1,0:T(8,128)}, f32[4,64,256]{2,1,0:T(8,128)S(1)}, u32[]{:S(2)}, u32[]{:S(2)}) collective-permute-start(f32[4,64,256]{2,1,0:T(8,128)} %get-tuple-element.766), channel_id=1, source_target_pairs={{0,4},{4,8},{8,12},{12,16},{16,20},{20,24},{24,28},{28,32},{32,36}... | collective-permute-start | bytes 786440 | tf_op jit(solution)/shard_map/while/body/eval_jaxpr/ppermute | solution.py:25
  330.3 26.0 %collective-permute-start = (f32[4,64,256]{2,1,0:T(8,128)}, f32[4,64,256]{2,1,0:T(8,128)S(1)}, u32[]{:S(2)}, u32[]{:S(2)}) collective-permute-start(f32[4,64,256]{2,1,0:T(8,128)} %get-tuple-element.766), channel_id=1, source_target_pairs={{0,4},{4,8},{8,12},{12,16},{16,20},{20,24},{24,28},{28,32},{32,36}... | collective-permute-start | bytes 786440 | tf_op jit(solution)/shard_map/while/body/eval_jaxpr/ppermute | solution.py:25
  366.5 18.4 %collective-permute-start = (f32[4,64,256]{2,1,0:T(8,128)}, f32[4,64,256]{2,1,0:T(8,128)S(1)}, u32[]{:S(2)}, u32[]{:S(2)}) collective-permute-start(f32[4,64,256]{2,1,0:T(8,128)} %get-tuple-element.766), channel_id=1, source_target_pairs={{0,4},{4,8},{8,12},{12,16},{16,20},{20,24},{24,28},{28,32},{32,36}... | collective-permute-start | bytes 786440 | tf_op jit(solution)/shard_map/while/body/eval_jaxpr/ppermute | solution.py:25
  394.7 31.4 %collective-permute-start = (f32[4,64,256]{2,1,0:T(8,128)}, f32[4,64,256]{2,1,0:T(8,128)S(1)}, u32[]{:S(2)}, u32[]{:S(2)}) collective-permute-start(f32[4,64,256]{2,1,0:T(8,128)} %get-tuple-element.766), channel_id=1, source_target_pairs={{0,4},{4,8},{8,12},{12,16},{16,20},{20,24},{24,28},{28,32},{32,36}... | collective-permute-start | bytes 786440 | tf_op jit(solution)/shard_map/while/body/eval_jaxpr/ppermute | solution.py:25
  426.9 12.7 collective-permute-start
  440.3 12.8 collective-permute-start
  453.7 18.7 %collective-permute-start = (f32[4,64,256]{2,1,0:T(8,128)}, f32[4,64,256]{2,1,0:T(8,128)S(1)}, u32[]{:S(2)}, u32[]{:S(2)}) collective-permute-start(f32[4,64,256]{2,1,0:T(8,128)} %get-tuple-element.766), channel_id=1, source_target_pairs={{0,4},{4,8},{8,12},{12,16},{16,20},{20,24},{24,28},{28,32},{32,36}... | collective-permute-start | bytes 786440 | tf_op jit(solution)/shard_map/while/body/eval_jaxpr/ppermute | solution.py:25
  483.2 16.2 %collective-permute-start = (f32[4,64,256]{2,1,0:T(8,128)}, f32[4,64,256]{2,1,0:T(8,128)S(1)}, u32[]{:S(2)}, u32[]{:S(2)}) collective-permute-start(f32[4,64,256]{2,1,0:T(8,128)} %get-tuple-element.766), channel_id=1, source_target_pairs={{0,4},{4,8},{8,12},{12,16},{16,20},{20,24},{24,28},{28,32},{32,36}... | collective-permute-start | bytes 786440 | tf_op jit(solution)/shard_map/while/body/eval_jaxpr/ppermute | solution.py:25
  500.1 11.5 collective-permute-start
  512.3 17.0 %collective-permute-start = (f32[4,64,256]{2,1,0:T(8,128)}, f32[4,64,256]{2,1,0:T(8,128)S(1)}, u32[]{:S(2)}, u32[]{:S(2)}) collective-permute-start(f32[4,64,256]{2,1,0:T(8,128)} %get-tuple-element.766), channel_id=1, source_target_pairs={{0,4},{4,8},{8,12},{12,16},{16,20},{20,24},{24,28},{28,32},{32,36}... | collective-permute-start | bytes 786440 | tf_op jit(solution)/shard_map/while/body/eval_jaxpr/ppermute | solution.py:25
  541.5 13.2 collective-permute-start
  555.4 11.6 collective-permute-start
  567.7 18.8 %collective-permute-start = (f32[4,64,256]{2,1,0:T(8,128)}, f32[4,64,256]{2,1,0:T(8,128)S(1)}, u32[]{:S(2)}, u32[]{:S(2)}) collective-permute-start(f32[4,64,256]{2,1,0:T(8,128)} %get-tuple-element.766), channel_id=1, source_target_pairs={{0,4},{4,8},{8,12},{12,16},{16,20},{20,24},{24,28},{28,32},{32,36}... | collective-permute-start | bytes 786440 | tf_op jit(solution)/shard_map/while/body/eval_jaxpr/ppermute | solution.py:25
  598.3 18.7 %collective-permute-start = (f32[4,64,256]{2,1,0:T(8,128)}, f32[4,64,256]{2,1,0:T(8,128)S(1)}, u32[]{:S(2)}, u32[]{:S(2)}) collective-permute-start(f32[4,64,256]{2,1,0:T(8,128)} %get-tuple-element.766), channel_id=1, source_target_pairs={{0,4},{4,8},{8,12},{12,16},{16,20},{20,24},{24,28},{28,32},{32,36}... | collective-permute-start | bytes 786440 | tf_op jit(solution)/shard_map/while/body/eval_jaxpr/ppermute | solution.py:25
  627.9 16.9 %collective-permute-start = (f32[4,64,256]{2,1,0:T(8,128)}, f32[4,64,256]{2,1,0:T(8,128)S(1)}, u32[]{:S(2)}, u32[]{:S(2)}) collective-permute-start(f32[4,64,256]{2,1,0:T(8,128)} %get-tuple-element.766), channel_id=1, source_target_pairs={{0,4},{4,8},{8,12},{12,16},{16,20},{20,24},{24,28},{28,32},{32,36}... | collective-permute-start | bytes 786440 | tf_op jit(solution)/shard_map/while/body/eval_jaxpr/ppermute | solution.py:25
  645.5 14.7 collective-permute-start
  663.1 24.3 %collective-permute-start.1 = (f32[4,64,256]{2,1,0:T(8,128)S(1)}, f32[4,64,256]{2,1,0:T(8,128)S(1)}, u32[]{:S(2)}, u32[]{:S(2)}) collective-permute-start(f32[4,64,256]{2,1,0:T(8,128)S(1)} %get-tuple-element.778), channel_id=1, source_target_pairs={{4,0},{8,4},{12,8},{16,12},{20,16},{24,20},{28,24},{32,28},{36,32}... | collective-permute-start | bytes 786440 | tf_op jit(solution)/shard_map/while/body/eval_jaxpr/ppermute | solution.py:25
  696.9 19.8 %collective-permute-start.1 = (f32[4,64,256]{2,1,0:T(8,128)S(1)}, f32[4,64,256]{2,1,0:T(8,128)S(1)}, u32[]{:S(2)}, u32[]{:S(2)}) collective-permute-start(f32[4,64,256]{2,1,0:T(8,128)S(1)} %get-tuple-element.778), channel_id=1, source_target_pairs={{4,0},{8,4},{12,8},{16,12},{20,16},{24,20},{28,24},{32,28},{36,32}... | collective-permute-start | bytes 786440 | tf_op jit(solution)/shard_map/while/body/eval_jaxpr/ppermute | solution.py:25
  725.5 28.4 %collective-permute-start.1 = (f32[4,64,256]{2,1,0:T(8,128)S(1)}, f32[4,64,256]{2,1,0:T(8,128)S(1)}, u32[]{:S(2)}, u32[]{:S(2)}) collective-permute-start(f32[4,64,256]{2,1,0:T(8,128)S(1)} %get-tuple-element.778), channel_id=1, source_target_pairs={{4,0},{8,4},{12,8},{16,12},{20,16},{24,20},{28,24},{32,28},{36,32}... | collective-permute-start | bytes 786440 | tf_op jit(solution)/shard_map/while/body/eval_jaxpr/ppermute | solution.py:25
  753.9 11.8 collective-permute-start.1
  765.7 14.4 collective-permute-start.1
  780.2 16.1 %collective-permute-start.1 = (f32[4,64,256]{2,1,0:T(8,128)S(1)}, f32[4,64,256]{2,1,0:T(8,128)S(1)}, u32[]{:S(2)}, u32[]{:S(2)}) collective-permute-start(f32[4,64,256]{2,1,0:T(8,128)S(1)} %get-tuple-element.778), channel_id=1, source_target_pairs={{4,0},{8,4},{12,8},{16,12},{20,16},{24,20},{28,24},{32,28},{36,32}... | collective-permute-start | bytes 786440 | tf_op jit(solution)/shard_map/while/body/eval_jaxpr/ppermute | solution.py:25
  805.4 19.1 %collective-permute-start.1 = (f32[4,64,256]{2,1,0:T(8,128)S(1)}, f32[4,64,256]{2,1,0:T(8,128)S(1)}, u32[]{:S(2)}, u32[]{:S(2)}) collective-permute-start(f32[4,64,256]{2,1,0:T(8,128)S(1)} %get-tuple-element.778), channel_id=1, source_target_pairs={{4,0},{8,4},{12,8},{16,12},{20,16},{24,20},{28,24},{32,28},{36,32}... | collective-permute-start | bytes 786440 | tf_op jit(solution)/shard_map/while/body/eval_jaxpr/ppermute | solution.py:25
  824.6 13.8 collective-permute-start.1
  838.5 13.7 collective-permute-start.1
  863.1 11.9 collective-permute-start.1
  875.0 19.4 %collective-permute-start.1 = (f32[4,64,256]{2,1,0:T(8,128)S(1)}, f32[4,64,256]{2,1,0:T(8,128)S(1)}, u32[]{:S(2)}, u32[]{:S(2)}) collective-permute-start(f32[4,64,256]{2,1,0:T(8,128)S(1)} %get-tuple-element.778), channel_id=1, source_target_pairs={{4,0},{8,4},{12,8},{16,12},{20,16},{24,20},{28,24},{32,28},{36,32}... | collective-permute-start | bytes 786440 | tf_op jit(solution)/shard_map/while/body/eval_jaxpr/ppermute | solution.py:25
  894.5 22.4 %collective-permute-start.1 = (f32[4,64,256]{2,1,0:T(8,128)S(1)}, f32[4,64,256]{2,1,0:T(8,128)S(1)}, u32[]{:S(2)}, u32[]{:S(2)}) collective-permute-start(f32[4,64,256]{2,1,0:T(8,128)S(1)} %get-tuple-element.778), channel_id=1, source_target_pairs={{4,0},{8,4},{12,8},{16,12},{20,16},{24,20},{28,24},{32,28},{36,32}... | collective-permute-start | bytes 786440 | tf_op jit(solution)/shard_map/while/body/eval_jaxpr/ppermute | solution.py:25
  927.6 20.4 %collective-permute-start.1 = (f32[4,64,256]{2,1,0:T(8,128)S(1)}, f32[4,64,256]{2,1,0:T(8,128)S(1)}, u32[]{:S(2)}, u32[]{:S(2)}) collective-permute-start(f32[4,64,256]{2,1,0:T(8,128)S(1)} %get-tuple-element.778), channel_id=1, source_target_pairs={{4,0},{8,4},{12,8},{16,12},{20,16},{24,20},{28,24},{32,28},{36,32}... | collective-permute-start | bytes 786440 | tf_op jit(solution)/shard_map/while/body/eval_jaxpr/ppermute | solution.py:25
  956.9 21.5 %collective-permute-start.1 = (f32[4,64,256]{2,1,0:T(8,128)S(1)}, f32[4,64,256]{2,1,0:T(8,128)S(1)}, u32[]{:S(2)}, u32[]{:S(2)}) collective-permute-start(f32[4,64,256]{2,1,0:T(8,128)S(1)} %get-tuple-element.778), channel_id=1, source_target_pairs={{4,0},{8,4},{12,8},{16,12},{20,16},{24,20},{28,24},{32,28},{36,32}... | collective-permute-start | bytes 786440 | tf_op jit(solution)/shard_map/while/body/eval_jaxpr/ppermute | solution.py:25
  978.5 12.2 collective-permute-start.1
  990.7 14.5 collective-permute-start.1
  1005.2 15.0 collective-permute-start.1
  1020.3 14.8 collective-permute-start.1
  1035.1 18.7 %collective-permute-start.1 = (f32[4,64,256]{2,1,0:T(8,128)S(1)}, f32[4,64,256]{2,1,0:T(8,128)S(1)}, u32[]{:S(2)}, u32[]{:S(2)}) collective-permute-start(f32[4,64,256]{2,1,0:T(8,128)S(1)} %get-tuple-element.778), channel_id=1, source_target_pairs={{4,0},{8,4},{12,8},{16,12},{20,16},{24,20},{28,24},{32,28},{36,32}... | collective-permute-start | bytes 786440 | tf_op jit(solution)/shard_map/while/body/eval_jaxpr/ppermute | solution.py:25
  1053.9 14.2 collective-permute-start.1
  1089.9 11.3 collective-permute-start.1
  1101.2 11.3 collective-permute-start.1
  1112.5 394.7 %collective-permute-start.1 = (f32[4,64,256]{2,1,0:T(8,128)S(1)}, f32[4,64,256]{2,1,0:T(8,128)S(1)}, u32[]{:S(2)}, u32[]{:S(2)}) collective-permute-start(f32[4,64,256]{2,1,0:T(8,128)S(1)} %get-tuple-element.778), channel_id=1, source_target_pairs={{4,0},{8,4},{12,8},{16,12},{20,16},{24,20},{28,24},{32,28},{36,32}... | collective-permute-start | bytes 786440 | tf_op jit(solution)/shard_map/while/body/eval_jaxpr/ppermute | solution.py:25
  1542.7 15.2 collective-permute-start.1
  1570.2 11.6 collective-permute-start.1
  (30 other events, 264.7 us)
where the time goes:
time: 1610 us; the launch traced here: 1600 us
  waiting for transfers between devices  1010 us (63%)
  starting transfers between devices  394 us (24%)
  matrix products  143 us (9%)
  local copies, waits for them, and re-layouts  37.9 us (2%)
  other arithmetic  17.3 us (1%)
    ppermute x70, waiting for transfers between devices, passed_along(): return lax.ppermute(block, axis, route)  1010 us
    ppermute x70, starting transfers between devices, passed_along(): return lax.ppermute(block, axis, route)  389 us
    dot_general x40, matrix products, typed_product(): jnp.einsum('tpq,rqw->trpw', blocks_table, state_in, precision=precise)  96.5 us
    dot_general x32, matrix products, inverse_product(): jnp.einsum('pq,rqw->rpw', diag_inverse, balance, precision=precise)  47 us
  transfers between devices with their start and end apart: 72, of which 70 were waited for; matrix products, arithmetic and copies ran while one was open for 2% of the time, Pallas kernels for 0%

commit v1 on v0

v1 whole, which is shorter than its diff:
```python
import functools

import jax
import jax.numpy as jnp
from jax import lax
from jax.experimental import pallas as pl
from jax.experimental.pallas import tpu as pltpu
from jax.sharding import PartitionSpec as P

precise = lax.Precision.HIGHEST
LANES = 128


def padded_2(block, sides, width):
    for axis, dim in sides:
        count = lax.axis_size(axis)
        forward = [(i, i + 1) for i in range(count - 1)]
        backward = [(target, source) for source, target in forward]
        low = lax.ppermute(
            lax.slice_in_dim(block, block.shape[dim] - width, None, axis=dim), axis, forward
        )
        high = lax.ppermute(lax.slice_in_dim(block, 0, width, axis=dim), axis, backward)
        block = jnp.concatenate([low, block, high], axis=dim)
    return block


def typed_product(blocks_table, type_ids, state_in):
    products = jnp.einsum("tpq,rqw->trpw", blocks_table, state_in, precision=precise)
    kinds = jnp.arange(blocks_table.shape[0], dtype=jnp.int32)
    selector = (type_ids[None, :] == kinds[:, None]).astype(jnp.float32)
    return jnp.sum(products * selector[:, None, None, :], axis=0)


def span_block(padded, face_types, span_scale, up_blocks, offset, breadth):
    lower_side = lax.dynamic_slice_in_dim(padded, offset, breadth, 3)
    upper_side = lax.dynamic_slice_in_dim(padded, offset + 2, breadth, 3)
    lower_types = face_types[1]
    upper_types = face_types[2]
    lower_scale = span_scale[0]
    upper_scale = span_scale[1]
    results = []
    for row_index in range(padded.shape[0]):
        lower_term = lower_scale[row_index] * typed_product(
            up_blocks, lower_types[row_index], lower_side[row_index]
        )
        upper_term = upper_scale[row_index] * typed_product(
            up_blocks, upper_types[row_index], upper_side[row_index]
        )
        results.append(lower_term + upper_term)
    return jnp.stack(results)


def kernel_typed(table_ref, types, state):
    dof = state.shape[0]
    products = jnp.dot(table_ref[...], state, precision=precise, preferred_element_type=jnp.float32)
    picked = jnp.zeros_like(state)
    for kind in range(table_ref.shape[0] // dof):
        picked = jnp.where(types == kind, products[kind * dof:(kind + 1) * dof], picked)
    return picked


def barrier_with_neighbours(me, length):
    barrier = pltpu.get_barrier_semaphore()

    @pl.when(me > 0)
    def _():
        pl.semaphore_signal(barrier, inc=1, device_id={"stream": me - 1},
                            device_id_type=pl.DeviceIdType.MESH)

    @pl.when(me < length - 1)
    def _():
        pl.semaphore_signal(barrier, inc=1, device_id={"stream": me + 1},
                            device_id_type=pl.DeviceIdType.MESH)

    ends = jnp.logical_or(me == 0, me == length - 1)

    @pl.when(ends)
    def _():
        pl.semaphore_wait(barrier, 1)

    @pl.when(jnp.logical_not(ends))
    def _():
        pl.semaphore_wait(barrier, 2)


def sweep_kernel(length, direction, balance_ref, types_ref, scale_ref, denom_ref, table_ref, inverse_ref,
                 out_ref, recv_ref, send_ref, send_sem, recv_sem):
    me = lax.axis_index("stream")
    rows, tracers, dof, columns = balance_ref.shape
    groups = columns // LANES
    blocks = tracers * groups
    if direction > 0:
        has_source = me > 0
        has_target = me < length - 1
        target = me + 1
    else:
        has_source = me < length - 1
        has_target = me > 0
        target = me - 1

    @pl.when(jnp.logical_not(has_source))
    def _():
        recv_ref[...] = jnp.zeros(recv_ref.shape, jnp.float32)

    barrier_with_neighbours(me, length)

    def copy_of(k):
        return pltpu.make_async_remote_copy(
            src_ref=send_ref.at[k],
            dst_ref=recv_ref.at[k],
            send_sem=send_sem.at[k],
            recv_sem=recv_sem.at[k],
            device_id={"stream": target},
            device_id_type=pl.DeviceIdType.MESH,
        )

    row_order = list(range(rows)) if direction > 0 else list(range(rows - 1, -1, -1))

    def block_step(k, carry):
        tracer = k % tracers
        group = k // tracers
        cols = pl.ds(pl.multiple_of(group * LANES, LANES), LANES)

        @pl.when(has_source)
        def _():
            copy_of(k).wait_recv()

        state = recv_ref[k]
        for row in row_order:
            types = types_ref[pl.ds(row, 1), cols]
            scale = scale_ref[pl.ds(row, 1), cols]
            denom = denom_ref[pl.ds(row, 1), cols]
            if direction > 0:
                balance = balance_ref[row, tracer, :, cols] - scale * kernel_typed(table_ref, types, state)
                state = jnp.dot(inverse_ref[...], balance, precision=precise,
                                preferred_element_type=jnp.float32) / denom
                out_ref[row, tracer, :, cols] = state
            else:
                solved = balance_ref[row, tracer, :, cols] - jnp.dot(
                    inverse_ref[...], state, precision=precise, preferred_element_type=jnp.float32) / denom
                out_ref[row, tracer, :, cols] = solved
                state = scale * kernel_typed(table_ref, types, solved)
        send_ref[k] = state

        @pl.when(has_target)
        def _():
            copy_of(k).start()

        return carry

    lax.fori_loop(0, blocks, block_step, 0)

    def drain(k, carry):
        copy_of(k).wait_send()
        return carry

    @pl.when(has_target)
    def _():
        lax.fori_loop(0, blocks, drain, 0)


def sweep(direction, collective_id, balance, types, scale, denom, table, inverse):
    rows, tracers, dof, columns = balance.shape
    length = lax.axis_size("stream")
    blocks = tracers * (columns // LANES)
    vmem = pltpu.VMEM
    return pl.pallas_call(
        functools.partial(sweep_kernel, length, direction),
        out_shape=jax.ShapeDtypeStruct(balance.shape, jnp.float32),
        in_specs=[pl.BlockSpec(memory_space=vmem)] * 6,
        out_specs=pl.BlockSpec(memory_space=vmem),
        scratch_shapes=[
            pltpu.VMEM((blocks, dof, LANES), jnp.float32),
            pltpu.VMEM((blocks, dof, LANES), jnp.float32),
            pltpu.SemaphoreType.DMA((blocks,)),
            pltpu.SemaphoreType.DMA((blocks,)),
        ],
        compiler_params=pltpu.CompilerParams(
            collective_id=collective_id, has_side_effects=True, vmem_limit_bytes=60 * 1024 * 1024
        ),
    )(balance, types, scale, denom, table, inverse)


def per_device(
    rhs, lagged, face_types, stream_scale, span_scale, absorb, up_blocks, down_blocks, diag_inverse
):
    columns = rhs.shape[3]
    padded = padded_2(lagged, (("span", 3),), 1)
    denominator = stream_scale + span_scale[0] + span_scale[1] + absorb
    span_terms = span_block(padded, face_types, span_scale, up_blocks, 0, columns)
    dof = up_blocks.shape[1]
    up_table = up_blocks.reshape(-1, dof)
    down_table = down_blocks.reshape(-1, dof)
    forward_part = sweep(1, 0, rhs - span_terms, face_types[0], stream_scale, denominator, up_table,
                         diag_inverse)
    increment = sweep(-1, 1, forward_part, face_types[0], stream_scale, denominator, down_table,
                      diag_inverse)
    return increment


def solution(mesh):
    return jax.shard_map(
        per_device,
        mesh=mesh,
        in_specs=(
            P("stream", None, None, "span"),
            P("stream", None, None, "span"),
            P(None, "stream", "span"),
            P("stream", "span"),
            P(None, "stream", "span"),
            P("stream", "span"),
            P(),
            P(),
            P(),
        ),
        out_specs=P("stream", None, None, "span"),
        check_vma=False,
    )
```

time: 1610 us -> 582 us (0.36)
  waiting for transfers between devices: 1010 us -> 0.01 us
  Pallas kernels: 0 us -> 513 us
  starting transfers between devices: 394 us -> 4.35 us
  matrix products: 143 us -> 45.9 us
  local copies, waits for them, and re-layouts: 37.9 us -> 12 us
    ppermute x70 -> x0, waiting for transfers between devices: 1010 us -> none  [passed_along(): return lax.ppermute(block, axis, route)]
    pallas_call x0 -> x2, Pallas kernels: none -> 513 us  [sweep(): pl.pallas_call(functools.partial(sweep_kernel, length, direction), out_sh...]
    ppermute x70 -> x0, starting transfers between devices: 389 us -> none  [passed_along(): return lax.ppermute(block, axis, route)]
    dot_general x40 -> x8, matrix products: 96.5 us -> 45.9 us  [typed_product(): jnp.einsum('tpq,rqw->trpw', blocks_table, state_in, precision=precise)]
    dot_general x32 -> x0, matrix products: 47 us -> none  [inverse_product(): jnp.einsum('pq,rqw->rpw', diag_inverse, balance, precision=precise)]
    another operation x66 -> x0, local copies, waits for them, and re-layouts: 27.5 us -> none
  transfers between devices with their start and end apart: 72 -> 2, of which waited for: 70 -> 0; matrix products, arithmetic and copies ran while one was open for 2% -> 5% of each run, Pallas kernels for 0% -> 0%
where the time goes in v1:
time: 582 us; the launch traced here: 581 us
  Pallas kernels  513 us (88%)
  matrix products  45.9 us (8%)
  local copies, waits for them, and re-layouts  12 us (2%)
    pallas_call x2, Pallas kernels, sweep(): pl.pallas_call(functools.partial(sweep_kernel, length, direction), out_sh...  513 us
    dot_general x8, matrix products, typed_product(): jnp.einsum('tpq,rqw->trpw', blocks_table, state_in, precision=precise)  45.9 us
  transfers between devices with their start and end apart: 2, of which 0 were waited for; matrix products, arithmetic and copies ran while one was open for 5% of the time, Pallas kernels for 0%

profile of v1, /device:TPU:0, one launch (start us, length us, event | category | flops | bytes accessed | tf_op | source)
XLA Modules:
  0.0 581.2 jit_solution(10967445265985596198)
XLA Ops:
  0.0 1.4 fusion.42
  1.4 1.3 collective-permute-start.1
  2.7 3.1 collective-permute-start
  5.8 0.9 fusion.43
  6.7 1.3 slice_bitcast_fusion.8.types_ref
  8.1 0.9 fusion.44
  9.0 1.4 fusion.37.denom_ref
  10.4 0.0 copy-start.1
  10.4 2.6 constant_dynamic-update-slice_fusion.1
  13.1 0.0 collective-permute-done.1
  13.1 0.0 copy-done.1
  13.1 5.7 fusion.4
  18.8 0.0 copy-start
  18.8 5.7 fusion.6
  24.5 5.7 fusion
  30.2 5.7 fusion.2
  35.9 0.0 collective-permute-done
  35.9 0.0 copy-done
  35.9 5.9 %fusion.5 = f32[4,64,1024]{2,1,0:T(8,128)S(1)} fusion(f32[6,1024]{1,0:T(8,128)S(1)} %fusion.31, f32[4,4,64,1024]{3,2,1,0:T(8,128)S(1)} %copy-done, f32[4,4,64,1]{3,2,1,0:T(8,128)S(1)} %collective-permute-done, f32[6,64,64]{2,1,0:T(8,128)S(1)} %copy-done.1), kind=kOutput, calls=%fused_computation.11 | convolution fusion | flops 1211105280 | bytes 5369856 | tf_op jit(solution)/shard_map/tpq,rqw->trpw/dot_general | solution.py:28
  41.8 5.7 fusion.7
  47.5 0.5 fusion.19
  48.0 5.7 fusion.1
  53.8 0.0 copy-start.2
  53.8 5.9 %fusion.3 = f32[4,64,1024]{2,1,0:T(8,128)S(1)} fusion(f32[6,1024]{1,0:T(8,128)S(1)} %fusion.33, f32[4,4,64,1024]{3,2,1,0:T(8,128)S(1)} %copy-done, f32[4,4,64,1]{3,2,1,0:T(8,128)S(1)} %collective-permute-done, f32[6,64,64]{2,1,0:T(8,128)S(1)} %copy-done.1), kind=kOutput, calls=%fused_computation.7 | convolution fusion | flops 1211105280 | bytes 5369856 | tf_op jit(solution)/shard_map/tpq,rqw->trpw/dot_general | solution.py:28
  59.7 0.5 fusion.17
  60.2 0.0 copy-done.2
  60.2 3.0 maximum_subtract_fusion.balance_ref
  63.2 83.7 %shard_map.91.balance_ref = f32[4,4,64,1024]{3,2,1,0:T(8,128)} custom-call(f32[4,4,64,1024]{3,2,1,0:T(8,128)} %maximum_subtract_fusion.balance_ref, s32[4,1024]{1,0:T(4,128)} %slice_bitcast_fusion.8.types_ref, f32[4,1024]{1,0:T(4,128)} %scale_ref.3, f32[4,1024]{1,0:T(4,128)} %fusion.37.denom_ref, f32[384,64]{1,0:T(8,128)} %bitcast.157, f32[64,64]{1,0:T(8,128)} %inverse_ref.3), custom_call_target="tpu_custom_call" | custom-call | tf_op jit(solution)/shard_map/pallas_call | solution.py:167
  146.9 429.5 %shard_map.92 = f32[4,4,64,1024]{3,2,1,0:T(8,128)} custom-call(f32[4,4,64,1024]{3,2,1,0:T(8,128)} %shard_map.91.balance_ref, s32[4,1024]{1,0:T(4,128)} %slice_bitcast_fusion.8.types_ref, f32[4,1024]{1,0:T(4,128)} %scale_ref.3, f32[4,1024]{1,0:T(4,128)} %fusion.37.denom_ref, f32[384,64]{1,0:T(8,128)} %bitcast.158, f32[64,64]{1,0:T(8,128)} %inverse_ref.3), custom_call_target="tpu_custom_call" | custom-call | tf_op jit(solution)/shard_map/pallas_call | solution.py:167
  576.4 4.8 copy.20
  (9 shorter events, 0.1 us)
Async XLA Ops:
  1.4 11.7 %collective-permute-start.1 = (f32[4,4,64,1]{3,2,1,0:T(8,128)S(1)}, f32[4,4,64,1]{3,2,1,0:T(8,128)S(1)}, u32[]{:S(2)}, u32[]{:S(2)}) collective-permute-start(f32[4,4,64,1]{3,2,1,0:T(8,128)S(1)} %get-tuple-element.6), channel_id=1, source_target_pairs={{1,0},{2,1},{3,2},{5,4},{6,5},{7,6},{9,8},{10,9},{11,10},{13,12},{... | collective-permute-start | bytes 12296 | tf_op jit(solution)/shard_map/ppermute | solution.py:22
  2.7 33.2 %collective-permute-start = (f32[4,4,64,1]{3,2,1,0:T(8,128)S(1)}, f32[4,4,64,1]{3,2,1,0:T(8,128)S(1)}, u32[]{:S(2)}, u32[]{:S(2)}) collective-permute-start(f32[4,4,64,1]{3,2,1,0:T(8,128)S(1)} %get-tuple-element.5), channel_id=1, source_target_pairs={{0,1},{1,2},{2,3},{4,5},{5,6},{6,7},{8,9},{9,10},{10,11},{12,13},{... | collective-permute-start | bytes 12296 | tf_op jit(solution)/shard_map/ppermute | solution.py:19
  10.4 2.7 copy-start.1
  18.8 17.1 %copy-start = (f32[4,4,64,1024]{3,2,1,0:T(8,128)S(1)}, f32[4,4,64,1024]{3,2,1,0:T(8,128)}, u32[]{:S(2)}) copy-start(f32[4,4,64,1024]{3,2,1,0:T(8,128)} %param.10) | copy-start | bytes 12582916
  53.8 6.4 %copy-start.2 = (f32[4,4,64,1024]{3,2,1,0:T(8,128)S(1)}, f32[4,4,64,1024]{3,2,1,0:T(8,128)}, u32[]{:S(2)}) copy-start(f32[4,4,64,1024]{3,2,1,0:T(8,128)} %param.9) | copy-start | bytes 12582916

commit v2 on v1

--- a/solution.py
+++ b/solution.py
@@ -50,11 +50,22 @@
     return jnp.stack(results)
 
 
+def split_table(table):
+    high = lax.reduce_precision(table, exponent_bits=8, mantissa_bits=7)
+    low = table - high
+    high = high.astype(jnp.bfloat16)
+    low = low.astype(jnp.bfloat16)
+    return jnp.concatenate([high, low, high], axis=1)
+
+
 def kernel_typed(table_ref, types, state):
     dof = state.shape[0]
-    products = jnp.dot(table_ref[...], state, precision=precise, preferred_element_type=jnp.float32)
-    picked = jnp.zeros_like(state)
-    for kind in range(table_ref.shape[0] // dof):
+    high = state.astype(jnp.bfloat16)
+    low = (state - high.astype(jnp.float32)).astype(jnp.bfloat16)
+    stacked = jnp.concatenate([high, high, low], axis=0)
+    products = jnp.dot(table_ref[...], stacked, preferred_element_type=jnp.float32)
+    picked = products[0:dof]
+    for kind in range(1, table_ref.shape[0] // dof):
         picked = jnp.where(types == kind, products[kind * dof:(kind + 1) * dof], picked)
     return picked
 
@@ -83,12 +94,12 @@
         pl.semaphore_wait(barrier, 2)
 
 
-def sweep_kernel(length, direction, balance_ref, types_ref, scale_ref, denom_ref, table_ref, inverse_ref,
+def sweep_kernel(length, direction, width, grouped, start_ref, types_ref, coeff_ref, denom_ref, table_ref,
                  out_ref, recv_ref, send_ref, send_sem, recv_sem):
     me = lax.axis_index("stream")
-    rows, tracers, dof, columns = balance_ref.shape
-    groups = columns // LANES
-    blocks = tracers * groups
+    rows, tracers, dof, columns = start_ref.shape
+    sets = tracers // grouped
+    blocks = sets * (columns // width)
     if direction > 0:
         has_source = me > 0
         has_target = me < length - 1
@@ -116,10 +127,15 @@
 
     row_order = list(range(rows)) if direction > 0 else list(range(rows - 1, -1, -1))
 
+    def gathered(ref, row, first, cols):
+        return jnp.concatenate([ref[row, first + tracer, :, cols] for tracer in range(grouped)], axis=1)
+
+    def lanes(ref, row, cols):
+        return jnp.concatenate([ref[pl.ds(row, 1), cols]] * grouped, axis=1)
+
     def block_step(k, carry):
-        tracer = k % tracers
-        group = k // tracers
-        cols = pl.ds(pl.multiple_of(group * LANES, LANES), LANES)
+        first = (k % sets) * grouped
+        cols = pl.ds(pl.multiple_of((k // sets) * width, width), width)
 
         @pl.when(has_source)
         def _():
@@ -127,19 +143,16 @@
 
         state = recv_ref[k]
         for row in row_order:
-            types = types_ref[pl.ds(row, 1), cols]
-            scale = scale_ref[pl.ds(row, 1), cols]
-            denom = denom_ref[pl.ds(row, 1), cols]
+            types = lanes(types_ref, row, cols)
+            coeff = lanes(coeff_ref, row, cols)
             if direction > 0:
-                balance = balance_ref[row, tracer, :, cols] - scale * kernel_typed(table_ref, types, state)
-                state = jnp.dot(inverse_ref[...], balance, precision=precise,
-                                preferred_element_type=jnp.float32) / denom
-                out_ref[row, tracer, :, cols] = state
+                state = gathered(start_ref, row, first, cols) - coeff * kernel_typed(table_ref, types, state)
+                solved = state
             else:
-                solved = balance_ref[row, tracer, :, cols] - jnp.dot(
-                    inverse_ref[...], state, precision=precise, preferred_element_type=jnp.float32) / denom
-                out_ref[row, tracer, :, cols] = solved
-                state = scale * kernel_typed(table_ref, types, solved)
+                solved = gathered(start_ref, row, first, cols) - state / lanes(denom_ref, row, cols)
+                state = coeff * kernel_typed(table_ref, types, solved)
+            for tracer in range(grouped):
+                out_ref[row, first + tracer, :, cols] = solved[:, tracer * width:(tracer + 1) * width]
         send_ref[k] = state
 
         @pl.when(has_target)
@@ -159,42 +172,45 @@
         lax.fori_loop(0, blocks, drain, 0)
 
 
-def sweep(direction, collective_id, balance, types, scale, denom, table, inverse):
-    rows, tracers, dof, columns = balance.shape
+def sweep(direction, collective_id, width, grouped, start, types, coeff, denom, table):
+    rows, tracers, dof, columns = start.shape
+    blocks = (tracers // grouped) * (columns // width)
     length = lax.axis_size("stream")
-    blocks = tracers * (columns // LANES)
     vmem = pltpu.VMEM
     return pl.pallas_call(
-        functools.partial(sweep_kernel, length, direction),
-        out_shape=jax.ShapeDtypeStruct(balance.shape, jnp.float32),
-        in_specs=[pl.BlockSpec(memory_space=vmem)] * 6,
+        functools.partial(sweep_kernel, length, direction, width, grouped),
+        out_shape=jax.ShapeDtypeStruct(start.shape, jnp.float32),
+        in_specs=[pl.BlockSpec(memory_space=vmem)] * 5,
         out_specs=pl.BlockSpec(memory_space=vmem),
         scratch_shapes=[
-            pltpu.VMEM((blocks, dof, LANES), jnp.float32),
-            pltpu.VMEM((blocks, dof, LANES), jnp.float32),
+            pltpu.VMEM((blocks, dof, grouped * width), jnp.float32),
+            pltpu.VMEM((blocks, dof, grouped * width), jnp.float32),
             pltpu.SemaphoreType.DMA((blocks,)),
             pltpu.SemaphoreType.DMA((blocks,)),
         ],
         compiler_params=pltpu.CompilerParams(
             collective_id=collective_id, has_side_effects=True, vmem_limit_bytes=60 * 1024 * 1024
         ),
-    )(balance, types, scale, denom, table, inverse)
+    )(start, types, coeff, denom, table)
 
 
 def per_device(
     rhs, lagged, face_types, stream_scale, span_scale, absorb, up_blocks, down_blocks, diag_inverse
 ):
     columns = rhs.shape[3]
+    dof = up_blocks.shape[1]
     padded = padded_2(lagged, (("span", 3),), 1)
     denominator = stream_scale + span_scale[0] + span_scale[1] + absorb
     span_terms = span_block(padded, face_types, span_scale, up_blocks, 0, columns)
-    dof = up_blocks.shape[1]
-    up_table = up_blocks.reshape(-1, dof)
-    down_table = down_blocks.reshape(-1, dof)
-    forward_part = sweep(1, 0, rhs - span_terms, face_types[0], stream_scale, denominator, up_table,
-                         diag_inverse)
-    increment = sweep(-1, 1, forward_part, face_types[0], stream_scale, denominator, down_table,
-                      diag_inverse)
+    start = jnp.einsum("pq,nrqc->nrpc", diag_inverse, rhs - span_terms, precision=precise)
+    start = start / denominator[:, None, None, :]
+    coeff = stream_scale / denominator
+    up_table = split_table(jnp.einsum("pq,tqs->tps", diag_inverse, up_blocks, precision=precise).reshape(-1, dof))
+    down_table = split_table(jnp.einsum("pq,tqs->tps", diag_inverse, down_blocks, precision=precise).reshape(-1, dof))
+    width = LANES
+    grouped = 1
+    forward_part = sweep(1, 0, width, grouped, start, face_types[0], coeff, denominator, up_table)
+    increment = sweep(-1, 1, width, grouped, forward_part, face_types[0], stream_scale, denominator, down_table)
     return increment
 
 

time: 582 us -> 416 us (0.71)
  Pallas kernels: 513 us -> 336 us
  matrix products: 45.9 us -> 58.5 us
    pallas_call x2, Pallas kernels: 513 us -> 336 us  [sweep(): pl.pallas_call(functools.partial(sweep_kernel, length, direction, width,...]
    dot_general x0 -> x3, matrix products: none -> 7.19 us  [the longest x1 6.22 us: per_device(): jnp.einsum('pq,nrqc->nrpc', diag_inverse, rhs - span_terms, precision=pre...]
  transfers between devices with their start and end apart: 2 -> 2, of which waited for: 0 -> 0; matrix products, arithmetic and copies ran while one was open for 5% -> 9% of each run, Pallas kernels for 0% -> 0%
where the time goes in v2:
time: 416 us
  Pallas kernels  336 us (81%)
  matrix products  58.5 us (14%)
  local copies, waits for them, and re-layouts  12.9 us (3%)
  starting transfers between devices  4.62 us (1%)
    pallas_call x2, Pallas kernels, sweep(): pl.pallas_call(functools.partial(sweep_kernel, length, direction, width,...  336 us
    dot_general x8, matrix products, typed_product(): jnp.einsum('tpq,rqw->trpw', blocks_table, state_in, precision=precise)  51.3 us
    unnamed x22, local copies, waits for them, and re-layouts  9.62 us
  transfers between devices with their start and end apart: 2, of which 0 were waited for; matrix products, arithmetic and copies ran while one was open for 9% of the time, Pallas kernels for 0%

profile of v2, /device:TPU:0, one launch (start us, length us, event | category | flops | bytes accessed | tf_op | source)
XLA Modules:
  0.0 415.8 jit_solution(1307854785503189613)
XLA Ops:
  0.0 0.0 copy-start
  0.0 1.5 fusion.57
  1.5 0.0 copy-start.7
  1.5 0.0 copy-start.4
  1.5 0.0 copy-start.5
  1.5 1.4 collective-permute-start.1
  2.9 0.0 copy-start.2
  2.9 0.0 copy-start.6
  2.9 0.0 copy-start.8
  3.0 3.2 collective-permute-start
  6.2 4.8 %constant_dynamic-update-slice_fusion.1 = f32[4,4,64,1025]{3,2,1,0:T(8,128)} fusion(f32[4,4,64,1024]{3,2,1,0:T(8,128)} %param.10), kind=kLoop, calls=%fused_computation.95 | loop fusion | bytes 8388608
  10.9 0.0 copy-done.7
  11.0 0.6 slice_bitcast_fusion.8.types_ref
  11.6 0.0 copy-done.4
  11.7 0.0 copy-done
  11.7 0.0 copy-done.5
  11.7 0.5 convolution_bitcast_fusion.1
  12.2 0.1 copy.11
  12.4 0.0 copy-done.2
  12.4 0.5 convolution_bitcast_fusion
  12.9 0.1 copy.13
  13.1 0.0 copy-done.6
  13.1 0.0 copy-done.8
  13.1 0.6 fusion.55
  13.7 0.8 pad_maximum_fusion.1.table_ref
  14.5 0.8 pad_maximum_fusion.2.table_ref
  15.3 0.0 collective-permute-done.1
  15.3 0.9 constant_dynamic-update-slice_fusion
  16.2 7.2 %fusion.4 = f32[4,64,1024]{2,1,0:T(8,128)S(1)} fusion(f32[6,1024]{1,0:T(8,128)S(1)} %fusion.44, f32[4,4,64,1025]{3,2,1,0:T(8,128)} %constant_dynamic-update-slice_fusion, f32[6,64,64]{2,1,0:T(8,128)S(1)} %copy-done), kind=kOutput, calls=%fused_computation.9 | convolution fusion | flops 1210843136 | bytes 2220032 | tf_op jit(solution)/shard_map/tpq,rqw->trpw/dot_general | solution.py:28
  23.4 0.0 copy-start.1
  23.4 7.1 %fusion.6 = f32[4,64,1024]{2,1,0:T(8,128)S(1)} fusion(f32[6,1024]{1,0:T(8,128)S(1)} %fusion.42, f32[4,4,64,1025]{3,2,1,0:T(8,128)} %constant_dynamic-update-slice_fusion, f32[6,64,64]{2,1,0:T(8,128)S(1)} %copy-done), kind=kOutput, calls=%fused_computation.13 | convolution fusion | flops 1210843136 | bytes 2220032 | tf_op jit(solution)/shard_map/tpq,rqw->trpw/dot_general | solution.py:28
  30.6 7.0 %fusion = f32[4,64,1024]{2,1,0:T(8,128)S(1)} fusion(f32[6,1024]{1,0:T(8,128)S(1)} %fusion.48, f32[4,4,64,1025]{3,2,1,0:T(8,128)} %constant_dynamic-update-slice_fusion, f32[6,64,64]{2,1,0:T(8,128)S(1)} %copy-done), kind=kOutput, calls=%fused_computation.1 | convolution fusion | flops 1210843136 | bytes 2220032 | tf_op jit(solution)/shard_map/tpq,rqw->trpw/dot_general | solution.py:28
  37.6 7.0 %fusion.2 = f32[4,64,1024]{2,1,0:T(8,128)S(1)} fusion(f32[6,1024]{1,0:T(8,128)S(1)} %fusion.46, f32[4,4,64,1025]{3,2,1,0:T(8,128)} %constant_dynamic-update-slice_fusion, f32[6,64,64]{2,1,0:T(8,128)S(1)} %copy-done), kind=kOutput, calls=%fused_computation.5 | convolution fusion | flops 1210843136 | bytes 2220032 | tf_op jit(solution)/shard_map/tpq,rqw->trpw/dot_general | solution.py:28
  44.6 0.0 collective-permute-done
  44.6 0.0 copy-done.1
  44.6 5.9 %fusion.5 = f32[4,64,1024]{2,1,0:T(8,128)S(1)} fusion(f32[6,1024]{1,0:T(8,128)S(1)} %fusion.43, f32[4,4,64,1024]{3,2,1,0:T(8,128)S(1)} %copy-done.1, f32[4,4,64,1]{3,2,1,0:T(8,128)S(1)} %collective-permute-done, f32[6,64,64]{2,1,0:T(8,128)S(1)} %copy-done), kind=kOutput, calls=%fused_computation.11 | convolution fusion | flops 1211105280 | bytes 5369856 | tf_op jit(solution)/shard_map/tpq,rqw->trpw/dot_general | solution.py:28
  50.5 5.7 %fusion.7 = f32[4,64,1024]{2,1,0:T(8,128)S(1)} fusion(f32[6,1024]{1,0:T(8,128)S(1)} %fusion.41, f32[4,4,64,1024]{3,2,1,0:T(8,128)S(1)} %copy-done.1, f32[4,4,64,1]{3,2,1,0:T(8,128)S(1)} %collective-permute-done, f32[6,64,64]{2,1,0:T(8,128)S(1)} %copy-done), kind=kOutput, calls=%fused_computation.15 | convolution fusion | flops 1211105280 | bytes 5369856 | tf_op jit(solution)/shard_map/tpq,rqw->trpw/dot_general | solution.py:28
  56.2 0.7 fusion.26
  56.9 5.7 %fusion.1 = f32[4,64,1024]{2,1,0:T(8,128)S(1)} fusion(f32[6,1024]{1,0:T(8,128)S(1)} %fusion.47, f32[4,4,64,1024]{3,2,1,0:T(8,128)S(1)} %copy-done.1, f32[4,4,64,1]{3,2,1,0:T(8,128)S(1)} %collective-permute-done, f32[6,64,64]{2,1,0:T(8,128)S(1)} %copy-done), kind=kOutput, calls=%fused_computation.3 | convolution fusion | flops 1211105280 | bytes 5369856 | tf_op jit(solution)/shard_map/tpq,rqw->trpw/dot_general | solution.py:28
  62.6 0.0 copy-start.9
  62.6 5.7 %fusion.3 = f32[4,64,1024]{2,1,0:T(8,128)S(1)} fusion(f32[6,1024]{1,0:T(8,128)S(1)} %fusion.45, f32[4,4,64,1024]{3,2,1,0:T(8,128)S(1)} %copy-done.1, f32[4,4,64,1]{3,2,1,0:T(8,128)S(1)} %collective-permute-done, f32[6,64,64]{2,1,0:T(8,128)S(1)} %copy-done), kind=kOutput, calls=%fused_computation.7 | convolution fusion | flops 1211105280 | bytes 5369856 | tf_op jit(solution)/shard_map/tpq,rqw->trpw/dot_general | solution.py:28
  68.3 0.7 fusion.24
  69.0 0.0 copy-done.3
  69.0 0.0 copy-done.9
  69.0 6.2 %divide_bitcast_fusion.start_ref = f32[4,4,64,1024]{3,2,1,0:T(8,128)} fusion(f32[4,1024]{1,0:T(4,128)S(1)} %get-tuple-element.6.denom_ref, f32[4,4,64,1024]{3,2,1,0:T(8,128)S(1)} %copy-done.9, f32[1,4,64,1024]{3,2,1,0:T(8,128)S(1)} %get-tuple-element.29, f32[1,4,64,1024]{3,2,1,0:T(8,128)S(1)} %get-tuple-element.30, ...), kind=kOutput, calls=%fused_computation.24 | convolution fusion | flops 810549248 | bytes 12615680 | tf_op jit(solution)/shard_map/pq,nrqc->nrpc/dot_general | solution.py:205
  75.2 38.4 %shard_map.91.start_ref = f32[4,4,64,1024]{3,2,1,0:T(8,128)} custom-call(f32[4,4,64,1024]{3,2,1,0:T(8,128)} %divide_bitcast_fusion.start_ref, s32[4,1024]{1,0:T(4,128)} %slice_bitcast_fusion.8.types_ref, f32[4,1024]{1,0:T(4,128)} %get-tuple-element.5.coeff_ref, f32[4,1024]{1,0:T(4,128)} %copy-done.3, bf16[384,192]{1,0:T(8,128)(2,1)} %pad_maximum_fusion.1.table_ref), custom_call_target="tpu_custom_call" | custom-call | tf_op jit(solution)/shard_map/pallas_call | solution.py:180
  113.6 297.4 %shard_map.92 = f32[4,4,64,1024]{3,2,1,0:T(8,128)} custom-call(f32[4,4,64,1024]{3,2,1,0:T(8,128)} %shard_map.91.start_ref, s32[4,1024]{1,0:T(4,128)} %slice_bitcast_fusion.8.types_ref, f32[4,1024]{1,0:T(4,128)} %coeff_ref.1, f32[4,1024]{1,0:T(4,128)} %copy-done.3, bf16[384,192]{1,0:T(8,128)(2,1)} %pad_maximum_fusion.2.table_ref), custom_call_target="tpu_custom_call" | custom-call | tf_op jit(solution)/shard_map/pallas_call | solution.py:180
  411.0 4.8 %copy.27 = f32[4,4,64,1024]{3,2,1,0:T(8,128)} copy(f32[4,4,64,1024]{3,2,1,0:T(8,128)} %shard_map.92) | data formatting | bytes 8388608
  (13 shorter events, 0.2 us)
Async XLA Ops:
  0.0 11.7 %copy-start = (f32[6,64,64]{2,1,0:T(8,128)S(1)}, f32[6,64,64]{2,1,0:T(8,128)}, u32[]{:S(2)}) copy-start(f32[6,64,64]{2,1,0:T(8,128)} %param.15) | copy-start | bytes 294916
  1.5 9.5 %copy-start.7 = (s32[3,4,1024]{2,1,0:T(4,128)S(1)}, s32[3,4,1024]{2,1,0:T(4,128)}, u32[]{:S(2)}) copy-start(s32[3,4,1024]{2,1,0:T(4,128)} %param.11) | copy-start | bytes 147460
  1.5 10.1 %copy-start.4 = (f32[2,4,1024]{2,1,0:T(4,128)S(1)}, f32[2,4,1024]{2,1,0:T(4,128)}, u32[]{:S(2)}) copy-start(f32[2,4,1024]{2,1,0:T(4,128)} %param.13) | copy-start | bytes 98308
  1.5 10.2 %copy-start.5 = (f32[64,64]{1,0:T(8,128)S(1)}, f32[64,64]{1,0:T(8,128)}, u32[]{:S(2)}) copy-start(f32[64,64]{1,0:T(8,128)} %param.17) | copy-start | bytes 49156
  1.5 13.8 %collective-permute-start.1 = (f32[4,4,64,1]{3,2,1,0:T(8,128)S(1)}, f32[4,4,64,1]{3,2,1,0:T(8,128)S(1)}, u32[]{:S(2)}, u32[]{:S(2)}) collective-permute-start(f32[4,4,64,1]{3,2,1,0:T(8,128)S(1)} %get-tuple-element.8), channel_id=1, source_target_pairs={{1,0},{2,1},{3,2},{5,4},{6,5},{7,6},{9,8},{10,9},{11,10},{13,12},{... | collective-permute-start | bytes 12296 | tf_op jit(solution)/shard_map/ppermute | solution.py:22
  2.9 9.5 %copy-start.2 = (f32[6,64,64]{2,1,0:T(8,128)S(1)}, f32[6,64,64]{2,1,0:T(8,128)}, u32[]{:S(2)}) copy-start(f32[6,64,64]{2,1,0:T(8,128)} %param.16) | copy-start | bytes 294916
  2.9 10.1 %copy-start.6 = (f32[4,1024]{1,0:T(4,128)S(1)}, f32[4,1024]{1,0:T(4,128)}, u32[]{:S(2)}) copy-start(f32[4,1024]{1,0:T(4,128)} %coeff_ref.1) | copy-start | bytes 49156
  2.9 10.1 %copy-start.8 = (f32[4,1024]{1,0:T(4,128)S(1)}, f32[4,1024]{1,0:T(4,128)}, u32[]{:S(2)}) copy-start(f32[4,1024]{1,0:T(4,128)} %param.14) | copy-start | bytes 49156
  3.0 41.6 %collective-permute-start = (f32[4,4,64,1]{3,2,1,0:T(8,128)S(1)}, f32[4,4,64,1]{3,2,1,0:T(8,128)S(1)}, u32[]{:S(2)}, u32[]{:S(2)}) collective-permute-start(f32[4,4,64,1]{3,2,1,0:T(8,128)S(1)} %get-tuple-element.7), channel_id=1, source_target_pairs={{0,1},{1,2},{2,3},{4,5},{5,6},{6,7},{8,9},{9,10},{10,11},{12,13},{... | collective-permute-start | bytes 12296 | tf_op jit(solution)/shard_map/ppermute | solution.py:19
  13.7 55.3 %copy-start.3 = (f32[4,1024]{1,0:T(4,128)}, f32[4,1024]{1,0:T(4,128)S(1)}, u32[]{:S(2)}) copy-start(f32[4,1024]{1,0:T(4,128)S(1)} %get-tuple-element.6.denom_ref) | copy-start | bytes 49156
  23.4 21.2 %copy-start.1 = (f32[4,4,64,1024]{3,2,1,0:T(8,128)S(1)}, f32[4,4,64,1024]{3,2,1,0:T(8,128)}, u32[]{:S(2)}) copy-start(f32[4,4,64,1024]{3,2,1,0:T(8,128)} %param.10) | copy-start | bytes 12582916
  62.6 6.4 %copy-start.9 = (f32[4,4,64,1024]{3,2,1,0:T(8,128)S(1)}, f32[4,4,64,1024]{3,2,1,0:T(8,128)}, u32[]{:S(2)}) copy-start(f32[4,4,64,1024]{3,2,1,0:T(8,128)} %param.9) | copy-start | bytes 12582916

commit v3 on v2

--- a/solution.py
+++ b/solution.py
@@ -8,6 +8,7 @@
 from jax.sharding import PartitionSpec as P
 
 precise = lax.Precision.HIGHEST
+fast = lax.Precision.HIGH
 LANES = 128
 
 
@@ -25,7 +26,7 @@
 
 
 def typed_product(blocks_table, type_ids, state_in):
-    products = jnp.einsum("tpq,rqw->trpw", blocks_table, state_in, precision=precise)
+    products = jnp.einsum("tpq,rqw->trpw", blocks_table, state_in, precision=fast)
     kinds = jnp.arange(blocks_table.shape[0], dtype=jnp.int32)
     selector = (type_ids[None, :] == kinds[:, None]).astype(jnp.float32)
     return jnp.sum(products * selector[:, None, None, :], axis=0)
@@ -202,7 +203,7 @@
     padded = padded_2(lagged, (("span", 3),), 1)
     denominator = stream_scale + span_scale[0] + span_scale[1] + absorb
     span_terms = span_block(padded, face_types, span_scale, up_blocks, 0, columns)
-    start = jnp.einsum("pq,nrqc->nrpc", diag_inverse, rhs - span_terms, precision=precise)
+    start = jnp.einsum("pq,nrqc->nrpc", diag_inverse, rhs - span_terms, precision=fast)
     start = start / denominator[:, None, None, :]
     coeff = stream_scale / denominator
     up_table = split_table(jnp.einsum("pq,tqs->tps", diag_inverse, up_blocks, precision=precise).reshape(-1, dof))

time: 416 us -> 395 us (0.950)
  matrix products: 58.5 us -> 37.1 us
    dot_general x9, matrix products: 57.5 us -> 36.1 us  [the longest x8 31.6 us: typed_product(): jnp.einsum('tpq,rqw->trpw', blocks_table, state_in, precision=fast)]
  transfers between devices with their start and end apart: 2 -> 2, of which waited for: 0 -> 0; matrix products, arithmetic and copies ran while one was open for 9% -> 7% of each run, Pallas kernels for 0% -> 0%
where the time goes in v3:
time: 395 us; the launch traced here: 394 us
  Pallas kernels  336 us (85%)
  matrix products  37.1 us (9%)
  local copies, waits for them, and re-layouts  12.9 us (3%)
  starting transfers between devices  4.62 us (1%)
    pallas_call x2, Pallas kernels, sweep(): pl.pallas_call(functools.partial(sweep_kernel, length, direction, width,...  336 us
    dot_general x8, matrix products, typed_product(): jnp.einsum('tpq,rqw->trpw', blocks_table, state_in, precision=fast)  31.6 us
    unnamed x22, local copies, waits for them, and re-layouts  9.62 us
  transfers between devices with their start and end apart: 2, of which 0 were waited for; matrix products, arithmetic and copies ran while one was open for 7% of the time, Pallas kernels for 0%

profile of v3, /device:TPU:0, one launch (start us, length us, event | category | flops | bytes accessed | tf_op | source)
XLA Modules:
  0.0 394.3 jit_solution(4440854614125430984)
XLA Ops:
  0.0 0.0 copy-start
  0.0 1.5 fusion.57
  1.5 0.0 copy-start.7
  1.5 0.0 copy-start.4
  1.5 0.0 copy-start.5
  1.5 1.4 collective-permute-start.1
  2.9 0.0 copy-start.2
  2.9 0.0 copy-start.6
  2.9 0.0 copy-start.8
  3.0 3.2 collective-permute-start
  6.2 4.8 %constant_dynamic-update-slice_fusion.1 = f32[4,4,64,1025]{3,2,1,0:T(8,128)} fusion(f32[4,4,64,1024]{3,2,1,0:T(8,128)} %param.10), kind=kLoop, calls=%fused_computation.95 | loop fusion | bytes 8388608
  10.9 0.0 copy-done.7
  11.0 0.6 slice_bitcast_fusion.8.types_ref
  11.6 0.0 copy-done.4
  11.7 0.0 copy-done
  11.7 0.0 copy-done.5
  11.7 0.5 convolution_bitcast_fusion.1
  12.2 0.1 copy.11
  12.4 0.0 copy-done.2
  12.4 0.5 convolution_bitcast_fusion
  12.9 0.1 copy.13
  13.1 0.0 copy-done.6
  13.1 0.0 copy-done.8
  13.1 0.6 fusion.55
  13.7 0.8 pad_maximum_fusion.1.table_ref
  14.5 0.8 pad_maximum_fusion.2.table_ref
  15.3 0.0 collective-permute-done.1
  15.3 0.9 constant_dynamic-update-slice_fusion
  16.2 4.7 %fusion.4 = f32[4,64,1024]{2,1,0:T(8,128)S(1)} fusion(f32[6,1024]{1,0:T(8,128)S(1)} %fusion.44, f32[4,4,64,1025]{3,2,1,0:T(8,128)} %constant_dynamic-update-slice_fusion, f32[6,64,64]{2,1,0:T(8,128)S(1)} %copy-done), kind=kOutput, calls=%fused_computation.9 | convolution fusion | flops 606863360 | bytes 2220032 | tf_op jit(solution)/shard_map/tpq,rqw->trpw/dot_general | solution.py:29
  20.9 0.0 copy-start.1
  20.9 4.7 %fusion.6 = f32[4,64,1024]{2,1,0:T(8,128)S(1)} fusion(f32[6,1024]{1,0:T(8,128)S(1)} %fusion.42, f32[4,4,64,1025]{3,2,1,0:T(8,128)} %constant_dynamic-update-slice_fusion, f32[6,64,64]{2,1,0:T(8,128)S(1)} %copy-done), kind=kOutput, calls=%fused_computation.13 | convolution fusion | flops 606863360 | bytes 2220032 | tf_op jit(solution)/shard_map/tpq,rqw->trpw/dot_general | solution.py:29
  25.6 4.5 %fusion = f32[4,64,1024]{2,1,0:T(8,128)S(1)} fusion(f32[6,1024]{1,0:T(8,128)S(1)} %fusion.48, f32[4,4,64,1025]{3,2,1,0:T(8,128)} %constant_dynamic-update-slice_fusion, f32[6,64,64]{2,1,0:T(8,128)S(1)} %copy-done), kind=kOutput, calls=%fused_computation.1 | convolution fusion | flops 606863360 | bytes 2220032 | tf_op jit(solution)/shard_map/tpq,rqw->trpw/dot_general | solution.py:29
  30.2 4.5 %fusion.2 = f32[4,64,1024]{2,1,0:T(8,128)S(1)} fusion(f32[6,1024]{1,0:T(8,128)S(1)} %fusion.46, f32[4,4,64,1025]{3,2,1,0:T(8,128)} %constant_dynamic-update-slice_fusion, f32[6,64,64]{2,1,0:T(8,128)S(1)} %copy-done), kind=kOutput, calls=%fused_computation.5 | convolution fusion | flops 606863360 | bytes 2220032 | tf_op jit(solution)/shard_map/tpq,rqw->trpw/dot_general | solution.py:29
  34.7 0.0 collective-permute-done
  34.7 0.0 copy-done.1
  34.7 3.2 fusion.5
  38.0 3.3 fusion.7
  41.2 0.7 fusion.26
  41.9 3.3 fusion.1
  45.2 0.0 copy-start.9
  45.2 3.5 fusion.3
  48.6 0.7 fusion.24
  49.3 0.0 copy-done.3
  49.3 0.0 copy-done.9
  49.3 4.4 %divide_bitcast_fusion.start_ref = f32[4,4,64,1024]{3,2,1,0:T(8,128)} fusion(f32[4,1024]{1,0:T(4,128)S(1)} %get-tuple-element.6.denom_ref, f32[4,4,64,1024]{3,2,1,0:T(8,128)S(1)} %copy-done.9, f32[1,4,64,1024]{3,2,1,0:T(8,128)S(1)} %get-tuple-element.29, f32[1,4,64,1024]{3,2,1,0:T(8,128)S(1)} %get-tuple-element.30, ...), kind=kOutput, calls=%fused_computation.24 | convolution fusion | flops 407896064 | bytes 12615680 | tf_op jit(solution)/shard_map/pq,nrqc->nrpc/dot_general | solution.py:206
  53.8 38.4 %shard_map.91.start_ref = f32[4,4,64,1024]{3,2,1,0:T(8,128)} custom-call(f32[4,4,64,1024]{3,2,1,0:T(8,128)} %divide_bitcast_fusion.start_ref, s32[4,1024]{1,0:T(4,128)} %slice_bitcast_fusion.8.types_ref, f32[4,1024]{1,0:T(4,128)} %get-tuple-element.5.coeff_ref, f32[4,1024]{1,0:T(4,128)} %copy-done.3, bf16[384,192]{1,0:T(8,128)(2,1)} %pad_maximum_fusion.1.table_ref), custom_call_target="tpu_custom_call" | custom-call | tf_op jit(solution)/shard_map/pallas_call | solution.py:181
  92.1 297.4 %shard_map.92 = f32[4,4,64,1024]{3,2,1,0:T(8,128)} custom-call(f32[4,4,64,1024]{3,2,1,0:T(8,128)} %shard_map.91.start_ref, s32[4,1024]{1,0:T(4,128)} %slice_bitcast_fusion.8.types_ref, f32[4,1024]{1,0:T(4,128)} %coeff_ref.1, f32[4,1024]{1,0:T(4,128)} %copy-done.3, bf16[384,192]{1,0:T(8,128)(2,1)} %pad_maximum_fusion.2.table_ref), custom_call_target="tpu_custom_call" | custom-call | tf_op jit(solution)/shard_map/pallas_call | solution.py:181
  389.6 4.8 %copy.27 = f32[4,4,64,1024]{3,2,1,0:T(8,128)} copy(f32[4,4,64,1024]{3,2,1,0:T(8,128)} %shard_map.92) | data formatting | bytes 8388608
  (13 shorter events, 0.2 us)
Async XLA Ops:
  0.0 11.7 %copy-start = (f32[6,64,64]{2,1,0:T(8,128)S(1)}, f32[6,64,64]{2,1,0:T(8,128)}, u32[]{:S(2)}) copy-start(f32[6,64,64]{2,1,0:T(8,128)} %param.15) | copy-start | bytes 294916
  1.5 9.5 %copy-start.7 = (s32[3,4,1024]{2,1,0:T(4,128)S(1)}, s32[3,4,1024]{2,1,0:T(4,128)}, u32[]{:S(2)}) copy-start(s32[3,4,1024]{2,1,0:T(4,128)} %param.11) | copy-start | bytes 147460
  1.5 10.1 %copy-start.4 = (f32[2,4,1024]{2,1,0:T(4,128)S(1)}, f32[2,4,1024]{2,1,0:T(4,128)}, u32[]{:S(2)}) copy-start(f32[2,4,1024]{2,1,0:T(4,128)} %param.13) | copy-start | bytes 98308
  1.5 10.2 %copy-start.5 = (f32[64,64]{1,0:T(8,128)S(1)}, f32[64,64]{1,0:T(8,128)}, u32[]{:S(2)}) copy-start(f32[64,64]{1,0:T(8,128)} %param.17) | copy-start | bytes 49156
  1.5 13.8 %collective-permute-start.1 = (f32[4,4,64,1]{3,2,1,0:T(8,128)S(1)}, f32[4,4,64,1]{3,2,1,0:T(8,128)S(1)}, u32[]{:S(2)}, u32[]{:S(2)}) collective-permute-start(f32[4,4,64,1]{3,2,1,0:T(8,128)S(1)} %get-tuple-element.8), channel_id=1, source_target_pairs={{1,0},{2,1},{3,2},{5,4},{6,5},{7,6},{9,8},{10,9},{11,10},{13,12},{... | collective-permute-start | bytes 12296 | tf_op jit(solution)/shard_map/ppermute | solution.py:23
  2.9 9.5 %copy-start.2 = (f32[6,64,64]{2,1,0:T(8,128)S(1)}, f32[6,64,64]{2,1,0:T(8,128)}, u32[]{:S(2)}) copy-start(f32[6,64,64]{2,1,0:T(8,128)} %param.16) | copy-start | bytes 294916
  2.9 10.1 %copy-start.6 = (f32[4,1024]{1,0:T(4,128)S(1)}, f32[4,1024]{1,0:T(4,128)}, u32[]{:S(2)}) copy-start(f32[4,1024]{1,0:T(4,128)} %coeff_ref.1) | copy-start | bytes 49156
  2.9 10.1 %copy-start.8 = (f32[4,1024]{1,0:T(4,128)S(1)}, f32[4,1024]{1,0:T(4,128)}, u32[]{:S(2)}) copy-start(f32[4,1024]{1,0:T(4,128)} %param.14) | copy-start | bytes 49156
  3.0 31.7 %collective-permute-start = (f32[4,4,64,1]{3,2,1,0:T(8,128)S(1)}, f32[4,4,64,1]{3,2,1,0:T(8,128)S(1)}, u32[]{:S(2)}, u32[]{:S(2)}) collective-permute-start(f32[4,4,64,1]{3,2,1,0:T(8,128)S(1)} %get-tuple-element.7), channel_id=1, source_target_pairs={{0,1},{1,2},{2,3},{4,5},{5,6},{6,7},{8,9},{9,10},{10,11},{12,13},{... | collective-permute-start | bytes 12296 | tf_op jit(solution)/shard_map/ppermute | solution.py:20
  13.7 35.6 %copy-start.3 = (f32[4,1024]{1,0:T(4,128)}, f32[4,1024]{1,0:T(4,128)S(1)}, u32[]{:S(2)}) copy-start(f32[4,1024]{1,0:T(4,128)S(1)} %get-tuple-element.6.denom_ref) | copy-start | bytes 49156
  20.9 13.8 %copy-start.1 = (f32[4,4,64,1024]{3,2,1,0:T(8,128)S(1)}, f32[4,4,64,1024]{3,2,1,0:T(8,128)}, u32[]{:S(2)}) copy-start(f32[4,4,64,1024]{3,2,1,0:T(8,128)} %param.10) | copy-start | bytes 12582916
  45.2 4.2 %copy-start.9 = (f32[4,4,64,1024]{3,2,1,0:T(8,128)S(1)}, f32[4,4,64,1024]{3,2,1,0:T(8,128)}, u32[]{:S(2)}) copy-start(f32[4,4,64,1024]{3,2,1,0:T(8,128)} %param.9) | copy-start | bytes 12582916

commit v4 on v3

--- a/solution.py
+++ b/solution.py
@@ -195,6 +195,147 @@
     )(start, types, coeff, denom, table)
 
 
+def both_kernel(length, width, start_ref, types_ref, coeff_ref, scale_ref, inverse_ref, up_ref, down_ref,
+                out_ref, part_ref, recv_f, send_f, recv_b, send_b, sems):
+    me = lax.axis_index("stream")
+    rows, tracers, dof, columns = start_ref.shape
+    sets = tracers
+    blocks = sets * (columns // width)
+    first_dev = me == 0
+    last_dev = me == length - 1
+
+    @pl.when(first_dev)
+    def _():
+        recv_f[...] = jnp.zeros(recv_f.shape, jnp.float32)
+
+    @pl.when(last_dev)
+    def _():
+        recv_b[...] = jnp.zeros(recv_b.shape, jnp.float32)
+
+    barrier_with_neighbours(me, length)
+
+    def copy_f(k):
+        return pltpu.make_async_remote_copy(
+            src_ref=send_f.at[k], dst_ref=recv_f.at[k], send_sem=sems.at[0, k], recv_sem=sems.at[1, k],
+            device_id={"stream": me + 1}, device_id_type=pl.DeviceIdType.MESH)
+
+    def copy_b(k):
+        return pltpu.make_async_remote_copy(
+            src_ref=send_b.at[k], dst_ref=recv_b.at[k], send_sem=sems.at[2, k], recv_sem=sems.at[3, k],
+            device_id={"stream": me - 1}, device_id_type=pl.DeviceIdType.MESH)
+
+    def place(k):
+        tracer = k % sets
+        cols = pl.ds(pl.multiple_of((k // sets) * width, width), width)
+        return tracer, cols
+
+    def forward_block(k):
+        tracer, cols = place(k)
+
+        @pl.when(jnp.logical_not(first_dev))
+        def _():
+            copy_f(k).wait_recv()
+
+        state = recv_f[k]
+        for row in range(rows):
+            types = types_ref[pl.ds(row, 1), cols]
+            coeff = coeff_ref[pl.ds(row, 1), cols]
+            state = start_ref[row, tracer, :, cols] - coeff * kernel_typed(up_ref, types, state)
+            part_ref[row, tracer, :, cols] = state
+        send_f[k] = state
+
+        @pl.when(jnp.logical_not(last_dev))
+        def _():
+            copy_f(k).start()
+
+    def backward_block(k):
+        tracer, cols = place(k)
+
+        @pl.when(jnp.logical_not(last_dev))
+        def _():
+            copy_b(k).wait_recv()
+
+        state = recv_b[k]
+        for row in range(rows - 1, -1, -1):
+            types = types_ref[pl.ds(row, 1), cols]
+            scale = scale_ref[pl.ds(row, 1), cols]
+            solved = part_ref[row, tracer, :, cols] - state * inverse_ref[pl.ds(row, 1), cols]
+            out_ref[row, tracer, :, cols] = solved
+            state = scale * kernel_typed(down_ref, types, solved)
+        send_b[k] = state
+
+        @pl.when(jnp.logical_not(first_dev))
+        def _():
+            copy_b(k).start()
+
+    lead = jnp.minimum(jnp.maximum(((2 * (length - 1) - 2 * me) * 17) // 6, 1), blocks)
+    tail = 2 * blocks - lead
+
+    def step(s, carry):
+        paired = jnp.logical_and(s >= lead, s < tail)
+        odd = (s - lead) % 2 == 1
+
+        @pl.when(s < lead)
+        def _():
+            forward_block(s)
+
+        @pl.when(jnp.logical_and(paired, odd))
+        def _():
+            forward_block(lead + (s - lead) // 2)
+
+        @pl.when(jnp.logical_and(paired, jnp.logical_not(odd)))
+        def _():
+            backward_block((s - lead) // 2)
+
+        @pl.when(s >= tail)
+        def _():
+            backward_block(s - blocks)
+
+        return carry
+
+    lax.fori_loop(0, 2 * blocks, step, 0)
+
+    def drain_f(k, carry):
+        copy_f(k).wait_send()
+        return carry
+
+    def drain_b(k, carry):
+        copy_b(k).wait_send()
+        return carry
+
+    @pl.when(jnp.logical_not(last_dev))
+    def _():
+        lax.fori_loop(0, blocks, drain_f, 0)
+
+    @pl.when(jnp.logical_not(first_dev))
+    def _():
+        lax.fori_loop(0, blocks, drain_b, 0)
+
+
+def both_sweeps(width, start, types, coeff, scale, inverse, up_table, down_table):
+    rows, tracers, dof, columns = start.shape
+    blocks = tracers * (columns // width)
+    length = lax.axis_size("stream")
+    vmem = pltpu.VMEM
+    return pl.pallas_call(
+        functools.partial(both_kernel, length, width),
+        out_shape=jax.ShapeDtypeStruct(start.shape, jnp.float32),
+        in_specs=[pl.BlockSpec(memory_space=vmem)] * 7,
+        out_specs=pl.BlockSpec(memory_space=vmem),
+        scratch_shapes=[
+            pltpu.VMEM(start.shape, jnp.float32),
+            pltpu.VMEM((blocks, dof, width), jnp.float32),
+            pltpu.VMEM((blocks, dof, width), jnp.float32),
+            pltpu.VMEM((blocks, dof, width), jnp.float32),
+            pltpu.VMEM((blocks, dof, width), jnp.float32),
+            pltpu.SemaphoreType.DMA((4, blocks)),
+        ],
+        compiler_params=pltpu.CompilerParams(
+            collective_id=0, has_side_effects=True, vmem_limit_bytes=60 * 1024 * 1024
+        ),
+    )(start, types, coeff, scale, inverse, up_table, down_table)
+
+
 def per_device(
     rhs, lagged, face_types, stream_scale, span_scale, absorb, up_blocks, down_blocks, diag_inverse
 ):
@@ -206,13 +347,10 @@
     start = jnp.einsum("pq,nrqc->nrpc", diag_inverse, rhs - span_terms, precision=fast)
     start = start / denominator[:, None, None, :]
     coeff = stream_scale / denominator
+    inverse = 1.0 / denominator
     up_table = split_table(jnp.einsum("pq,tqs->tps", diag_inverse, up_blocks, precision=precise).reshape(-1, dof))
     down_table = split_table(jnp.einsum("pq,tqs->tps", diag_inverse, down_blocks, precision=precise).reshape(-1, dof))
-    width = LANES
-    grouped = 1
-    forward_part = sweep(1, 0, width, grouped, start, face_types[0], coeff, denominator, up_table)
-    increment = sweep(-1, 1, width, grouped, forward_part, face_types[0], stream_scale, denominator, down_table)
-    return increment
+    return both_sweeps(LANES, start, face_types[0], coeff, stream_scale, inverse, up_table, down_table)
 
 
 def solution(mesh):

time: 395 us -> 390 us (0.987)
  Pallas kernels: 336 us -> 331 us
    pallas_call x2 -> x1, Pallas kernels: 336 us -> 331 us  [both_sweeps(): pl.pallas_call(functools.partial(both_kernel, length, width), out_shape=j...]
    unnamed x22 -> x20, local copies, waits for them, and re-layouts: 9.62 us -> 9.62 us
where the time goes in v4:
time: 390 us
  Pallas kernels  331 us (85%)
  matrix products  37 us (9%)
  local copies, waits for them, and re-layouts  12.9 us (3%)
  starting transfers between devices  4.49 us (1%)
    pallas_call x1, Pallas kernels, both_sweeps(): pl.pallas_call(functools.partial(both_kernel, length, width), out_shape=j...  331 us
    dot_general x8, matrix products, typed_product(): jnp.einsum('tpq,rqw->trpw', blocks_table, state_in, precision=fast)  31.6 us
    unnamed x20, local copies, waits for them, and re-layouts  9.62 us
  transfers between devices with their start and end apart: 2, of which 0 were waited for; matrix products, arithmetic and copies ran while one was open for 7% of the time, Pallas kernels for 0%

profile of v4, /device:TPU:0, one launch (start us, length us, event | category | flops | bytes accessed | tf_op | source)
XLA Modules:
  0.0 389.8 jit_solution(2087596129786764533)
XLA Ops:
  0.0 0.0 copy-start
  0.0 1.5 fusion.56
  1.5 0.0 copy-start.6
  1.5 0.0 copy-start.4
  1.5 0.0 copy-start.2
  1.5 0.0 copy-start.5
  1.5 1.4 collective-permute-start.1
  2.9 0.0 copy-start.3
  2.9 0.0 copy-start.7
  3.0 3.1 collective-permute-start
  6.0 4.8 %constant_dynamic-update-slice_fusion.1 = f32[4,4,64,1025]{3,2,1,0:T(8,128)} fusion(f32[4,4,64,1024]{3,2,1,0:T(8,128)} %param.10), kind=kLoop, calls=%fused_computation.96 | loop fusion | bytes 8388608
  10.8 0.0 copy-done.6
  10.8 0.6 slice_bitcast_fusion.8.types_ref
  11.5 0.0 copy-done.4
  11.6 0.0 copy-done.2
  11.6 0.0 copy-done.5
  11.6 0.5 convolution_bitcast_fusion
  12.1 0.1 copy.13
  12.3 0.0 copy-done
  12.3 0.5 convolution_bitcast_fusion.1
  12.8 0.1 copy.11
  12.9 0.0 copy-done.3
  12.9 0.0 copy-done.7
  12.9 0.6 broadcast_divide_fusion
  13.6 1.0 pad_maximum_fusion.1
  14.5 0.6 div.22.coeff_ref
  15.1 0.0 collective-permute-done.1
  15.1 0.9 constant_dynamic-update-slice_fusion
  16.1 4.7 %fusion.4 = f32[4,64,1024]{2,1,0:T(8,128)S(1)} fusion(f32[6,1024]{1,0:T(8,128)S(1)} %fusion.44, f32[4,4,64,1025]{3,2,1,0:T(8,128)} %constant_dynamic-update-slice_fusion, f32[6,64,64]{2,1,0:T(8,128)S(1)} %copy-done), kind=kOutput, calls=%fused_computation.9 | convolution fusion | flops 606863360 | bytes 2220032 | tf_op jit(solution)/shard_map/tpq,rqw->trpw/dot_general | solution.py:29
  20.8 0.0 copy-start.1
  20.8 4.7 %fusion.6 = f32[4,64,1024]{2,1,0:T(8,128)S(1)} fusion(f32[6,1024]{1,0:T(8,128)S(1)} %fusion.42, f32[4,4,64,1025]{3,2,1,0:T(8,128)} %constant_dynamic-update-slice_fusion, f32[6,64,64]{2,1,0:T(8,128)S(1)} %copy-done), kind=kOutput, calls=%fused_computation.13 | convolution fusion | flops 606863360 | bytes 2220032 | tf_op jit(solution)/shard_map/tpq,rqw->trpw/dot_general | solution.py:29
  25.4 4.5 %fusion = f32[4,64,1024]{2,1,0:T(8,128)S(1)} fusion(f32[6,1024]{1,0:T(8,128)S(1)} %fusion.48, f32[4,4,64,1025]{3,2,1,0:T(8,128)} %constant_dynamic-update-slice_fusion, f32[6,64,64]{2,1,0:T(8,128)S(1)} %copy-done), kind=kOutput, calls=%fused_computation.1 | convolution fusion | flops 606863360 | bytes 2220032 | tf_op jit(solution)/shard_map/tpq,rqw->trpw/dot_general | solution.py:29
  30.0 4.5 %fusion.2 = f32[4,64,1024]{2,1,0:T(8,128)S(1)} fusion(f32[6,1024]{1,0:T(8,128)S(1)} %fusion.46, f32[4,4,64,1025]{3,2,1,0:T(8,128)} %constant_dynamic-update-slice_fusion, f32[6,64,64]{2,1,0:T(8,128)S(1)} %copy-done), kind=kOutput, calls=%fused_computation.5 | convolution fusion | flops 606863360 | bytes 2220032 | tf_op jit(solution)/shard_map/tpq,rqw->trpw/dot_general | solution.py:29
  34.5 0.0 collective-permute-done
  34.5 0.0 copy-done.1
  34.5 3.2 fusion.5
  37.8 3.3 fusion.7
  41.0 0.7 fusion.26
  41.7 3.3 fusion.1
  45.0 0.0 copy-start.8
  45.0 3.5 fusion.3
  48.5 0.7 fusion.24
  49.1 0.0 copy-done.8
  49.2 4.4 %divide_bitcast_fusion.start_ref = f32[4,4,64,1024]{3,2,1,0:T(8,128)} fusion(f32[4,1024]{1,0:T(4,128)S(1)} %get-tuple-element.6, f32[4,4,64,1024]{3,2,1,0:T(8,128)S(1)} %copy-done.8, f32[1,4,64,1024]{3,2,1,0:T(8,128)S(1)} %get-tuple-element.29, f32[1,4,64,1024]{3,2,1,0:T(8,128)S(1)} %get-tuple-element.30, f32[1,4,64,1024]{3,2,1,0:T(8,128)S(1)} %get-tuple-element.31, ...), kind=kOutput, calls=%fused_computation.24 | convolution fusion | flops 407896064 | bytes 12615680 | tf_op jit(solution)/shard_map/pq,nrqc->nrpc/dot_general | solution.py:347
  53.6 331.4 %shard_map.91 = f32[4,4,64,1024]{3,2,1,0:T(8,128)} custom-call(f32[4,4,64,1024]{3,2,1,0:T(8,128)} %divide_bitcast_fusion.start_ref, s32[4,1024]{1,0:T(4,128)} %slice_bitcast_fusion.8.types_ref, f32[4,1024]{1,0:T(4,128)} %div.22.coeff_ref, f32[4,1024]{1,0:T(4,128)} %scale_ref.1, f32[4,1024]{1,0:T(4,128)} %get-tuple-element.5.inverse_ref, ...), custom_call_target="tpu_custom_call" | custom-call | tf_op jit(solution)/shard_map/pallas_call | solution.py:320
  385.0 4.8 %copy.27 = f32[4,4,64,1024]{3,2,1,0:T(8,128)} copy(f32[4,4,64,1024]{3,2,1,0:T(8,128)} %shard_map.91) | data formatting | bytes 8388608
  (12 shorter events, 0.2 us)
Async XLA Ops:
  0.0 12.3 %copy-start = (f32[6,64,64]{2,1,0:T(8,128)S(1)}, f32[6,64,64]{2,1,0:T(8,128)}, u32[]{:S(2)}) copy-start(f32[6,64,64]{2,1,0:T(8,128)} %param.15) | copy-start | bytes 294916
  1.5 9.3 %copy-start.6 = (s32[3,4,1024]{2,1,0:T(4,128)S(1)}, s32[3,4,1024]{2,1,0:T(4,128)}, u32[]{:S(2)}) copy-start(s32[3,4,1024]{2,1,0:T(4,128)} %param.11) | copy-start | bytes 147460
  1.5 10.0 %copy-start.4 = (f32[2,4,1024]{2,1,0:T(4,128)S(1)}, f32[2,4,1024]{2,1,0:T(4,128)}, u32[]{:S(2)}) copy-start(f32[2,4,1024]{2,1,0:T(4,128)} %param.13) | copy-start | bytes 98308
  1.5 10.1 %copy-start.2 = (f32[6,64,64]{2,1,0:T(8,128)S(1)}, f32[6,64,64]{2,1,0:T(8,128)}, u32[]{:S(2)}) copy-start(f32[6,64,64]{2,1,0:T(8,128)} %param.16) | copy-start | bytes 294916
  1.5 10.1 %copy-start.5 = (f32[64,64]{1,0:T(8,128)S(1)}, f32[64,64]{1,0:T(8,128)}, u32[]{:S(2)}) copy-start(f32[64,64]{1,0:T(8,128)} %param.17) | copy-start | bytes 49156
  1.5 13.6 %collective-permute-start.1 = (f32[4,4,64,1]{3,2,1,0:T(8,128)S(1)}, f32[4,4,64,1]{3,2,1,0:T(8,128)S(1)}, u32[]{:S(2)}, u32[]{:S(2)}) collective-permute-start(f32[4,4,64,1]{3,2,1,0:T(8,128)S(1)} %get-tuple-element.8), channel_id=1, source_target_pairs={{1,0},{2,1},{3,2},{5,4},{6,5},{7,6},{9,8},{10,9},{11,10},{13,12},{... | collective-permute-start | bytes 12296 | tf_op jit(solution)/shard_map/ppermute | solution.py:23
  2.9 10.0 %copy-start.3 = (f32[4,1024]{1,0:T(4,128)S(1)}, f32[4,1024]{1,0:T(4,128)}, u32[]{:S(2)}) copy-start(f32[4,1024]{1,0:T(4,128)} %scale_ref.1) | copy-start | bytes 49156
  2.9 10.0 %copy-start.7 = (f32[4,1024]{1,0:T(4,128)S(1)}, f32[4,1024]{1,0:T(4,128)}, u32[]{:S(2)}) copy-start(f32[4,1024]{1,0:T(4,128)} %param.14) | copy-start | bytes 49156
  3.0 31.6 %collective-permute-start = (f32[4,4,64,1]{3,2,1,0:T(8,128)S(1)}, f32[4,4,64,1]{3,2,1,0:T(8,128)S(1)}, u32[]{:S(2)}, u32[]{:S(2)}) collective-permute-start(f32[4,4,64,1]{3,2,1,0:T(8,128)S(1)} %get-tuple-element.7), channel_id=1, source_target_pairs={{0,1},{1,2},{2,3},{4,5},{5,6},{6,7},{8,9},{9,10},{10,11},{12,13},{... | collective-permute-start | bytes 12296 | tf_op jit(solution)/shard_map/ppermute | solution.py:20
  20.8 13.8 %copy-start.1 = (f32[4,4,64,1024]{3,2,1,0:T(8,128)S(1)}, f32[4,4,64,1024]{3,2,1,0:T(8,128)}, u32[]{:S(2)}) copy-start(f32[4,4,64,1024]{3,2,1,0:T(8,128)} %param.10) | copy-start | bytes 12582916
  45.0 4.2 %copy-start.8 = (f32[4,4,64,1024]{3,2,1,0:T(8,128)S(1)}, f32[4,4,64,1024]{3,2,1,0:T(8,128)}, u32[]{:S(2)}) copy-start(f32[4,4,64,1024]{3,2,1,0:T(8,128)} %param.9) | copy-start | bytes 12582916

commit v5 on v4

--- a/solution.py
+++ b/solution.py
@@ -343,8 +343,19 @@
     dof = up_blocks.shape[1]
     padded = padded_2(lagged, (("span", 3),), 1)
     denominator = stream_scale + span_scale[0] + span_scale[1] + absorb
-    span_terms = span_block(padded, face_types, span_scale, up_blocks, 0, columns)
-    start = jnp.einsum("pq,nrqc->nrpc", diag_inverse, rhs - span_terms, precision=fast)
+    kinds = up_blocks.shape[0]
+    lower_side = padded[..., : columns] * span_scale[0][:, None, None, :]
+    upper_side = padded[..., 2:] * span_scale[1][:, None, None, :]
+    lower_types = face_types[1][:, None, None, :]
+    upper_types = face_types[2][:, None, None, :]
+    faces = [
+        jnp.where(lower_types == kind, lower_side, 0.0) + jnp.where(upper_types == kind, upper_side, 0.0)
+        for kind in range(kinds)
+    ]
+    stacked = jnp.concatenate([rhs] + [-face for face in faces], axis=2)
+    tables = jnp.einsum("pq,tqs->tps", diag_inverse, up_blocks, precision=precise)
+    combined = jnp.concatenate([diag_inverse] + [tables[kind] for kind in range(kinds)], axis=1)
+    start = jnp.einsum("pk,nrkc->nrpc", combined, stacked, precision=fast)
     start = start / denominator[:, None, None, :]
     coeff = stream_scale / denominator
     inverse = 1.0 / denominator

time: 390 us -> 402 us (1.031)
  other arithmetic: 3.64 us -> 32.7 us
  matrix products: 37 us -> 17.5 us
    unnamed x0 -> x5, other arithmetic: none -> 25.1 us
    dot_general x9 -> x1, matrix products: 36.1 us -> 16.7 us  [per_device(): start = jnp.einsum('pk,nrkc->nrpc', combined, stacked, precision=fast)]
    concatenate x0 -> x1, other arithmetic: none -> 4.48 us  [per_device(): stacked = jnp.concatenate([rhs] + [-face for face in faces], axis=2)]
    unnamed x20 -> x16, local copies, waits for them, and re-layouts: 9.62 us -> 9.73 us
  transfers between devices with their start and end apart: 2 -> 2, of which waited for: 0 -> 0; matrix products, arithmetic and copies ran while one was open for 7% -> 3% of each run, Pallas kernels for 0% -> 0%
where the time goes in v5:
time: 402 us; the launch traced here: 398 us
  Pallas kernels  332 us (83%)
  other arithmetic  32.7 us (8%)
  matrix products  17.5 us (4%)
  local copies, waits for them, and re-layouts  13.5 us (3%)
    pallas_call x1, Pallas kernels, both_sweeps(): pl.pallas_call(functools.partial(both_kernel, length, width), out_shape=j...  332 us
    unnamed x5, other arithmetic  25.1 us
    dot_general x1, matrix products, per_device(): start = jnp.einsum('pk,nrkc->nrpc', combined, stacked, precision=fast)  16.7 us
    unnamed x16, local copies, waits for them, and re-layouts  9.73 us
  transfers between devices with their start and end apart: 2, of which 0 were waited for; matrix products, arithmetic and copies ran while one was open for 3% of the time, Pallas kernels for 0%

profile of v5, /device:TPU:0, one launch (start us, length us, event | category | flops | bytes accessed | tf_op | source)
XLA Modules:
  0.0 398.3 jit_solution(6951066360633366311)
XLA Ops:
  0.0 0.0 copy-start
  0.0 1.5 fusion.8
  1.5 1.3 collective-permute-start
  2.8 1.3 collective-permute-start.1
  4.1 0.8 compare_bitcast_fusion.1
  4.9 1.3 slice_bitcast_fusion.6.types_ref
  6.2 0.7 slice_bitcast_fusion.7
  6.9 0.0 copy-start.2
  6.9 0.0 copy-start.3
  6.9 0.0 copy-start.4
  7.0 0.0 copy-start.5
  7.0 0.0 copy-start.6
  7.0 4.9 %constant_dynamic-update-slice_fusion = f32[4,4,448,1024]{3,2,1,0:T(8,128)} fusion(f32[4,4,64,1024]{3,2,1,0:T(8,128)} %param.9), kind=kLoop, calls=%fused_computation.30 | loop fusion | bytes 8388608
  11.9 0.0 copy-done
  11.9 0.0 copy-done.2
  11.9 0.3 fusion.6
  12.3 0.0 copy-done.3
  12.3 0.5 convolution_bitcast_fusion
  12.8 0.1 copy.11
  12.9 0.0 copy-done.4
  12.9 0.0 copy-done.5
  13.0 0.0 copy-done.6
  13.0 0.6 broadcast_divide_fusion
  13.6 1.0 pad_maximum_fusion.2
  14.6 0.6 div.22.coeff_ref
  15.2 0.1 concatenate.22
  15.3 0.0 collective-permute-done
  15.3 0.0 collective-permute-done.1
  15.3 0.0 copy-start.1
  15.3 7.4 %negate_dynamic-update-slice_fusion.5 = f32[4,4,448,1024]{3,2,1,0:T(8,128)} fusion(f32[4,4,448,1024]{3,2,1,0:T(8,128)} %constant_dynamic-update-slice_fusion, pred[4,1024]{1,0:T(4,128)(4,1)S(1)} %get-tuple-element.30, pred[4,1024]{1,0:T(4,128)(4,1)S(1)} %get-tuple-element.29, f32[4,1024]{1,0:T(4,128)S(1)} %get-tuple-element.32, ...), kind=kLoop, calls=%fused_computation.10 | loop fusion | flops 8388608 | bytes 8437760
  22.7 0.0 copy-done.1
  22.7 4.4 %negate_dynamic-update-slice_fusion.4 = f32[4,4,448,1024]{3,2,1,0:T(8,128)} fusion(f32[4,4,448,1024]{3,2,1,0:T(8,128)} %negate_dynamic-update-slice_fusion.5, pred[4,1024]{1,0:T(4,128)(4,1)S(1)} %get-tuple-element.24, pred[4,1024]{1,0:T(4,128)(4,1)S(1)} %get-tuple-element.20, f32[4,1024]{1,0:T(4,128)S(1)} %get-tuple-element.32, ...), kind=kLoop, calls=%fused_computation.9 | loop fusion | flops 8388608 | bytes 8437760
  27.1 4.4 %negate_dynamic-update-slice_fusion.3 = f32[4,4,448,1024]{3,2,1,0:T(8,128)} fusion(f32[4,4,448,1024]{3,2,1,0:T(8,128)} %negate_dynamic-update-slice_fusion.4, pred[4,1024]{1,0:T(4,128)(4,1)S(1)} %get-tuple-element.25, pred[4,1024]{1,0:T(4,128)(4,1)S(1)} %get-tuple-element.21, f32[4,1024]{1,0:T(4,128)S(1)} %get-tuple-element.32, ...), kind=kLoop, calls=%fused_computation.8 | loop fusion | flops 8388608 | bytes 8437760
  31.5 4.5 %negate_dynamic-update-slice_fusion.2 = f32[4,4,448,1024]{3,2,1,0:T(8,128)} fusion(f32[4,4,448,1024]{3,2,1,0:T(8,128)} %negate_dynamic-update-slice_fusion.3, pred[4,1024]{1,0:T(4,128)(4,1)S(1)} %get-tuple-element.26, pred[4,1024]{1,0:T(4,128)(4,1)S(1)} %get-tuple-element.22, f32[4,1024]{1,0:T(4,128)S(1)} %get-tuple-element.32, ...), kind=kLoop, calls=%fused_computation.7 | loop fusion | flops 8388608 | bytes 8437760
  36.0 4.4 %negate_dynamic-update-slice_fusion.1 = f32[4,4,448,1024]{3,2,1,0:T(8,128)} fusion(f32[4,4,448,1024]{3,2,1,0:T(8,128)} %negate_dynamic-update-slice_fusion.2, pred[4,1024]{1,0:T(4,128)(4,1)S(1)} %get-tuple-element.27, pred[4,1024]{1,0:T(4,128)(4,1)S(1)} %get-tuple-element.23, f32[4,1024]{1,0:T(4,128)S(1)} %get-tuple-element.32, ...), kind=kLoop, calls=%fused_computation.6 | loop fusion | flops 8388608 | bytes 8437760
  40.4 4.5 %negate_dynamic-update-slice_fusion = f32[4,4,448,1024]{3,2,1,0:T(8,128)} fusion(f32[4,4,448,1024]{3,2,1,0:T(8,128)} %negate_dynamic-update-slice_fusion.1, pred[4,1024]{1,0:T(4,128)(4,1)S(1)} %get-tuple-element.28, pred[4,1024]{1,0:T(4,128)(4,1)S(1)} %get-tuple-element.19, f32[4,1024]{1,0:T(4,128)S(1)} %get-tuple-element.32, ...), kind=kLoop, calls=%fused_computation.5 | loop fusion | flops 8388608 | bytes 8437760 | tf_op jit(solution)/shard_map/concatenate | solution.py:355
  44.9 16.7 %divide_bitcast_fusion.start_ref = f32[4,4,64,1024]{3,2,1,0:T(8,128)} fusion(f32[4,1024]{1,0:T(4,128)S(1)} %get-tuple-element.6, f32[4,4,448,1024]{3,2,1,0:T(8,128)} %negate_dynamic-update-slice_fusion, f32[64,448]{1,0:T(8,128)S(1)} %concatenate.22), kind=kOutput, calls=%fused_computation.4 | convolution fusion | flops 2819620864 | bytes 33685504 | tf_op jit(solution)/shard_map/pk,nrkc->nrpc/dot_general | solution.py:358
  61.6 331.9 %shard_map.91 = f32[4,4,64,1024]{3,2,1,0:T(8,128)} custom-call(f32[4,4,64,1024]{3,2,1,0:T(8,128)} %divide_bitcast_fusion.start_ref, s32[4,1024]{1,0:T(4,128)} %slice_bitcast_fusion.6.types_ref, f32[4,1024]{1,0:T(4,128)} %div.22.coeff_ref, f32[4,1024]{1,0:T(4,128)} %scale_ref.1, f32[4,1024]{1,0:T(4,128)} %get-tuple-element.5.inverse_ref, ...), custom_call_target="tpu_custom_call" | custom-call | tf_op jit(solution)/shard_map/pallas_call | solution.py:320
  393.5 4.8 %copy.21 = f32[4,4,64,1024]{3,2,1,0:T(8,128)} copy(f32[4,4,64,1024]{3,2,1,0:T(8,128)} %shard_map.91) | data formatting | bytes 8388608
  (3 shorter events, 0.1 us)
Async XLA Ops:
  0.0 11.9 %copy-start = (f32[6,64,64]{2,1,0:T(8,128)S(1)}, f32[6,64,64]{2,1,0:T(8,128)}, u32[]{:S(2)}) copy-start(f32[6,64,64]{2,1,0:T(8,128)} %param.15) | copy-start | bytes 294916
  1.5 13.8 %collective-permute-start = (f32[4,4,64,1]{3,2,1,0:T(8,128)S(1)}, f32[4,4,64,1]{3,2,1,0:T(8,128)S(1)}, u32[]{:S(2)}, u32[]{:S(2)}) collective-permute-start(f32[4,4,64,1]{3,2,1,0:T(8,128)S(1)} %get-tuple-element.8), channel_id=1, source_target_pairs={{0,1},{1,2},{2,3},{4,5},{5,6},{6,7},{8,9},{9,10},{10,11},{12,13},{... | collective-permute-start | bytes 12296 | tf_op jit(solution)/shard_map/ppermute | solution.py:20
  2.8 12.5 %collective-permute-start.1 = (f32[4,4,64,1]{3,2,1,0:T(8,128)S(1)}, f32[4,4,64,1]{3,2,1,0:T(8,128)S(1)}, u32[]{:S(2)}, u32[]{:S(2)}) collective-permute-start(f32[4,4,64,1]{3,2,1,0:T(8,128)S(1)} %get-tuple-element.7), channel_id=1, source_target_pairs={{1,0},{2,1},{3,2},{5,4},{6,5},{7,6},{9,8},{10,9},{11,10},{13,12},{... | collective-permute-start | bytes 12296 | tf_op jit(solution)/shard_map/ppermute | solution.py:23
  6.9 4.9 %copy-start.2 = (f32[64,64]{1,0:T(8,128)S(1)}, f32[64,64]{1,0:T(8,128)}, u32[]{:S(2)}) copy-start(f32[64,64]{1,0:T(8,128)} %param.17) | copy-start | bytes 49156
  6.9 5.3 %copy-start.3 = (f32[6,64,64]{2,1,0:T(8,128)S(1)}, f32[6,64,64]{2,1,0:T(8,128)}, u32[]{:S(2)}) copy-start(f32[6,64,64]{2,1,0:T(8,128)} %param.16) | copy-start | bytes 294916
  6.9 6.0 %copy-start.4 = (f32[4,1024]{1,0:T(4,128)S(1)}, f32[4,1024]{1,0:T(4,128)}, u32[]{:S(2)}) copy-start(f32[4,1024]{1,0:T(4,128)} %scale_ref.1) | copy-start | bytes 49156
  7.0 6.0 %copy-start.5 = (f32[2,4,1024]{2,1,0:T(4,128)S(1)}, f32[2,4,1024]{2,1,0:T(4,128)}, u32[]{:S(2)}) copy-start(f32[2,4,1024]{2,1,0:T(4,128)} %param.13) | copy-start | bytes 98308
  7.0 6.0 %copy-start.6 = (f32[4,1024]{1,0:T(4,128)S(1)}, f32[4,1024]{1,0:T(4,128)}, u32[]{:S(2)}) copy-start(f32[4,1024]{1,0:T(4,128)} %param.14) | copy-start | bytes 49156
  15.3 7.5 %copy-start.1 = (f32[4,4,64,1024]{3,2,1,0:T(8,128)S(1)}, f32[4,4,64,1024]{3,2,1,0:T(8,128)}, u32[]{:S(2)}) copy-start(f32[4,4,64,1024]{3,2,1,0:T(8,128)} %param.10) | copy-start | bytes 12582916

commit v6 on v4

--- a/solution.py
+++ b/solution.py
@@ -57,6 +57,29 @@
     high = high.astype(jnp.bfloat16)
     low = low.astype(jnp.bfloat16)
     return jnp.concatenate([high, low, high], axis=1)
+
+
+def split_masked_table(tables):
+    kinds, dof, _ = tables.shape
+    flat = jnp.transpose(tables, (1, 0, 2)).reshape(dof, kinds * dof)
+    high = lax.reduce_precision(flat, exponent_bits=8, mantissa_bits=7)
+    low = flat - high
+    high = high.astype(jnp.bfloat16)
+    low = low.astype(jnp.bfloat16)
+    return jnp.concatenate([high, low, high], axis=1)
+
+
+def kernel_masked(table_ref, types, state):
+    dof = state.shape[0]
+    kinds = table_ref.shape[1] // (3 * dof)
+    high = state.astype(jnp.bfloat16)
+    low = (state - high.astype(jnp.float32)).astype(jnp.bfloat16)
+    zero = jnp.zeros_like(high)
+    masks = [types == kind for kind in range(kinds)]
+    highs = [jnp.where(mask, high, zero) for mask in masks]
+    lows = [jnp.where(mask, low, zero) for mask in masks]
+    stacked = jnp.concatenate(highs + highs + lows, axis=0)
+    return jnp.dot(table_ref[...], stacked, preferred_element_type=jnp.float32)
 
 
 def kernel_typed(table_ref, types, state):
@@ -240,7 +263,7 @@
         for row in range(rows):
             types = types_ref[pl.ds(row, 1), cols]
             coeff = coeff_ref[pl.ds(row, 1), cols]
-            state = start_ref[row, tracer, :, cols] - coeff * kernel_typed(up_ref, types, state)
+            state = start_ref[row, tracer, :, cols] - coeff * kernel_masked(up_ref, types, state)
             part_ref[row, tracer, :, cols] = state
         send_f[k] = state
 
@@ -261,7 +284,7 @@
             scale = scale_ref[pl.ds(row, 1), cols]
             solved = part_ref[row, tracer, :, cols] - state * inverse_ref[pl.ds(row, 1), cols]
             out_ref[row, tracer, :, cols] = solved
-            state = scale * kernel_typed(down_ref, types, solved)
+            state = scale * kernel_masked(down_ref, types, solved)
         send_b[k] = state
 
         @pl.when(jnp.logical_not(first_dev))
@@ -348,8 +371,8 @@
     start = start / denominator[:, None, None, :]
     coeff = stream_scale / denominator
     inverse = 1.0 / denominator
-    up_table = split_table(jnp.einsum("pq,tqs->tps", diag_inverse, up_blocks, precision=precise).reshape(-1, dof))
-    down_table = split_table(jnp.einsum("pq,tqs->tps", diag_inverse, down_blocks, precision=precise).reshape(-1, dof))
+    up_table = split_masked_table(jnp.einsum("pq,tqs->tps", diag_inverse, up_blocks, precision=precise))
+    down_table = split_masked_table(jnp.einsum("pq,tqs->tps", diag_inverse, down_blocks, precision=precise))
     return both_sweeps(LANES, start, face_types[0], coeff, stream_scale, inverse, up_table, down_table)
 
 

time: 390 us -> 370 us (0.949)
  Pallas kernels: 331 us -> 316 us
  matrix products: 37 us -> 32.9 us
    pallas_call x1, Pallas kernels: 331 us -> 316 us  [both_sweeps(): pl.pallas_call(functools.partial(both_kernel, length, width), out_shape=j...]
    dot_general x8, matrix products: 31.6 us -> 26.1 us  [typed_product(): jnp.einsum('tpq,rqw->trpw', blocks_table, state_in, precision=fast)]
    unnamed x20 -> x16, local copies, waits for them, and re-layouts: 9.62 us -> 7.43 us
  transfers between devices with their start and end apart: 2 -> 2, of which waited for: 0 -> 0; matrix products, arithmetic and copies ran while one was open for 7% -> 6% of each run, Pallas kernels for 0% -> 0%
where the time goes in v6:
time: 370 us; the launch traced here: 369 us
  Pallas kernels  316 us (85%)
  matrix products  32.9 us (9%)
  local copies, waits for them, and re-layouts  12.6 us (3%)
  starting transfers between devices  4.35 us (1%)
    pallas_call x1, Pallas kernels, both_sweeps(): pl.pallas_call(functools.partial(both_kernel, length, width), out_shape=j...  316 us
    dot_general x8, matrix products, typed_product(): jnp.einsum('tpq,rqw->trpw', blocks_table, state_in, precision=fast)  26.1 us
    unnamed x16, local copies, waits for them, and re-layouts  7.43 us
  transfers between devices with their start and end apart: 2, of which 0 were waited for; matrix products, arithmetic and copies ran while one was open for 6% of the time, Pallas kernels for 0%

profile of v6, /device:TPU:0, one launch (start us, length us, event | category | flops | bytes accessed | tf_op | source)
XLA Modules:
  0.0 369.2 jit_solution(1275004010060420183)
XLA Ops:
  0.0 0.0 copy-start
  0.0 0.0 copy-start.3
  0.0 0.0 copy-start.2
  0.0 0.0 copy-start.5
  0.0 1.5 fusion.58
  1.5 1.3 collective-permute-start.1
  2.8 3.1 collective-permute-start
  5.8 1.0 fusion.59
  6.8 1.3 slice_bitcast_fusion.8.types_ref
  8.2 0.9 fusion.60
  9.1 1.3 fusion.39
  10.4 0.1 copy.13
  10.5 0.1 reshape.260
  10.6 0.0 copy-done
  10.7 1.1 fusion.41
  11.7 0.1 copy.12
  11.9 0.1 reshape.259
  12.0 0.0 copy-done.3
  12.0 0.0 copy-done.2
  12.0 0.0 copy-done.5
  12.0 0.6 broadcast_divide_fusion
  12.6 0.7 pad_maximum_fusion.1
  13.3 2.6 constant_dynamic-update-slice_fusion.1
  16.0 0.6 div.22.coeff_ref
  16.6 0.0 collective-permute-done.1
  16.6 3.2 fusion.4
  19.9 0.0 copy-start.1
  19.9 3.2 fusion.6
  23.1 3.2 fusion
  26.4 3.2 fusion.2
  29.6 0.0 collective-permute-done
  29.6 0.0 copy-done.1
  29.6 3.3 fusion.5
  32.9 3.3 fusion.7
  36.2 0.7 fusion.26
  36.8 3.3 fusion.1
  40.1 0.0 copy-start.4
  40.1 0.0 copy-start.6
  40.1 3.4 fusion.3
  43.5 0.7 fusion.24
  44.2 0.0 copy-done.4
  44.2 0.0 copy-done.6
  44.2 4.4 %divide_bitcast_fusion.start_ref = f32[4,4,64,1024]{3,2,1,0:T(8,128)} fusion(f32[4,1024]{1,0:T(4,128)S(1)} %get-tuple-element.6, f32[4,4,64,1024]{3,2,1,0:T(8,128)S(1)} %copy-done.6, f32[1,4,64,1024]{3,2,1,0:T(8,128)S(1)} %get-tuple-element.29, f32[1,4,64,1024]{3,2,1,0:T(8,128)S(1)} %get-tuple-element.30, f32[1,4,64,1024]{3,2,1,0:T(8,128)S(1)} %get-tuple-element.31, ...), kind=kOutput, calls=%fused_computation.24 | convolution fusion | flops 407896064 | bytes 12615680 | tf_op jit(solution)/shard_map/pq,nrqc->nrpc/dot_general | solution.py:370
  48.7 315.7 %shard_map.91 = f32[4,4,64,1024]{3,2,1,0:T(8,128)} custom-call(f32[4,4,64,1024]{3,2,1,0:T(8,128)} %divide_bitcast_fusion.start_ref, s32[4,1024]{1,0:T(4,128)} %slice_bitcast_fusion.8.types_ref, f32[4,1024]{1,0:T(4,128)} %div.22.coeff_ref, f32[4,1024]{1,0:T(4,128)} %scale_ref.1, f32[4,1024]{1,0:T(4,128)} %get-tuple-element.5.inverse_ref, ...), custom_call_target="tpu_custom_call" | custom-call | tf_op jit(solution)/shard_map/pallas_call | solution.py:343
  364.4 4.8 %copy.25 = f32[4,4,64,1024]{3,2,1,0:T(8,128)} copy(f32[4,4,64,1024]{3,2,1,0:T(8,128)} %shard_map.91) | data formatting | bytes 8388608
  (11 shorter events, 0.1 us)
Async XLA Ops:
  0.0 10.6 %copy-start = (f32[6,64,64]{2,1,0:T(8,128)S(1)}, f32[6,64,64]{2,1,0:T(8,128)}, u32[]{:S(2)}) copy-start(f32[6,64,64]{2,1,0:T(8,128)} %param.15) | copy-start | bytes 294916
  0.0 12.0 %copy-start.3 = (f32[2,4,1024]{2,1,0:T(4,128)S(1)}, f32[2,4,1024]{2,1,0:T(4,128)}, u32[]{:S(2)}) copy-start(f32[2,4,1024]{2,1,0:T(4,128)} %param.13) | copy-start | bytes 98308
  0.0 12.0 %copy-start.2 = (f32[4,1024]{1,0:T(4,128)S(1)}, f32[4,1024]{1,0:T(4,128)}, u32[]{:S(2)}) copy-start(f32[4,1024]{1,0:T(4,128)} %scale_ref.1) | copy-start | bytes 49156
  0.0 12.0 %copy-start.5 = (f32[4,1024]{1,0:T(4,128)S(1)}, f32[4,1024]{1,0:T(4,128)}, u32[]{:S(2)}) copy-start(f32[4,1024]{1,0:T(4,128)} %param.14) | copy-start | bytes 49156
  1.5 15.1 %collective-permute-start.1 = (f32[4,4,64,1]{3,2,1,0:T(8,128)S(1)}, f32[4,4,64,1]{3,2,1,0:T(8,128)S(1)}, u32[]{:S(2)}, u32[]{:S(2)}) collective-permute-start(f32[4,4,64,1]{3,2,1,0:T(8,128)S(1)} %get-tuple-element.8), channel_id=1, source_target_pairs={{1,0},{2,1},{3,2},{5,4},{6,5},{7,6},{9,8},{10,9},{11,10},{13,12},{... | collective-permute-start | bytes 12296 | tf_op jit(solution)/shard_map/ppermute | solution.py:23
  2.8 26.8 %collective-permute-start = (f32[4,4,64,1]{3,2,1,0:T(8,128)S(1)}, f32[4,4,64,1]{3,2,1,0:T(8,128)S(1)}, u32[]{:S(2)}, u32[]{:S(2)}) collective-permute-start(f32[4,4,64,1]{3,2,1,0:T(8,128)S(1)} %get-tuple-element.7), channel_id=1, source_target_pairs={{0,1},{1,2},{2,3},{4,5},{5,6},{6,7},{8,9},{9,10},{10,11},{12,13},{... | collective-permute-start | bytes 12296 | tf_op jit(solution)/shard_map/ppermute | solution.py:20
  19.9 9.8 %copy-start.1 = (f32[4,4,64,1024]{3,2,1,0:T(8,128)S(1)}, f32[4,4,64,1024]{3,2,1,0:T(8,128)}, u32[]{:S(2)}) copy-start(f32[4,4,64,1024]{3,2,1,0:T(8,128)} %param.10) | copy-start | bytes 12582916
  40.1 4.1 %copy-start.4 = (f32[64,64]{1,0:T(8,128)S(1)}, f32[64,64]{1,0:T(8,128)}, u32[]{:S(2)}) copy-start(f32[64,64]{1,0:T(8,128)} %param.17) | copy-start | bytes 49156
  40.1 4.1 %copy-start.6 = (f32[4,4,64,1024]{3,2,1,0:T(8,128)S(1)}, f32[4,4,64,1024]{3,2,1,0:T(8,128)}, u32[]{:S(2)}) copy-start(f32[4,4,64,1024]{3,2,1,0:T(8,128)} %param.9) | copy-start | bytes 12582916

commit v7 on v6

--- a/solution.py
+++ b/solution.py
@@ -364,10 +364,31 @@
 ):
     columns = rhs.shape[3]
     dof = up_blocks.shape[1]
-    padded = padded_2(lagged, (("span", 3),), 1)
     denominator = stream_scale + span_scale[0] + span_scale[1] + absorb
-    span_terms = span_block(padded, face_types, span_scale, up_blocks, 0, columns)
-    start = jnp.einsum("pq,nrqc->nrpc", diag_inverse, rhs - span_terms, precision=fast)
+    tables = jnp.einsum("pq,tqs->tps", diag_inverse, up_blocks, precision=precise)
+    count = lax.axis_size("span")
+    rightward = [(i, i + 1) for i in range(count - 1)]
+    leftward = [(i + 1, i) for i in range(count - 1)]
+    halo_low = lax.ppermute(lagged[..., columns - 1:], "span", rightward)
+    halo_high = lax.ppermute(lagged[..., :1], "span", leftward)
+    low_types = jnp.concatenate([face_types[1][:, 1:], face_types[1][:, :1]], axis=1)
+    high_types = jnp.concatenate([face_types[2][:, -1:], face_types[2][:, :-1]], axis=1)
+    low_scale = jnp.concatenate([span_scale[0][:, 1:], span_scale[0][:, :1]], axis=1)
+    high_scale = jnp.concatenate([span_scale[1][:, -1:], span_scale[1][:, :-1]], axis=1)
+    lows = []
+    highs = []
+    for row in range(rhs.shape[0]):
+        lows.append(low_scale[row] * typed_product(tables, low_types[row], lagged[row]))
+        highs.append(high_scale[row] * typed_product(tables, high_types[row], lagged[row]))
+    lows = jnp.stack(lows)
+    highs = jnp.stack(highs)
+    low_edge = jnp.einsum("npq,nrq->nrp", tables[face_types[1][:, 0]], halo_low[..., 0], precision=fast)
+    high_edge = jnp.einsum("npq,nrq->nrp", tables[face_types[2][:, -1]], halo_high[..., 0], precision=fast)
+    low_edge = low_edge * span_scale[0][:, None, None, 0]
+    high_edge = high_edge * span_scale[1][:, None, None, -1]
+    lower = jnp.concatenate([low_edge[..., None], lows[..., :-1]], axis=3)
+    upper = jnp.concatenate([highs[..., 1:], high_edge[..., None]], axis=3)
+    start = jnp.einsum("pq,nrqc->nrpc", diag_inverse, rhs, precision=fast) - lower - upper
     start = start / denominator[:, None, None, :]
     coeff = stream_scale / denominator
     inverse = 1.0 / denominator

time: 370 us -> 384 us (1.038)
  other arithmetic: 3.36 us -> 12.8 us
  local copies, waits for them, and re-layouts: 12.6 us -> 17.3 us
    dot_general x8 -> x4, matrix products: 26.1 us -> 16.9 us  [typed_product(): jnp.einsum('tpq,rqw->trpw', blocks_table, state_in, precision=fast)]
    dot_general x1 -> x3, matrix products: 4.45 us -> 12.1 us  [the longest x1 9.95 us: per_device(): jnp.einsum('pq,nrqc->nrpc', diag_inverse, rhs, precision=fast) - lower]
    mul x0 -> x8, other arithmetic: none -> 5.93 us  [the longest x4 4.48 us: per_device(): high_scale[row] * typed_product(tables, high_types[row], lagged[row])]
  transfers between devices with their start and end apart: 2 -> 2, of which waited for: 0 -> 0; matrix products, arithmetic and copies ran while one was open for 6% -> 11% of each run, Pallas kernels for 0% -> 0%
where the time goes in v7:
time: 384 us; the launch traced here: 380 us
  Pallas kernels  316 us (82%)
  matrix products  30.6 us (8%)
  local copies, waits for them, and re-layouts  17.3 us (5%)
  other arithmetic  12.8 us (3%)
    pallas_call x1, Pallas kernels, both_sweeps(): pl.pallas_call(functools.partial(both_kernel, length, width), out_shape=j...  316 us
    dot_general x4, matrix products, typed_product(): jnp.einsum('tpq,rqw->trpw', blocks_table, state_in, precision=fast)  16.9 us
    dot_general x1, matrix products, per_device(): jnp.einsum('pq,nrqc->nrpc', diag_inverse, rhs, precision=fast) - lower  9.95 us
  transfers between devices with their start and end apart: 2, of which 0 were waited for; matrix products, arithmetic and copies ran while one was open for 11% of the time, Pallas kernels for 0%

profile of v7, /device:TPU:0, one launch (start us, length us, event | category | flops | bytes accessed | tf_op | source)
XLA Modules:
  0.0 379.9 jit_solution(3916314013050181081)
XLA Ops:
  0.0 1.5 fusion.54
  1.5 0.8 copy.51
  2.3 1.9 collective-permute-start
  4.2 0.8 copy.52
  5.0 1.3 collective-permute-start.1
  6.3 0.7 slice_bitcast_fusion.3
  7.0 0.7 slice_reduce_fusion.1
  7.7 1.4 slice_bitcast_fusion
  9.2 0.7 fusion.52
  9.9 0.1 fusion.41
  10.0 0.1 fusion.47
  10.1 1.3 slice_reduce_fusion
  11.4 0.6 fusion.37
  12.0 0.6 fusion.33
  12.6 0.6 pad_clamp_fusion.1
  13.2 1.2 fusion.28
  14.5 0.1 copy.50
  14.6 0.7 fusion.23
  15.3 0.3 fusion.26
  15.6 0.1 copy.33
  15.7 0.1 reshape.226
  15.8 5.3 %multiply_reduce_fusion.5 = (f32[64,4,1024]{2,0,1:T(8,128)S(1)}, f32[64,4,1024]{2,0,1:T(8,128)S(1)}) fusion(f32[6,1024]{1,0:T(8,128)S(1)} %fusion.32, f32[6,1024]{1,0:T(8,128)S(1)} %fusion.36, f32[4,4,64,1024]{3,2,1,0:T(8,128)} %param.10, f32[6,64,64]{2,1,0:T(8,128)S(1)} %fusion.28), kind=kOutput, calls=%fused_computation.7 | convolution fusion | flops 609746944 | bytes 3293184 | tf_op jit(solution)/shard_map/tpq,rqw->trpw/dot_general | solution.py:29
  21.1 0.1 fusion.50
  21.2 0.1 bitcast_multiply_fusion.5
  21.4 3.9 %multiply_reduce_fusion.6 = (f32[64,4,1024]{2,0,1:T(8,128)S(1)}, f32[64,4,1024]{2,0,1:T(8,128)S(1)}) fusion(f32[6,1024]{1,0:T(8,128)S(1)} %fusion.31, f32[6,1024]{1,0:T(8,128)S(1)} %fusion.35, f32[4,4,64,1024]{3,2,1,0:T(8,128)S(1)} %copy-done.1, f32[6,64,64]{2,1,0:T(8,128)S(1)} %fusion.28), kind=kOutput, calls=%fused_computation.8 | convolution fusion | flops 609746944 | bytes 3407872 | tf_op jit(solution)/shard_map/tpq,rqw->trpw/dot_general | solution.py:29
  25.2 0.1 bitcast_multiply_fusion.6
  25.4 3.9 %multiply_reduce_fusion.7 = (f32[64,4,1024]{2,0,1:T(8,128)S(1)}, f32[64,4,1024]{2,0,1:T(8,128)S(1)}) fusion(f32[6,1024]{1,0:T(8,128)S(1)} %fusion.30, f32[6,1024]{1,0:T(8,128)S(1)} %fusion.34, f32[4,4,64,1024]{3,2,1,0:T(8,128)S(1)} %copy-done.1, f32[6,64,64]{2,1,0:T(8,128)S(1)} %fusion.28), kind=kOutput, calls=%fused_computation.9 | convolution fusion | flops 609746944 | bytes 3407872 | tf_op jit(solution)/shard_map/tpq,rqw->trpw/dot_general | solution.py:29
  29.2 0.1 bitcast_multiply_fusion.7
  29.4 0.1 fusion.44
  29.5 1.1 bitcast_multiply_fusion.1
  30.6 1.2 bitcast_multiply_fusion.2
  31.7 1.1 bitcast_multiply_fusion.3
  32.9 3.9 %multiply_reduce_fusion.4 = (f32[64,4,1024]{2,0,1:T(8,128)S(1)}, f32[64,4,1024]{2,0,1:T(8,128)S(1)}) fusion(f32[6,1024]{1,0:T(8,128)S(1)} %copy-done.9, f32[6,1024]{1,0:T(8,128)S(1)} %copy-done.8, f32[4,4,64,1024]{3,2,1,0:T(8,128)S(1)} %copy-done.1, f32[6,64,64]{2,1,0:T(8,128)S(1)} %fusion.28), kind=kOutput, calls=%fused_computation.6 | convolution fusion | flops 609746944 | bytes 3407872 | tf_op jit(solution)/shard_map/tpq,rqw->trpw/dot_general | solution.py:29
  36.8 1.1 bitcast_multiply_fusion.4
  37.9 1.1 bitcast_multiply_fusion
  39.0 0.6 broadcast_divide_fusion
  39.7 0.7 pad_maximum_fusion.6
  40.4 0.6 pad_clamp_fusion
  41.0 1.3 gather_fusion
  42.3 1.3 gather_fusion.1
  43.7 1.3 div.19.coeff_ref
  45.0 1.1 fusion.6
  46.1 1.1 copy.28
  47.1 1.1 fusion.5
  48.2 1.1 copy.31
  49.3 9.9 %fusion.2.start_ref = f32[4,4,64,1024]{3,2,1,0:T(8,128)} fusion(f32[1,4,64,1024]{3,2,1,0:T(8,128)} %bitcast_multiply_fusion, f32[1,4,64,1024]{3,2,1,0:T(8,128)} %bitcast_multiply_fusion.1, f32[1,4,64,1024]{3,2,1,0:T(8,128)} %bitcast_multiply_fusion.2, f32[1,4,64,1024]{3,2,1,0:T(8,128)} %bitcast_multiply_fusion.3, ...), kind=kOutput, calls=%fused_computation.13 | convolution fusion | flops 414187520 | bytes 16818176 | tf_op jit(solution)/shard_map/pq,nrqc->nrpc/dot_general | solution.py:391
  59.2 315.9 %shard_map.91 = f32[4,4,64,1024]{3,2,1,0:T(8,128)} custom-call(f32[4,4,64,1024]{3,2,1,0:T(8,128)} %fusion.2.start_ref, s32[4,1024]{1,0:T(4,128)} %get-tuple-element.21.types_ref, f32[4,1024]{1,0:T(4,128)} %div.19.coeff_ref, f32[4,1024]{1,0:T(4,128)} %scale_ref.1, f32[4,1024]{1,0:T(4,128)} %get-tuple-element.13.inverse_ref, ...), custom_call_target="tpu_custom_call" | custom-call | tf_op jit(solution)/shard_map/pallas_call | solution.py:343
  375.1 4.8 %copy.54 = f32[4,4,64,1024]{3,2,1,0:T(8,128)} copy(f32[4,4,64,1024]{3,2,1,0:T(8,128)} %shard_map.91) | data formatting | bytes 8388608
  (37 shorter events, 0.3 us)
Async XLA Ops:
  0.0 13.2 %copy-start = (f32[6,64,64]{2,1,0:T(8,128)S(1)}, f32[6,64,64]{2,1,0:T(8,128)}, u32[]{:S(2)}) copy-start(f32[6,64,64]{2,1,0:T(8,128)} %param.15) | copy-start | bytes 294916
  0.0 15.2 %copy-start.7 = (f32[64,64]{1,0:T(8,128)S(1)}, f32[64,64]{1,0:T(8,128)}, u32[]{:S(2)}) copy-start(f32[64,64]{1,0:T(8,128)} %param.17) | copy-start | bytes 49156
  0.0 15.2 %copy-start.2 = (f32[6,64,64]{2,1,0:T(8,128)S(1)}, f32[6,64,64]{2,1,0:T(8,128)}, u32[]{:S(2)}) copy-start(f32[6,64,64]{2,1,0:T(8,128)} %param.16) | copy-start | bytes 294916
  2.3 42.7 %collective-permute-start = (f32[4,4,64,1]{2,1,0,3:T(4,128)}, f32[4,4,64,1]{2,1,0,3:T(4,128)}, u32[]{:S(2)}, u32[]{:S(2)}) collective-permute-start(f32[4,4,64,1]{2,1,0,3:T(4,128)} %copy.51), channel_id=1, source_target_pairs={{0,1},{1,2},{2,3},{4,5},{5,6},{6,7},{8,9},{9,10},{10,11},{12,13},{... | collective-permute-start | bytes 12296 | tf_op jit(solution)/shard_map/ppermute | solution.py:372
  5.0 42.2 %collective-permute-start.1 = (f32[4,4,64,1]{2,1,0,3:T(4,128)}, f32[4,4,64,1]{2,1,0,3:T(4,128)}, u32[]{:S(2)}, u32[]{:S(2)}) collective-permute-start(f32[4,4,64,1]{2,1,0,3:T(4,128)} %copy.52), channel_id=1, source_target_pairs={{1,0},{2,1},{3,2},{5,4},{6,5},{7,6},{9,8},{10,9},{11,10},{13,12},{... | collective-permute-start | bytes 12296 | tf_op jit(solution)/shard_map/ppermute | solution.py:373
  15.8 5.6 %copy-start.1 = (f32[4,4,64,1024]{3,2,1,0:T(8,128)S(1)}, f32[4,4,64,1024]{3,2,1,0:T(8,128)}, u32[]{:S(2)}) copy-start(f32[4,4,64,1024]{3,2,1,0:T(8,128)} %param.10) | copy-start | bytes 12582916
  25.3 4.0 %copy-start.11 = (f32[4,1]{1,0:T(4,128)S(1)}, f32[4,1]{1,0:T(4,128)}, u32[]{:S(2)}) copy-start(f32[4,1]{1,0:T(4,128)} %get-tuple-element.43) | copy-start | bytes 52
  29.2 3.6 copy-start.8
  29.2 3.6 copy-start.9
  32.9 6.2 %copy-start.5 = (f32[4,1024]{1,0:T(4,128)S(1)}, f32[4,1024]{1,0:T(4,128)}, u32[]{:S(2)}) copy-start(f32[4,1024]{1,0:T(4,128)} %scale_ref.1) | copy-start | bytes 49156
  32.9 6.2 %copy-start.6 = (f32[2,4,1024]{2,1,0:T(4,128)S(1)}, f32[2,4,1024]{2,1,0:T(4,128)}, u32[]{:S(2)}) copy-start(f32[2,4,1024]{2,1,0:T(4,128)} %param.13) | copy-start | bytes 98308
  32.9 6.2 %copy-start.10 = (f32[4,1024]{1,0:T(4,128)S(1)}, f32[4,1024]{1,0:T(4,128)}, u32[]{:S(2)}) copy-start(f32[4,1024]{1,0:T(4,128)} %param.14) | copy-start | bytes 49156
  32.9 6.8 %copy-start.3 = (bf16[64,384]{1,0:T(8,128)(2,1)S(1)}, bf16[64,384]{1,0:T(8,128)(2,1)}, u32[]{:S(2)}) copy-start(bf16[64,384]{1,0:T(8,128)(2,1)} %get-tuple-element.19) | copy-start | bytes 147460
  32.9 6.8 %copy-start.4 = (bf16[64,384]{1,0:T(8,128)(2,1)S(1)}, bf16[64,384]{1,0:T(8,128)(2,1)}, u32[]{:S(2)}) copy-start(bf16[64,384]{1,0:T(8,128)(2,1)} %get-tuple-element.20) | copy-start | bytes 147460
  32.9 7.5 %copy-start.12 = (s32[4]{0:T(128)S(1)}, s32[4]{0:T(128)}, u32[]{:S(2)}) copy-start(s32[4]{0:T(128)} %get-tuple-element.51) | copy-start | bytes 52

commit v8 on v6

--- a/solution.py
+++ b/solution.py
@@ -218,12 +218,20 @@
     )(start, types, coeff, denom, table)
 
 
-def both_kernel(length, width, start_ref, types_ref, coeff_ref, scale_ref, inverse_ref, up_ref, down_ref,
-                out_ref, part_ref, recv_f, send_f, recv_b, send_b, sems):
+def both_kernel(length, width, lend, start_ref, types_ref, coeff_ref, scale_ref, inverse_ref, up_ref, down_ref,
+                out_ref, part_ref, ext_start, ext_types, ext_small, ext_part, ext_out, returned,
+                recv_f, send_f, recv_b, send_b, sems, lend_sems, back_sems):
     me = lax.axis_index("stream")
+    side = lax.axis_index("span")
+    lender = side % 2 == 0
+    partner = side + 1 - 2 * (side % 2)
     rows, tracers, dof, columns = start_ref.shape
     sets = tracers
-    blocks = sets * (columns // width)
+    own = sets * (columns // width)
+    lent = sets * lend
+    kept = own - lent
+    first_cols = columns - lend * width
+    count = jnp.where(lender, kept, own + lent)
     first_dev = me == 0
     last_dev = me == length - 1
 
@@ -235,7 +243,42 @@
     def _():
         recv_b[...] = jnp.zeros(recv_b.shape, jnp.float32)
 
-    barrier_with_neighbours(me, length)
+    barrier = pltpu.get_barrier_semaphore()
+    for target in (me - 1, me + 1):
+        @pl.when(jnp.logical_and(target >= 0, target < length))
+        def _():
+            pl.semaphore_signal(barrier, inc=1, device_id={"stream": target},
+                                device_id_type=pl.DeviceIdType.MESH)
+    pl.semaphore_signal(barrier, inc=1, device_id={"span": partner}, device_id_type=pl.DeviceIdType.MESH)
+    ends = jnp.logical_or(first_dev, last_dev)
+
+    @pl.when(ends)
+    def _():
+        pl.semaphore_wait(barrier, 2)
+
+    @pl.when(jnp.logical_not(ends))
+    def _():
+        pl.semaphore_wait(barrier, 3)
+
+    lend_cols = pl.ds(first_cols, lend * width)
+    small_refs = (types_ref, coeff_ref, scale_ref, inverse_ref)
+
+    def lend_copies():
+        copies = [pltpu.make_async_remote_copy(
+            src_ref=start_ref.at[:, :, :, lend_cols], dst_ref=ext_start, send_sem=lend_sems.at[0, 0],
+            recv_sem=lend_sems.at[1, 0], device_id={"span": partner}, device_id_type=pl.DeviceIdType.MESH)]
+        for index, ref in enumerate(small_refs):
+            target = ext_types if index == 0 else ext_small.at[index - 1]
+            copies.append(pltpu.make_async_remote_copy(
+                src_ref=ref.at[:, lend_cols], dst_ref=target, send_sem=lend_sems.at[0, index + 1],
+                recv_sem=lend_sems.at[1, index + 1], device_id={"span": partner},
+                device_id_type=pl.DeviceIdType.MESH))
+        return copies
+
+    @pl.when(lender)
+    def _():
+        for copy in lend_copies():
+            copy.start()
 
     def copy_f(k):
         return pltpu.make_async_remote_copy(
@@ -247,43 +290,42 @@
             src_ref=send_b.at[k], dst_ref=recv_b.at[k], send_sem=sems.at[2, k], recv_sem=sems.at[3, k],
             device_id={"stream": me - 1}, device_id_type=pl.DeviceIdType.MESH)
 
-    def place(k):
-        tracer = k % sets
-        cols = pl.ds(pl.multiple_of((k // sets) * width, width), width)
-        return tracer, cols
-
-    def forward_block(k):
-        tracer, cols = place(k)
-
+    def copy_back(j):
+        tracer = j % sets
+        cols = pl.ds(pl.multiple_of((j // sets) * width, width), width)
+        return pltpu.make_async_remote_copy(
+            src_ref=ext_out.at[:, tracer, :, cols], dst_ref=returned.at[:, tracer, :, cols],
+            send_sem=back_sems.at[0, j], recv_sem=back_sems.at[1, j], device_id={"span": partner},
+            device_id_type=pl.DeviceIdType.MESH)
+
+    def forward_rows(k, tracer, cols, start, small, part):
         @pl.when(jnp.logical_not(first_dev))
         def _():
             copy_f(k).wait_recv()
 
         state = recv_f[k]
         for row in range(rows):
-            types = types_ref[pl.ds(row, 1), cols]
-            coeff = coeff_ref[pl.ds(row, 1), cols]
-            state = start_ref[row, tracer, :, cols] - coeff * kernel_masked(up_ref, types, state)
-            part_ref[row, tracer, :, cols] = state
+            types = small(0)[pl.ds(row, 1), cols]
+            coeff = small(1)[pl.ds(row, 1), cols]
+            state = start[row, tracer, :, cols] - coeff * kernel_masked(up_ref, types, state)
+            part[row, tracer, :, cols] = state
         send_f[k] = state
 
         @pl.when(jnp.logical_not(last_dev))
         def _():
             copy_f(k).start()
 
-    def backward_block(k):
-        tracer, cols = place(k)
-
+    def backward_rows(k, tracer, cols, small, part, out):
         @pl.when(jnp.logical_not(last_dev))
         def _():
             copy_b(k).wait_recv()
 
         state = recv_b[k]
         for row in range(rows - 1, -1, -1):
-            types = types_ref[pl.ds(row, 1), cols]
-            scale = scale_ref[pl.ds(row, 1), cols]
-            solved = part_ref[row, tracer, :, cols] - state * inverse_ref[pl.ds(row, 1), cols]
-            out_ref[row, tracer, :, cols] = solved
+            types = small(0)[pl.ds(row, 1), cols]
+            scale = small(2)[pl.ds(row, 1), cols]
+            solved = part[row, tracer, :, cols] - state * small(3)[pl.ds(row, 1), cols]
+            out[row, tracer, :, cols] = solved
             state = scale * kernel_masked(down_ref, types, solved)
         send_b[k] = state
 
@@ -291,8 +333,45 @@
         def _():
             copy_b(k).start()
 
-    lead = jnp.minimum(jnp.maximum(((2 * (length - 1) - 2 * me) * 17) // 6, 1), blocks)
-    tail = 2 * blocks - lead
+    def own_small(index):
+        return small_refs[index]
+
+    def ext_small_ref(index):
+        return ext_types if index == 0 else ext_small.at[index - 1]
+
+    def place(k):
+        return k % sets, pl.ds(pl.multiple_of((k // sets) * width, width), width)
+
+    def forward_block(k):
+        @pl.when(k < own)
+        def _():
+            tracer, cols = place(k)
+            forward_rows(k, tracer, cols, start_ref, own_small, part_ref)
+
+        @pl.when(k == own)
+        def _():
+            for copy in lend_copies():
+                copy.wait_recv()
+
+        @pl.when(k >= own)
+        def _():
+            tracer, cols = place(k - own)
+            forward_rows(k, tracer, cols, ext_start, ext_small_ref, ext_part)
+
+    def backward_block(k):
+        @pl.when(k < own)
+        def _():
+            tracer, cols = place(k)
+            backward_rows(k, tracer, cols, own_small, part_ref, out_ref)
+
+        @pl.when(k >= own)
+        def _():
+            tracer, cols = place(k - own)
+            backward_rows(k, tracer, cols, ext_small_ref, ext_part, ext_out)
+            copy_back(k - own).start()
+
+    lead = jnp.minimum(jnp.maximum(((2 * (length - 1) - 2 * me) * 17) // 6, 1), count)
+    tail = 2 * count - lead
 
     def step(s, carry):
         paired = jnp.logical_and(s >= lead, s < tail)
@@ -312,11 +391,11 @@
 
         @pl.when(s >= tail)
         def _():
-            backward_block(s - blocks)
-
-        return carry
-
-    lax.fori_loop(0, 2 * blocks, step, 0)
+            backward_block(s - count)
+
+        return carry
+
+    lax.fori_loop(0, 2 * count, step, 0)
 
     def drain_f(k, carry):
         copy_f(k).wait_send()
@@ -328,30 +407,61 @@
 
     @pl.when(jnp.logical_not(last_dev))
     def _():
-        lax.fori_loop(0, blocks, drain_f, 0)
+        lax.fori_loop(0, count, drain_f, 0)
 
     @pl.when(jnp.logical_not(first_dev))
     def _():
-        lax.fori_loop(0, blocks, drain_b, 0)
+        lax.fori_loop(0, count, drain_b, 0)
+
+    def drain_back(j, carry):
+        copy_back(j).wait_send()
+        return carry
+
+    def take_back(j, carry):
+        copy_back(j).wait_recv()
+        return carry
+
+    @pl.when(lender)
+    def _():
+        for copy in lend_copies():
+            copy.wait_send()
+        lax.fori_loop(0, lent, take_back, 0)
+        out_ref[:, :, :, lend_cols] = returned[...]
+
+    @pl.when(jnp.logical_not(lender))
+    def _():
+        lax.fori_loop(0, lent, drain_back, 0)
 
 
 def both_sweeps(width, start, types, coeff, scale, inverse, up_table, down_table):
     rows, tracers, dof, columns = start.shape
-    blocks = tracers * (columns // width)
+    groups = columns // width
+    lend = max(1, groups * 3 // 8)
+    blocks = tracers * (groups + lend)
+    lent = tracers * lend
     length = lax.axis_size("stream")
     vmem = pltpu.VMEM
+    ext_shape = (rows, tracers, dof, lend * width)
     return pl.pallas_call(
-        functools.partial(both_kernel, length, width),
+        functools.partial(both_kernel, length, width, lend),
         out_shape=jax.ShapeDtypeStruct(start.shape, jnp.float32),
         in_specs=[pl.BlockSpec(memory_space=vmem)] * 7,
         out_specs=pl.BlockSpec(memory_space=vmem),
         scratch_shapes=[
             pltpu.VMEM(start.shape, jnp.float32),
+            pltpu.VMEM(ext_shape, jnp.float32),
+            pltpu.VMEM((rows, lend * width), jnp.int32),
+            pltpu.VMEM((3, rows, lend * width), jnp.float32),
+            pltpu.VMEM(ext_shape, jnp.float32),
+            pltpu.VMEM(ext_shape, jnp.float32),
+            pltpu.VMEM(ext_shape, jnp.float32),
             pltpu.VMEM((blocks, dof, width), jnp.float32),
             pltpu.VMEM((blocks, dof, width), jnp.float32),
             pltpu.VMEM((blocks, dof, width), jnp.float32),
             pltpu.VMEM((blocks, dof, width), jnp.float32),
             pltpu.SemaphoreType.DMA((4, blocks)),
+            pltpu.SemaphoreType.DMA((2, 5)),
+            pltpu.SemaphoreType.DMA((2, lent)),
         ],
         compiler_params=pltpu.CompilerParams(
             collective_id=0, has_side_effects=True, vmem_limit_bytes=60 * 1024 * 1024
@@ -373,7 +483,8 @@
     inverse = 1.0 / denominator
     up_table = split_masked_table(jnp.einsum("pq,tqs->tps", diag_inverse, up_blocks, precision=precise))
     down_table = split_masked_table(jnp.einsum("pq,tqs->tps", diag_inverse, down_blocks, precision=precise))
-    return both_sweeps(LANES, start, face_types[0], coeff, stream_scale, inverse, up_table, down_table)
+    small = [face_types[0], coeff, stream_scale, inverse]
+    return both_sweeps(LANES, start, *small, up_table, down_table)
 
 
 def solution(mesh):

time: 370 us -> 350 us (0.946)
  Pallas kernels: 316 us -> 296 us
    pallas_call x1, Pallas kernels: 316 us -> 296 us  [both_sweeps(): pl.pallas_call(functools.partial(both_kernel, length, width, lend), out_s...]
  transfers between devices with their start and end apart: 2 -> 2, of which waited for: 0 -> 0; matrix products, arithmetic and copies ran while one was open for 6% -> 7% of each run, Pallas kernels for 0% -> 0%
where the time goes in v8:
time: 350 us; the launch traced here: 349 us
  Pallas kernels  296 us (85%)
  matrix products  32.9 us (9%)
  local copies, waits for them, and re-layouts  12.6 us (4%)
  starting transfers between devices  4.35 us (1%)
    pallas_call x1, Pallas kernels, both_sweeps(): pl.pallas_call(functools.partial(both_kernel, length, width, lend), out_s...  296 us
    dot_general x8, matrix products, typed_product(): jnp.einsum('tpq,rqw->trpw', blocks_table, state_in, precision=fast)  26.1 us
    unnamed x16, local copies, waits for them, and re-layouts  7.43 us
  transfers between devices with their start and end apart: 2, of which 0 were waited for; matrix products, arithmetic and copies ran while one was open for 7% of the time, Pallas kernels for 0%

profile of v8, /device:TPU:0, one launch (start us, length us, event | category | flops | bytes accessed | tf_op | source)
XLA Modules:
  0.0 349.2 jit_solution(5857748778169536045)
XLA Ops:
  0.0 0.0 copy-start
  0.0 0.0 copy-start.3
  0.0 0.0 copy-start.2
  0.0 0.0 copy-start.5
  0.0 1.5 fusion.58
  1.5 1.3 collective-permute-start.1
  2.8 3.1 collective-permute-start
  5.8 1.0 fusion.59
  6.8 1.3 slice_bitcast_fusion.8.types_ref
  8.2 0.9 fusion.60
  9.1 1.3 fusion.39
  10.4 0.1 copy.13
  10.5 0.1 reshape.260
  10.6 0.0 copy-done
  10.7 1.1 fusion.41
  11.7 0.1 copy.12
  11.9 0.1 reshape.259
  12.0 0.0 copy-done.3
  12.0 0.0 copy-done.2
  12.0 0.0 copy-done.5
  12.0 0.6 broadcast_divide_fusion
  12.6 0.7 pad_maximum_fusion.1
  13.3 2.6 constant_dynamic-update-slice_fusion.1
  16.0 0.6 div.22.coeff_ref
  16.6 0.0 collective-permute-done.1
  16.6 3.2 fusion.4
  19.9 0.0 copy-start.1
  19.9 3.2 fusion.6
  23.1 3.2 fusion
  26.4 3.2 fusion.2
  29.6 0.0 collective-permute-done
  29.6 0.0 copy-done.1
  29.6 3.3 fusion.5
  32.9 3.3 fusion.7
  36.2 0.7 fusion.26
  36.8 3.3 fusion.1
  40.1 0.0 copy-start.4
  40.1 0.0 copy-start.6
  40.1 3.4 fusion.3
  43.5 0.7 fusion.24
  44.2 0.0 copy-done.4
  44.2 0.0 copy-done.6
  44.2 4.4 %divide_bitcast_fusion.start_ref = f32[4,4,64,1024]{3,2,1,0:T(8,128)} fusion(f32[4,1024]{1,0:T(4,128)S(1)} %get-tuple-element.6, f32[4,4,64,1024]{3,2,1,0:T(8,128)S(1)} %copy-done.6, f32[1,4,64,1024]{3,2,1,0:T(8,128)S(1)} %get-tuple-element.29, f32[1,4,64,1024]{3,2,1,0:T(8,128)S(1)} %get-tuple-element.30, f32[1,4,64,1024]{3,2,1,0:T(8,128)S(1)} %get-tuple-element.31, ...), kind=kOutput, calls=%fused_computation.24 | convolution fusion | flops 407896064 | bytes 12615680 | tf_op jit(solution)/shard_map/pq,nrqc->nrpc/dot_general | solution.py:480
  48.7 295.8 %shard_map.91 = f32[4,4,64,1024]{3,2,1,0:T(8,128)} custom-call(f32[4,4,64,1024]{3,2,1,0:T(8,128)} %divide_bitcast_fusion.start_ref, s32[4,1024]{1,0:T(4,128)} %slice_bitcast_fusion.8.types_ref, f32[4,1024]{1,0:T(4,128)} %div.22.coeff_ref, f32[4,1024]{1,0:T(4,128)} %scale_ref.1, f32[4,1024]{1,0:T(4,128)} %get-tuple-element.5.inverse_ref, ...), custom_call_target="tpu_custom_call" | custom-call | tf_op jit(solution)/shard_map/pallas_call | solution.py:445
  344.4 4.8 %copy.25 = f32[4,4,64,1024]{3,2,1,0:T(8,128)} copy(f32[4,4,64,1024]{3,2,1,0:T(8,128)} %shard_map.91) | data formatting | bytes 8388608
  (11 shorter events, 0.1 us)
Async XLA Ops:
  0.0 10.6 %copy-start = (f32[6,64,64]{2,1,0:T(8,128)S(1)}, f32[6,64,64]{2,1,0:T(8,128)}, u32[]{:S(2)}) copy-start(f32[6,64,64]{2,1,0:T(8,128)} %param.15) | copy-start | bytes 294916
  0.0 12.0 %copy-start.3 = (f32[2,4,1024]{2,1,0:T(4,128)S(1)}, f32[2,4,1024]{2,1,0:T(4,128)}, u32[]{:S(2)}) copy-start(f32[2,4,1024]{2,1,0:T(4,128)} %param.13) | copy-start | bytes 98308
  0.0 12.0 %copy-start.2 = (f32[4,1024]{1,0:T(4,128)S(1)}, f32[4,1024]{1,0:T(4,128)}, u32[]{:S(2)}) copy-start(f32[4,1024]{1,0:T(4,128)} %scale_ref.1) | copy-start | bytes 49156
  0.0 12.0 %copy-start.5 = (f32[4,1024]{1,0:T(4,128)S(1)}, f32[4,1024]{1,0:T(4,128)}, u32[]{:S(2)}) copy-start(f32[4,1024]{1,0:T(4,128)} %param.14) | copy-start | bytes 49156
  1.5 15.1 %collective-permute-start.1 = (f32[4,4,64,1]{3,2,1,0:T(8,128)S(1)}, f32[4,4,64,1]{3,2,1,0:T(8,128)S(1)}, u32[]{:S(2)}, u32[]{:S(2)}) collective-permute-start(f32[4,4,64,1]{3,2,1,0:T(8,128)S(1)} %get-tuple-element.8), channel_id=1, source_target_pairs={{1,0},{2,1},{3,2},{5,4},{6,5},{7,6},{9,8},{10,9},{11,10},{13,12},{... | collective-permute-start | bytes 12296 | tf_op jit(solution)/shard_map/ppermute | solution.py:23
  2.8 26.8 %collective-permute-start = (f32[4,4,64,1]{3,2,1,0:T(8,128)S(1)}, f32[4,4,64,1]{3,2,1,0:T(8,128)S(1)}, u32[]{:S(2)}, u32[]{:S(2)}) collective-permute-start(f32[4,4,64,1]{3,2,1,0:T(8,128)S(1)} %get-tuple-element.7), channel_id=1, source_target_pairs={{0,1},{1,2},{2,3},{4,5},{5,6},{6,7},{8,9},{9,10},{10,11},{12,13},{... | collective-permute-start | bytes 12296 | tf_op jit(solution)/shard_map/ppermute | solution.py:20
  19.9 9.8 %copy-start.1 = (f32[4,4,64,1024]{3,2,1,0:T(8,128)S(1)}, f32[4,4,64,1024]{3,2,1,0:T(8,128)}, u32[]{:S(2)}) copy-start(f32[4,4,64,1024]{3,2,1,0:T(8,128)} %param.10) | copy-start | bytes 12582916
  40.1 4.1 %copy-start.4 = (f32[64,64]{1,0:T(8,128)S(1)}, f32[64,64]{1,0:T(8,128)}, u32[]{:S(2)}) copy-start(f32[64,64]{1,0:T(8,128)} %param.17) | copy-start | bytes 49156
  40.1 4.1 %copy-start.6 = (f32[4,4,64,1024]{3,2,1,0:T(8,128)S(1)}, f32[4,4,64,1024]{3,2,1,0:T(8,128)}, u32[]{:S(2)}) copy-start(f32[4,4,64,1024]{3,2,1,0:T(8,128)} %param.9) | copy-start | bytes 12582916

commit v9 on v8

--- a/solution.py
+++ b/solution.py
@@ -436,7 +436,7 @@
 def both_sweeps(width, start, types, coeff, scale, inverse, up_table, down_table):
     rows, tracers, dof, columns = start.shape
     groups = columns // width
-    lend = max(1, groups * 3 // 8)
+    lend = max(1, groups // 2)
     blocks = tracers * (groups + lend)
     lent = tracers * lend
     length = lax.axis_size("stream")

time: 350 us -> 345 us (0.986)
  Pallas kernels: 296 us -> 291 us
    pallas_call x1, Pallas kernels: 296 us -> 291 us  [both_sweeps(): pl.pallas_call(functools.partial(both_kernel, length, width, lend), out_s...]
where the time goes in v9:
time: 345 us; the launch traced here: 344 us
  Pallas kernels  291 us (84%)
  matrix products  32.9 us (10%)
  local copies, waits for them, and re-layouts  12.6 us (4%)
  starting transfers between devices  4.35 us (1%)
    pallas_call x1, Pallas kernels, both_sweeps(): pl.pallas_call(functools.partial(both_kernel, length, width, lend), out_s...  291 us
    dot_general x8, matrix products, typed_product(): jnp.einsum('tpq,rqw->trpw', blocks_table, state_in, precision=fast)  26.1 us
    unnamed x16, local copies, waits for them, and re-layouts  7.43 us
  transfers between devices with their start and end apart: 2, of which 0 were waited for; matrix products, arithmetic and copies ran while one was open for 7% of the time, Pallas kernels for 0%

profile of v9, /device:TPU:0, one launch (start us, length us, event | category | flops | bytes accessed | tf_op | source)
XLA Modules:
  0.0 344.4 jit_solution(4012330089658222553)
XLA Ops:
  0.0 0.0 copy-start
  0.0 0.0 copy-start.3
  0.0 0.0 copy-start.2
  0.0 0.0 copy-start.5
  0.0 1.5 fusion.58
  1.5 1.3 collective-permute-start.1
  2.8 3.1 collective-permute-start
  5.8 1.0 fusion.59
  6.8 1.3 slice_bitcast_fusion.8.types_ref
  8.2 0.9 fusion.60
  9.1 1.3 fusion.39
  10.4 0.1 copy.13
  10.5 0.1 reshape.260
  10.6 0.0 copy-done
  10.7 1.1 fusion.41
  11.7 0.1 copy.12
  11.9 0.1 reshape.259
  12.0 0.0 copy-done.3
  12.0 0.0 copy-done.2
  12.0 0.0 copy-done.5
  12.0 0.6 broadcast_divide_fusion
  12.6 0.7 pad_maximum_fusion.1
  13.3 2.6 constant_dynamic-update-slice_fusion.1
  16.0 0.6 div.22.coeff_ref
  16.6 0.0 collective-permute-done.1
  16.6 3.2 fusion.4
  19.9 0.0 copy-start.1
  19.9 3.2 fusion.6
  23.1 3.2 fusion
  26.4 3.2 fusion.2
  29.6 0.0 collective-permute-done
  29.6 0.0 copy-done.1
  29.6 3.3 fusion.5
  32.9 3.3 fusion.7
  36.2 0.7 fusion.26
  36.8 3.3 fusion.1
  40.1 0.0 copy-start.4
  40.1 0.0 copy-start.6
  40.1 3.4 fusion.3
  43.5 0.7 fusion.24
  44.2 0.0 copy-done.4
  44.2 0.0 copy-done.6
  44.2 4.4 %divide_bitcast_fusion.start_ref = f32[4,4,64,1024]{3,2,1,0:T(8,128)} fusion(f32[4,1024]{1,0:T(4,128)S(1)} %get-tuple-element.6, f32[4,4,64,1024]{3,2,1,0:T(8,128)S(1)} %copy-done.6, f32[1,4,64,1024]{3,2,1,0:T(8,128)S(1)} %get-tuple-element.29, f32[1,4,64,1024]{3,2,1,0:T(8,128)S(1)} %get-tuple-element.30, f32[1,4,64,1024]{3,2,1,0:T(8,128)S(1)} %get-tuple-element.31, ...), kind=kOutput, calls=%fused_computation.24 | convolution fusion | flops 407896064 | bytes 12615680 | tf_op jit(solution)/shard_map/pq,nrqc->nrpc/dot_general | solution.py:480
  48.7 290.9 %shard_map.91 = f32[4,4,64,1024]{3,2,1,0:T(8,128)} custom-call(f32[4,4,64,1024]{3,2,1,0:T(8,128)} %divide_bitcast_fusion.start_ref, s32[4,1024]{1,0:T(4,128)} %slice_bitcast_fusion.8.types_ref, f32[4,1024]{1,0:T(4,128)} %div.22.coeff_ref, f32[4,1024]{1,0:T(4,128)} %scale_ref.1, f32[4,1024]{1,0:T(4,128)} %get-tuple-element.5.inverse_ref, ...), custom_call_target="tpu_custom_call" | custom-call | tf_op jit(solution)/shard_map/pallas_call | solution.py:445
  339.6 4.8 %copy.25 = f32[4,4,64,1024]{3,2,1,0:T(8,128)} copy(f32[4,4,64,1024]{3,2,1,0:T(8,128)} %shard_map.91) | data formatting | bytes 8388608
  (11 shorter events, 0.1 us)
Async XLA Ops:
  0.0 10.6 %copy-start = (f32[6,64,64]{2,1,0:T(8,128)S(1)}, f32[6,64,64]{2,1,0:T(8,128)}, u32[]{:S(2)}) copy-start(f32[6,64,64]{2,1,0:T(8,128)} %param.15) | copy-start | bytes 294916
  0.0 12.0 %copy-start.3 = (f32[2,4,1024]{2,1,0:T(4,128)S(1)}, f32[2,4,1024]{2,1,0:T(4,128)}, u32[]{:S(2)}) copy-start(f32[2,4,1024]{2,1,0:T(4,128)} %param.13) | copy-start | bytes 98308
  0.0 12.0 %copy-start.2 = (f32[4,1024]{1,0:T(4,128)S(1)}, f32[4,1024]{1,0:T(4,128)}, u32[]{:S(2)}) copy-start(f32[4,1024]{1,0:T(4,128)} %scale_ref.1) | copy-start | bytes 49156
  0.0 12.0 %copy-start.5 = (f32[4,1024]{1,0:T(4,128)S(1)}, f32[4,1024]{1,0:T(4,128)}, u32[]{:S(2)}) copy-start(f32[4,1024]{1,0:T(4,128)} %param.14) | copy-start | bytes 49156
  1.5 15.1 %collective-permute-start.1 = (f32[4,4,64,1]{3,2,1,0:T(8,128)S(1)}, f32[4,4,64,1]{3,2,1,0:T(8,128)S(1)}, u32[]{:S(2)}, u32[]{:S(2)}) collective-permute-start(f32[4,4,64,1]{3,2,1,0:T(8,128)S(1)} %get-tuple-element.8), channel_id=1, source_target_pairs={{1,0},{2,1},{3,2},{5,4},{6,5},{7,6},{9,8},{10,9},{11,10},{13,12},{... | collective-permute-start | bytes 12296 | tf_op jit(solution)/shard_map/ppermute | solution.py:23
  2.8 26.8 %collective-permute-start = (f32[4,4,64,1]{3,2,1,0:T(8,128)S(1)}, f32[4,4,64,1]{3,2,1,0:T(8,128)S(1)}, u32[]{:S(2)}, u32[]{:S(2)}) collective-permute-start(f32[4,4,64,1]{3,2,1,0:T(8,128)S(1)} %get-tuple-element.7), channel_id=1, source_target_pairs={{0,1},{1,2},{2,3},{4,5},{5,6},{6,7},{8,9},{9,10},{10,11},{12,13},{... | collective-permute-start | bytes 12296 | tf_op jit(solution)/shard_map/ppermute | solution.py:20
  19.9 9.8 %copy-start.1 = (f32[4,4,64,1024]{3,2,1,0:T(8,128)S(1)}, f32[4,4,64,1024]{3,2,1,0:T(8,128)}, u32[]{:S(2)}) copy-start(f32[4,4,64,1024]{3,2,1,0:T(8,128)} %param.10) | copy-start | bytes 12582916
  40.1 4.1 %copy-start.4 = (f32[64,64]{1,0:T(8,128)S(1)}, f32[64,64]{1,0:T(8,128)}, u32[]{:S(2)}) copy-start(f32[64,64]{1,0:T(8,128)} %param.17) | copy-start | bytes 49156
  40.1 4.1 %copy-start.6 = (f32[4,4,64,1024]{3,2,1,0:T(8,128)S(1)}, f32[4,4,64,1024]{3,2,1,0:T(8,128)}, u32[]{:S(2)}) copy-start(f32[4,4,64,1024]{3,2,1,0:T(8,128)} %param.9) | copy-start | bytes 12582916

commit v10 on v9

--- a/solution.py
+++ b/solution.py
@@ -436,7 +436,7 @@
 def both_sweeps(width, start, types, coeff, scale, inverse, up_table, down_table):
     rows, tracers, dof, columns = start.shape
     groups = columns // width
-    lend = max(1, groups // 2)
+    lend = max(1, groups * 5 // 8)
     blocks = tracers * (groups + lend)
     lent = tracers * lend
     length = lax.axis_size("stream")

time: 345 us -> 344 us (level)
  no operation moved by 1% of the time
where the time goes in v10:
time: 344 us; the launch traced here: 343 us
  Pallas kernels  289 us (84%)
  matrix products  32.9 us (10%)
  local copies, waits for them, and re-layouts  12.6 us (4%)
  starting transfers between devices  4.35 us (1%)
    pallas_call x1, Pallas kernels, both_sweeps(): pl.pallas_call(functools.partial(both_kernel, length, width, lend), out_s...  289 us
    dot_general x8, matrix products, typed_product(): jnp.einsum('tpq,rqw->trpw', blocks_table, state_in, precision=fast)  26.1 us
    unnamed x16, local copies, waits for them, and re-layouts  7.43 us
  transfers between devices with their start and end apart: 2, of which 0 were waited for; matrix products, arithmetic and copies ran while one was open for 7% of the time, Pallas kernels for 0%

profile of v10, /device:TPU:0, one launch (start us, length us, event | category | flops | bytes accessed | tf_op | source)
XLA Modules:
  0.0 342.9 jit_solution(12456682978476063237)
XLA Ops:
  0.0 0.0 copy-start
  0.0 0.0 copy-start.3
  0.0 0.0 copy-start.2
  0.0 0.0 copy-start.5
  0.0 1.5 fusion.58
  1.5 1.3 collective-permute-start.1
  2.8 3.1 collective-permute-start
  5.8 1.0 fusion.59
  6.8 1.3 slice_bitcast_fusion.8.types_ref
  8.2 0.9 fusion.60
  9.1 1.3 fusion.39
  10.4 0.1 copy.13
  10.5 0.1 reshape.260
  10.6 0.0 copy-done
  10.7 1.1 fusion.41
  11.7 0.1 copy.12
  11.9 0.1 reshape.259
  12.0 0.0 copy-done.3
  12.0 0.0 copy-done.2
  12.0 0.0 copy-done.5
  12.0 0.6 broadcast_divide_fusion
  12.6 0.7 pad_maximum_fusion.1
  13.3 2.6 constant_dynamic-update-slice_fusion.1
  16.0 0.6 div.22.coeff_ref
  16.6 0.0 collective-permute-done.1
  16.6 3.2 fusion.4
  19.9 0.0 copy-start.1
  19.9 3.2 fusion.6
  23.1 3.2 fusion
  26.4 3.2 fusion.2
  29.6 0.0 collective-permute-done
  29.6 0.0 copy-done.1
  29.6 3.3 fusion.5
  32.9 3.3 fusion.7
  36.2 0.7 fusion.26
  36.8 3.3 fusion.1
  40.1 0.0 copy-start.4
  40.1 0.0 copy-start.6
  40.1 3.4 %fusion.3 = f32[4,64,1024]{2,1,0:T(8,128)S(1)} fusion(f32[6,1024]{1,0:T(8,128)S(1)} %fusion.47, f32[4,4,64,1024]{3,2,1,0:T(8,128)S(1)} %copy-done.1, f32[4,4,64,1]{3,2,1,0:T(8,128)S(1)} %collective-permute-done, f32[6,64,64]{2,1,0:T(8,128)S(1)} %copy-done), kind=kOutput, calls=%fused_computation.7 | convolution fusion | flops 607125504 | bytes 5369856 | tf_op jit(solution)/shard_map/tpq,rqw->trpw/dot_general | solution.py:29
  43.5 0.7 fusion.24
  44.2 0.0 copy-done.4
  44.2 0.0 copy-done.6
  44.2 4.4 %divide_bitcast_fusion.start_ref = f32[4,4,64,1024]{3,2,1,0:T(8,128)} fusion(f32[4,1024]{1,0:T(4,128)S(1)} %get-tuple-element.6, f32[4,4,64,1024]{3,2,1,0:T(8,128)S(1)} %copy-done.6, f32[1,4,64,1024]{3,2,1,0:T(8,128)S(1)} %get-tuple-element.29, f32[1,4,64,1024]{3,2,1,0:T(8,128)S(1)} %get-tuple-element.30, f32[1,4,64,1024]{3,2,1,0:T(8,128)S(1)} %get-tuple-element.31, ...), kind=kOutput, calls=%fused_computation.24 | convolution fusion | flops 407896064 | bytes 12615680 | tf_op jit(solution)/shard_map/pq,nrqc->nrpc/dot_general | solution.py:480
  48.7 289.4 %shard_map.91 = f32[4,4,64,1024]{3,2,1,0:T(8,128)} custom-call(f32[4,4,64,1024]{3,2,1,0:T(8,128)} %divide_bitcast_fusion.start_ref, s32[4,1024]{1,0:T(4,128)} %slice_bitcast_fusion.8.types_ref, f32[4,1024]{1,0:T(4,128)} %div.22.coeff_ref, f32[4,1024]{1,0:T(4,128)} %scale_ref.1, f32[4,1024]{1,0:T(4,128)} %get-tuple-element.5.inverse_ref, ...), custom_call_target="tpu_custom_call" | custom-call | tf_op jit(solution)/shard_map/pallas_call | solution.py:445
  338.1 4.8 %copy.25 = f32[4,4,64,1024]{3,2,1,0:T(8,128)} copy(f32[4,4,64,1024]{3,2,1,0:T(8,128)} %shard_map.91) | data formatting | bytes 8388608
  (11 shorter events, 0.1 us)
Async XLA Ops:
  0.0 10.6 %copy-start = (f32[6,64,64]{2,1,0:T(8,128)S(1)}, f32[6,64,64]{2,1,0:T(8,128)}, u32[]{:S(2)}) copy-start(f32[6,64,64]{2,1,0:T(8,128)} %param.15) | copy-start | bytes 294916
  0.0 12.0 %copy-start.3 = (f32[2,4,1024]{2,1,0:T(4,128)S(1)}, f32[2,4,1024]{2,1,0:T(4,128)}, u32[]{:S(2)}) copy-start(f32[2,4,1024]{2,1,0:T(4,128)} %param.13) | copy-start | bytes 98308
  0.0 12.0 %copy-start.2 = (f32[4,1024]{1,0:T(4,128)S(1)}, f32[4,1024]{1,0:T(4,128)}, u32[]{:S(2)}) copy-start(f32[4,1024]{1,0:T(4,128)} %scale_ref.1) | copy-start | bytes 49156
  0.0 12.0 %copy-start.5 = (f32[4,1024]{1,0:T(4,128)S(1)}, f32[4,1024]{1,0:T(4,128)}, u32[]{:S(2)}) copy-start(f32[4,1024]{1,0:T(4,128)} %param.14) | copy-start | bytes 49156
  1.5 15.1 %collective-permute-start.1 = (f32[4,4,64,1]{3,2,1,0:T(8,128)S(1)}, f32[4,4,64,1]{3,2,1,0:T(8,128)S(1)}, u32[]{:S(2)}, u32[]{:S(2)}) collective-permute-start(f32[4,4,64,1]{3,2,1,0:T(8,128)S(1)} %get-tuple-element.8), channel_id=1, source_target_pairs={{1,0},{2,1},{3,2},{5,4},{6,5},{7,6},{9,8},{10,9},{11,10},{13,12},{... | collective-permute-start | bytes 12296 | tf_op jit(solution)/shard_map/ppermute | solution.py:23
  2.8 26.8 %collective-permute-start = (f32[4,4,64,1]{3,2,1,0:T(8,128)S(1)}, f32[4,4,64,1]{3,2,1,0:T(8,128)S(1)}, u32[]{:S(2)}, u32[]{:S(2)}) collective-permute-start(f32[4,4,64,1]{3,2,1,0:T(8,128)S(1)} %get-tuple-element.7), channel_id=1, source_target_pairs={{0,1},{1,2},{2,3},{4,5},{5,6},{6,7},{8,9},{9,10},{10,11},{12,13},{... | collective-permute-start | bytes 12296 | tf_op jit(solution)/shard_map/ppermute | solution.py:20
  19.9 9.8 %copy-start.1 = (f32[4,4,64,1024]{3,2,1,0:T(8,128)S(1)}, f32[4,4,64,1024]{3,2,1,0:T(8,128)}, u32[]{:S(2)}) copy-start(f32[4,4,64,1024]{3,2,1,0:T(8,128)} %param.10) | copy-start | bytes 12582916
  40.1 4.1 %copy-start.4 = (f32[64,64]{1,0:T(8,128)S(1)}, f32[64,64]{1,0:T(8,128)}, u32[]{:S(2)}) copy-start(f32[64,64]{1,0:T(8,128)} %param.17) | copy-start | bytes 49156
  40.1 4.1 %copy-start.6 = (f32[4,4,64,1024]{3,2,1,0:T(8,128)S(1)}, f32[4,4,64,1024]{3,2,1,0:T(8,128)}, u32[]{:S(2)}) copy-start(f32[4,4,64,1024]{3,2,1,0:T(8,128)} %param.9) | copy-start | bytes 12582916

commit v11 on v10

--- a/solution.py
+++ b/solution.py
@@ -370,7 +370,7 @@
             backward_rows(k, tracer, cols, ext_small_ref, ext_part, ext_out)
             copy_back(k - own).start()
 
-    lead = jnp.minimum(jnp.maximum(((2 * (length - 1) - 2 * me) * 17) // 6, 1), count)
+    lead = jnp.minimum(jnp.maximum((2 * (length - 1) - 2 * me) * 4, 1), count)
     tail = 2 * count - lead
 
     def step(s, carry):

time: 344 us -> 344 us (level)
  no operation moved by 1% of the time
where the time goes in v11:
time: 344 us; the launch traced here: 343 us
  Pallas kernels  289 us (84%)
  matrix products  32.9 us (10%)
  local copies, waits for them, and re-layouts  12.6 us (4%)
  starting transfers between devices  4.35 us (1%)
    pallas_call x1, Pallas kernels, both_sweeps(): pl.pallas_call(functools.partial(both_kernel, length, width, lend), out_s...  289 us
    dot_general x8, matrix products, typed_product(): jnp.einsum('tpq,rqw->trpw', blocks_table, state_in, precision=fast)  26.1 us
    unnamed x16, local copies, waits for them, and re-layouts  7.43 us
  transfers between devices with their start and end apart: 2, of which 0 were waited for; matrix products, arithmetic and copies ran while one was open for 7% of the time, Pallas kernels for 0%

profile of v11, /device:TPU:0, one launch (start us, length us, event | category | flops | bytes accessed | tf_op | source)
XLA Modules:
  0.0 342.9 jit_solution(7691411561165016674)
XLA Ops:
  0.0 0.0 copy-start
  0.0 0.0 copy-start.3
  0.0 0.0 copy-start.2
  0.0 0.0 copy-start.5
  0.0 1.5 fusion.58
  1.5 1.3 collective-permute-start.1
  2.8 3.1 collective-permute-start
  5.8 1.0 fusion.59
  6.8 1.3 slice_bitcast_fusion.8.types_ref
  8.2 0.9 fusion.60
  9.1 1.3 fusion.39
  10.4 0.1 copy.13
  10.5 0.1 reshape.260
  10.6 0.0 copy-done
  10.7 1.1 fusion.41
  11.7 0.1 copy.12
  11.9 0.1 reshape.259
  12.0 0.0 copy-done.3
  12.0 0.0 copy-done.2
  12.0 0.0 copy-done.5
  12.0 0.6 broadcast_divide_fusion
  12.6 0.7 pad_maximum_fusion.1
  13.3 2.6 constant_dynamic-update-slice_fusion.1
  16.0 0.6 div.22.coeff_ref
  16.6 0.0 collective-permute-done.1
  16.6 3.2 fusion.4
  19.9 0.0 copy-start.1
  19.9 3.2 fusion.6
  23.1 3.2 fusion
  26.4 3.2 fusion.2
  29.6 0.0 collective-permute-done
  29.6 0.0 copy-done.1
  29.6 3.3 fusion.5
  32.9 3.3 fusion.7
  36.2 0.7 fusion.26
  36.8 3.3 fusion.1
  40.1 0.0 copy-start.4
  40.1 0.0 copy-start.6
  40.1 3.4 %fusion.3 = f32[4,64,1024]{2,1,0:T(8,128)S(1)} fusion(f32[6,1024]{1,0:T(8,128)S(1)} %fusion.47, f32[4,4,64,1024]{3,2,1,0:T(8,128)S(1)} %copy-done.1, f32[4,4,64,1]{3,2,1,0:T(8,128)S(1)} %collective-permute-done, f32[6,64,64]{2,1,0:T(8,128)S(1)} %copy-done), kind=kOutput, calls=%fused_computation.7 | convolution fusion | flops 607125504 | bytes 5369856 | tf_op jit(solution)/shard_map/tpq,rqw->trpw/dot_general | solution.py:29
  43.5 0.7 fusion.24
  44.2 0.0 copy-done.4
  44.2 0.0 copy-done.6
  44.2 4.4 %divide_bitcast_fusion.start_ref = f32[4,4,64,1024]{3,2,1,0:T(8,128)} fusion(f32[4,1024]{1,0:T(4,128)S(1)} %get-tuple-element.6, f32[4,4,64,1024]{3,2,1,0:T(8,128)S(1)} %copy-done.6, f32[1,4,64,1024]{3,2,1,0:T(8,128)S(1)} %get-tuple-element.29, f32[1,4,64,1024]{3,2,1,0:T(8,128)S(1)} %get-tuple-element.30, f32[1,4,64,1024]{3,2,1,0:T(8,128)S(1)} %get-tuple-element.31, ...), kind=kOutput, calls=%fused_computation.24 | convolution fusion | flops 407896064 | bytes 12615680 | tf_op jit(solution)/shard_map/pq,nrqc->nrpc/dot_general | solution.py:480
  48.7 289.4 %shard_map.91 = f32[4,4,64,1024]{3,2,1,0:T(8,128)} custom-call(f32[4,4,64,1024]{3,2,1,0:T(8,128)} %divide_bitcast_fusion.start_ref, s32[4,1024]{1,0:T(4,128)} %slice_bitcast_fusion.8.types_ref, f32[4,1024]{1,0:T(4,128)} %div.22.coeff_ref, f32[4,1024]{1,0:T(4,128)} %scale_ref.1, f32[4,1024]{1,0:T(4,128)} %get-tuple-element.5.inverse_ref, ...), custom_call_target="tpu_custom_call" | custom-call | tf_op jit(solution)/shard_map/pallas_call | solution.py:445
  338.1 4.8 %copy.25 = f32[4,4,64,1024]{3,2,1,0:T(8,128)} copy(f32[4,4,64,1024]{3,2,1,0:T(8,128)} %shard_map.91) | data formatting | bytes 8388608
  (11 shorter events, 0.1 us)
Async XLA Ops:
  0.0 10.6 %copy-start = (f32[6,64,64]{2,1,0:T(8,128)S(1)}, f32[6,64,64]{2,1,0:T(8,128)}, u32[]{:S(2)}) copy-start(f32[6,64,64]{2,1,0:T(8,128)} %param.15) | copy-start | bytes 294916
  0.0 12.0 %copy-start.3 = (f32[2,4,1024]{2,1,0:T(4,128)S(1)}, f32[2,4,1024]{2,1,0:T(4,128)}, u32[]{:S(2)}) copy-start(f32[2,4,1024]{2,1,0:T(4,128)} %param.13) | copy-start | bytes 98308
  0.0 12.0 %copy-start.2 = (f32[4,1024]{1,0:T(4,128)S(1)}, f32[4,1024]{1,0:T(4,128)}, u32[]{:S(2)}) copy-start(f32[4,1024]{1,0:T(4,128)} %scale_ref.1) | copy-start | bytes 49156
  0.0 12.0 %copy-start.5 = (f32[4,1024]{1,0:T(4,128)S(1)}, f32[4,1024]{1,0:T(4,128)}, u32[]{:S(2)}) copy-start(f32[4,1024]{1,0:T(4,128)} %param.14) | copy-start | bytes 49156
  1.5 15.1 %collective-permute-start.1 = (f32[4,4,64,1]{3,2,1,0:T(8,128)S(1)}, f32[4,4,64,1]{3,2,1,0:T(8,128)S(1)}, u32[]{:S(2)}, u32[]{:S(2)}) collective-permute-start(f32[4,4,64,1]{3,2,1,0:T(8,128)S(1)} %get-tuple-element.8), channel_id=1, source_target_pairs={{1,0},{2,1},{3,2},{5,4},{6,5},{7,6},{9,8},{10,9},{11,10},{13,12},{... | collective-permute-start | bytes 12296 | tf_op jit(solution)/shard_map/ppermute | solution.py:23
  2.8 26.8 %collective-permute-start = (f32[4,4,64,1]{3,2,1,0:T(8,128)S(1)}, f32[4,4,64,1]{3,2,1,0:T(8,128)S(1)}, u32[]{:S(2)}, u32[]{:S(2)}) collective-permute-start(f32[4,4,64,1]{3,2,1,0:T(8,128)S(1)} %get-tuple-element.7), channel_id=1, source_target_pairs={{0,1},{1,2},{2,3},{4,5},{5,6},{6,7},{8,9},{9,10},{10,11},{12,13},{... | collective-permute-start | bytes 12296 | tf_op jit(solution)/shard_map/ppermute | solution.py:20
  19.9 9.8 %copy-start.1 = (f32[4,4,64,1024]{3,2,1,0:T(8,128)S(1)}, f32[4,4,64,1024]{3,2,1,0:T(8,128)}, u32[]{:S(2)}) copy-start(f32[4,4,64,1024]{3,2,1,0:T(8,128)} %param.10) | copy-start | bytes 12582916
  40.1 4.1 %copy-start.4 = (f32[64,64]{1,0:T(8,128)S(1)}, f32[64,64]{1,0:T(8,128)}, u32[]{:S(2)}) copy-start(f32[64,64]{1,0:T(8,128)} %param.17) | copy-start | bytes 49156
  40.1 4.1 %copy-start.6 = (f32[4,4,64,1024]{3,2,1,0:T(8,128)S(1)}, f32[4,4,64,1024]{3,2,1,0:T(8,128)}, u32[]{:S(2)}) copy-start(f32[4,4,64,1024]{3,2,1,0:T(8,128)} %param.9) | copy-start | bytes 12582916

commit v12 on v11

--- a/solution.py
+++ b/solution.py
@@ -219,7 +219,7 @@
 
 
 def both_kernel(length, width, lend, start_ref, types_ref, coeff_ref, scale_ref, inverse_ref, up_ref, down_ref,
-                out_ref, part_ref, ext_start, ext_types, ext_small, ext_part, ext_out, returned,
+                out_ref, part_ref, ext_start, ext_types, ext_small, ext_part, ext_out,
                 recv_f, send_f, recv_b, send_b, sems, lend_sems, back_sems):
     me = lax.axis_index("stream")
     side = lax.axis_index("span")
@@ -293,8 +293,9 @@
     def copy_back(j):
         tracer = j % sets
         cols = pl.ds(pl.multiple_of((j // sets) * width, width), width)
+        home = pl.ds(pl.multiple_of(first_cols + (j // sets) * width, width), width)
         return pltpu.make_async_remote_copy(
-            src_ref=ext_out.at[:, tracer, :, cols], dst_ref=returned.at[:, tracer, :, cols],
+            src_ref=ext_out.at[:, tracer, :, cols], dst_ref=out_ref.at[:, tracer, :, home],
             send_sem=back_sems.at[0, j], recv_sem=back_sems.at[1, j], device_id={"span": partner},
             device_id_type=pl.DeviceIdType.MESH)
 
@@ -426,7 +427,6 @@
         for copy in lend_copies():
             copy.wait_send()
         lax.fori_loop(0, lent, take_back, 0)
-        out_ref[:, :, :, lend_cols] = returned[...]
 
     @pl.when(jnp.logical_not(lender))
     def _():
@@ -454,7 +454,6 @@
             pltpu.VMEM((3, rows, lend * width), jnp.float32),
             pltpu.VMEM(ext_shape, jnp.float32),
             pltpu.VMEM(ext_shape, jnp.float32),
-            pltpu.VMEM(ext_shape, jnp.float32),
             pltpu.VMEM((blocks, dof, width), jnp.float32),
             pltpu.VMEM((blocks, dof, width), jnp.float32),
             pltpu.VMEM((blocks, dof, width), jnp.float32),

time: 344 us -> 344 us (level)
  no operation moved by 1% of the time
where the time goes in v12:
time: 344 us; the launch traced here: 343 us
  Pallas kernels  289 us (84%)
  matrix products  32.9 us (10%)
  local copies, waits for them, and re-layouts  12.6 us (4%)
  starting transfers between devices  4.35 us (1%)
    pallas_call x1, Pallas kernels, both_sweeps(): pl.pallas_call(functools.partial(both_kernel, length, width, lend), out_s...  289 us
    dot_general x8, matrix products, typed_product(): jnp.einsum('tpq,rqw->trpw', blocks_table, state_in, precision=fast)  26.1 us
    unnamed x16, local copies, waits for them, and re-layouts  7.43 us
  transfers between devices with their start and end apart: 2, of which 0 were waited for; matrix products, arithmetic and copies ran while one was open for 7% of the time, Pallas kernels for 0%

profile of v12, /device:TPU:0, one launch (start us, length us, event | category | flops | bytes accessed | tf_op | source)
XLA Modules:
  0.0 342.7 jit_solution(1622240748576318264)
XLA Ops:
  0.0 0.0 copy-start
  0.0 0.0 copy-start.3
  0.0 0.0 copy-start.2
  0.0 0.0 copy-start.5
  0.0 1.5 fusion.58
  1.5 1.3 collective-permute-start.1
  2.8 3.1 collective-permute-start
  5.8 1.0 fusion.59
  6.8 1.3 slice_bitcast_fusion.8.types_ref
  8.2 0.9 fusion.60
  9.1 1.3 fusion.39
  10.4 0.1 copy.13
  10.5 0.1 reshape.260
  10.6 0.0 copy-done
  10.7 1.1 fusion.41
  11.7 0.1 copy.12
  11.9 0.1 reshape.259
  12.0 0.0 copy-done.3
  12.0 0.0 copy-done.2
  12.0 0.0 copy-done.5
  12.0 0.6 broadcast_divide_fusion
  12.6 0.7 pad_maximum_fusion.1
  13.3 2.6 constant_dynamic-update-slice_fusion.1
  16.0 0.6 div.22.coeff_ref
  16.6 0.0 collective-permute-done.1
  16.6 3.2 fusion.4
  19.9 0.0 copy-start.1
  19.9 3.2 fusion.6
  23.1 3.2 fusion
  26.4 3.2 fusion.2
  29.6 0.0 collective-permute-done
  29.6 0.0 copy-done.1
  29.6 3.3 fusion.5
  32.9 3.3 fusion.7
  36.2 0.7 fusion.26
  36.8 3.3 fusion.1
  40.1 0.0 copy-start.4
  40.1 0.0 copy-start.6
  40.1 3.4 %fusion.3 = f32[4,64,1024]{2,1,0:T(8,128)S(1)} fusion(f32[6,1024]{1,0:T(8,128)S(1)} %fusion.47, f32[4,4,64,1024]{3,2,1,0:T(8,128)S(1)} %copy-done.1, f32[4,4,64,1]{3,2,1,0:T(8,128)S(1)} %collective-permute-done, f32[6,64,64]{2,1,0:T(8,128)S(1)} %copy-done), kind=kOutput, calls=%fused_computation.7 | convolution fusion | flops 607125504 | bytes 5369856 | tf_op jit(solution)/shard_map/tpq,rqw->trpw/dot_general | solution.py:29
  43.5 0.7 fusion.24
  44.2 0.0 copy-done.4
  44.2 0.0 copy-done.6
  44.2 4.4 %divide_bitcast_fusion.start_ref = f32[4,4,64,1024]{3,2,1,0:T(8,128)} fusion(f32[4,1024]{1,0:T(4,128)S(1)} %get-tuple-element.6, f32[4,4,64,1024]{3,2,1,0:T(8,128)S(1)} %copy-done.6, f32[1,4,64,1024]{3,2,1,0:T(8,128)S(1)} %get-tuple-element.29, f32[1,4,64,1024]{3,2,1,0:T(8,128)S(1)} %get-tuple-element.30, f32[1,4,64,1024]{3,2,1,0:T(8,128)S(1)} %get-tuple-element.31, ...), kind=kOutput, calls=%fused_computation.24 | convolution fusion | flops 407896064 | bytes 12615680 | tf_op jit(solution)/shard_map/pq,nrqc->nrpc/dot_general | solution.py:479
  48.7 289.2 %shard_map.91 = f32[4,4,64,1024]{3,2,1,0:T(8,128)} custom-call(f32[4,4,64,1024]{3,2,1,0:T(8,128)} %divide_bitcast_fusion.start_ref, s32[4,1024]{1,0:T(4,128)} %slice_bitcast_fusion.8.types_ref, f32[4,1024]{1,0:T(4,128)} %div.22.coeff_ref, f32[4,1024]{1,0:T(4,128)} %scale_ref.1, f32[4,1024]{1,0:T(4,128)} %get-tuple-element.5.inverse_ref, ...), custom_call_target="tpu_custom_call" | custom-call | tf_op jit(solution)/shard_map/pallas_call | solution.py:445
  337.9 4.8 %copy.25 = f32[4,4,64,1024]{3,2,1,0:T(8,128)} copy(f32[4,4,64,1024]{3,2,1,0:T(8,128)} %shard_map.91) | data formatting | bytes 8388608
  (11 shorter events, 0.1 us)
Async XLA Ops:
  0.0 10.6 %copy-start = (f32[6,64,64]{2,1,0:T(8,128)S(1)}, f32[6,64,64]{2,1,0:T(8,128)}, u32[]{:S(2)}) copy-start(f32[6,64,64]{2,1,0:T(8,128)} %param.15) | copy-start | bytes 294916
  0.0 12.0 %copy-start.3 = (f32[2,4,1024]{2,1,0:T(4,128)S(1)}, f32[2,4,1024]{2,1,0:T(4,128)}, u32[]{:S(2)}) copy-start(f32[2,4,1024]{2,1,0:T(4,128)} %param.13) | copy-start | bytes 98308
  0.0 12.0 %copy-start.2 = (f32[4,1024]{1,0:T(4,128)S(1)}, f32[4,1024]{1,0:T(4,128)}, u32[]{:S(2)}) copy-start(f32[4,1024]{1,0:T(4,128)} %scale_ref.1) | copy-start | bytes 49156
  0.0 12.0 %copy-start.5 = (f32[4,1024]{1,0:T(4,128)S(1)}, f32[4,1024]{1,0:T(4,128)}, u32[]{:S(2)}) copy-start(f32[4,1024]{1,0:T(4,128)} %param.14) | copy-start | bytes 49156
  1.5 15.1 %collective-permute-start.1 = (f32[4,4,64,1]{3,2,1,0:T(8,128)S(1)}, f32[4,4,64,1]{3,2,1,0:T(8,128)S(1)}, u32[]{:S(2)}, u32[]{:S(2)}) collective-permute-start(f32[4,4,64,1]{3,2,1,0:T(8,128)S(1)} %get-tuple-element.8), channel_id=1, source_target_pairs={{1,0},{2,1},{3,2},{5,4},{6,5},{7,6},{9,8},{10,9},{11,10},{13,12},{... | collective-permute-start | bytes 12296 | tf_op jit(solution)/shard_map/ppermute | solution.py:23
  2.8 26.8 %collective-permute-start = (f32[4,4,64,1]{3,2,1,0:T(8,128)S(1)}, f32[4,4,64,1]{3,2,1,0:T(8,128)S(1)}, u32[]{:S(2)}, u32[]{:S(2)}) collective-permute-start(f32[4,4,64,1]{3,2,1,0:T(8,128)S(1)} %get-tuple-element.7), channel_id=1, source_target_pairs={{0,1},{1,2},{2,3},{4,5},{5,6},{6,7},{8,9},{9,10},{10,11},{12,13},{... | collective-permute-start | bytes 12296 | tf_op jit(solution)/shard_map/ppermute | solution.py:20
  19.9 9.8 %copy-start.1 = (f32[4,4,64,1024]{3,2,1,0:T(8,128)S(1)}, f32[4,4,64,1024]{3,2,1,0:T(8,128)}, u32[]{:S(2)}) copy-start(f32[4,4,64,1024]{3,2,1,0:T(8,128)} %param.10) | copy-start | bytes 12582916
  40.1 4.1 %copy-start.4 = (f32[64,64]{1,0:T(8,128)S(1)}, f32[64,64]{1,0:T(8,128)}, u32[]{:S(2)}) copy-start(f32[64,64]{1,0:T(8,128)} %param.17) | copy-start | bytes 49156
  40.1 4.1 %copy-start.6 = (f32[4,4,64,1024]{3,2,1,0:T(8,128)S(1)}, f32[4,4,64,1024]{3,2,1,0:T(8,128)}, u32[]{:S(2)}) copy-start(f32[4,4,64,1024]{3,2,1,0:T(8,128)} %param.9) | copy-start | bytes 12582916

commit v13 on v12

--- a/solution.py
+++ b/solution.py
@@ -218,9 +218,13 @@
     )(start, types, coeff, denom, table)
 
 
-def both_kernel(length, width, lend, start_ref, types_ref, coeff_ref, scale_ref, inverse_ref, up_ref, down_ref,
+def both_kernel(length, width, lend, start_ref, faces_ref, coeff_ref, scale_ref, inverse_ref, tables_ref,
                 out_ref, part_ref, ext_start, ext_types, ext_small, ext_part, ext_out,
                 recv_f, send_f, recv_b, send_b, sems, lend_sems, back_sems):
+    types_ref = faces_ref.at[0]
+    half = tables_ref.shape[1] // 2
+    up_ref = tables_ref.at[:, pl.ds(0, half)]
+    down_ref = tables_ref.at[:, pl.ds(half, half)]
     me = lax.axis_index("stream")
     side = lax.axis_index("span")
     lender = side % 2 == 0
@@ -433,7 +437,7 @@
         lax.fori_loop(0, lent, drain_back, 0)
 
 
-def both_sweeps(width, start, types, coeff, scale, inverse, up_table, down_table):
+def both_sweeps(width, start, types, coeff, scale, inverse, tables):
     rows, tracers, dof, columns = start.shape
     groups = columns // width
     lend = max(1, groups * 5 // 8)
@@ -445,7 +449,7 @@
     return pl.pallas_call(
         functools.partial(both_kernel, length, width, lend),
         out_shape=jax.ShapeDtypeStruct(start.shape, jnp.float32),
-        in_specs=[pl.BlockSpec(memory_space=vmem)] * 7,
+        in_specs=[pl.BlockSpec(memory_space=vmem)] * 6,
         out_specs=pl.BlockSpec(memory_space=vmem),
         scratch_shapes=[
             pltpu.VMEM(start.shape, jnp.float32),
@@ -465,7 +469,7 @@
         compiler_params=pltpu.CompilerParams(
             collective_id=0, has_side_effects=True, vmem_limit_bytes=60 * 1024 * 1024
         ),
-    )(start, types, coeff, scale, inverse, up_table, down_table)
+    )(start, types, coeff, scale, inverse, tables)
 
 
 def per_device(
@@ -480,10 +484,19 @@
     start = start / denominator[:, None, None, :]
     coeff = stream_scale / denominator
     inverse = 1.0 / denominator
-    up_table = split_masked_table(jnp.einsum("pq,tqs->tps", diag_inverse, up_blocks, precision=precise))
-    down_table = split_masked_table(jnp.einsum("pq,tqs->tps", diag_inverse, down_blocks, precision=precise))
-    small = [face_types[0], coeff, stream_scale, inverse]
-    return both_sweeps(LANES, start, *small, up_table, down_table)
+    both = jnp.einsum("pq,tqs->tps", diag_inverse, jnp.concatenate([up_blocks, down_blocks]), precision=precise)
+    kinds = up_blocks.shape[0]
+    flat = jnp.transpose(both, (1, 0, 2)).reshape(dof, 2 * kinds * dof)
+    high = lax.reduce_precision(flat, exponent_bits=8, mantissa_bits=7)
+    low = (flat - high).astype(jnp.bfloat16)
+    high = high.astype(jnp.bfloat16)
+    width = kinds * dof
+    pieces = []
+    for part in (slice(0, width), slice(width, 2 * width)):
+        pieces += [high[:, part], low[:, part], high[:, part]]
+    tables = jnp.concatenate(pieces, axis=1)
+    small = [face_types, coeff, stream_scale, inverse]
+    return both_sweeps(LANES, start, *small, tables)
 
 
 def solution(mesh):

time: 344 us -> 342 us (level)
    unnamed x16 -> x24, local copies, waits for them, and re-layouts: 7.43 us -> 9.59 us
  transfers between devices with their start and end apart: 2 -> 2, of which waited for: 0 -> 0; matrix products, arithmetic and copies ran while one was open for 7% -> 6% of each run, Pallas kernels for 0% -> 0%
where the time goes in v13:
time: 342 us; the launch traced here: 341 us
  Pallas kernels  289 us (85%)
  matrix products  31 us (9%)
  local copies, waits for them, and re-layouts  13.1 us (4%)
  starting transfers between devices  4.35 us (1%)
    pallas_call x1, Pallas kernels, both_sweeps(): pl.pallas_call(functools.partial(both_kernel, length, width, lend), out_s...  289 us
    dot_general x8, matrix products, typed_product(): jnp.einsum('tpq,rqw->trpw', blocks_table, state_in, precision=fast)  26.1 us
    unnamed x24, local copies, waits for them, and re-layouts  9.59 us
  transfers between devices with their start and end apart: 2, of which 0 were waited for; matrix products, arithmetic and copies ran while one was open for 6% of the time, Pallas kernels for 0%

profile of v13, /device:TPU:0, one launch (start us, length us, event | category | flops | bytes accessed | tf_op | source)
XLA Modules:
  0.0 340.6 jit_solution(11676603148631911381)
XLA Ops:
  0.0 0.0 copy-start
  0.0 0.0 copy-start.5
  0.0 0.0 copy-start.4
  0.0 0.0 copy-start.6
  0.0 1.5 fusion.59
  1.5 1.3 collective-permute-start.1
  2.8 3.1 collective-permute-start
  5.8 1.0 fusion.60
  6.8 0.9 fusion.61
  7.8 1.0 copy.13
  8.9 1.0 copy.14
  9.9 0.0 copy-done
  9.9 0.5 fusion.28
  10.4 0.1 copy.25
  10.7 0.0 copy-done.5
  10.7 0.0 copy-done.4
  10.7 0.0 copy-done.6
  10.7 0.0 copy-start.3
  10.7 0.7 broadcast_divide_fusion
  11.4 0.0 copy-start.2
  11.4 2.6 constant_dynamic-update-slice_fusion.1
  14.0 0.6 div.22.coeff_ref
  14.6 0.0 collective-permute-done.1
  14.7 0.0 copy-done.3
  14.7 0.0 copy-done.2
  14.7 3.2 fusion.4
  18.0 0.0 copy-start.1
  18.0 3.2 fusion.6
  21.2 3.2 fusion
  24.5 3.2 fusion.2
  27.7 0.0 collective-permute-done
  27.7 0.0 copy-done.1
  27.7 3.2 fusion.5
  31.0 3.2 fusion.7
  34.2 0.7 fusion.26
  34.9 3.2 fusion.1
  38.2 0.0 copy-start.7
  38.2 3.4 %fusion.3 = f32[4,64,1024]{2,1,0:T(8,128)S(1)} fusion(f32[6,1024]{1,0:T(8,128)S(1)} %fusion.47, f32[4,4,64,1024]{3,2,1,0:T(8,128)S(1)} %copy-done.1, f32[4,4,64,1]{3,2,1,0:T(8,128)S(1)} %collective-permute-done, f32[6,64,64]{2,1,0:T(8,128)S(1)} %copy-done.2), kind=kOutput, calls=%fused_computation.7 | convolution fusion | flops 607125504 | bytes 5369856 | tf_op jit(solution)/shard_map/tpq,rqw->trpw/dot_general | solution.py:29
  41.6 0.5 fusion.24
  42.2 0.0 copy-done.7
  42.2 4.4 %divide_bitcast_fusion.start_ref = f32[4,4,64,1024]{3,2,1,0:T(8,128)} fusion(f32[4,1024]{1,0:T(4,128)S(1)} %get-tuple-element.6, f32[4,4,64,1024]{3,2,1,0:T(8,128)S(1)} %copy-done.7, f32[1,4,64,1024]{3,2,1,0:T(8,128)S(1)} %get-tuple-element.27, f32[1,4,64,1024]{3,2,1,0:T(8,128)S(1)} %get-tuple-element.28, f32[1,4,64,1024]{3,2,1,0:T(8,128)S(1)} %get-tuple-element.29, ...), kind=kOutput, calls=%fused_computation.24 | convolution fusion | flops 407896064 | bytes 12615680 | tf_op jit(solution)/shard_map/pq,nrqc->nrpc/dot_general | solution.py:483
  46.6 289.2 %shard_map.91 = f32[4,4,64,1024]{3,2,1,0:T(8,128)} custom-call(f32[4,4,64,1024]{3,2,1,0:T(8,128)} %divide_bitcast_fusion.start_ref, s32[3,4,1024]{2,1,0:T(4,128)} %faces_ref.1, f32[4,1024]{1,0:T(4,128)} %div.22.coeff_ref, f32[4,1024]{1,0:T(4,128)} %scale_ref.1, f32[4,1024]{1,0:T(4,128)} %get-tuple-element.5.inverse_ref, bf16[64,2304]{1,0:T(8,128)(2,1)} %copy-done.3), custom_call_target="tpu_custom_call" | custom-call | tf_op jit(solution)/shard_map/pallas_call | solution.py:449
  335.9 4.8 %copy.32 = f32[4,4,64,1024]{3,2,1,0:T(8,128)} copy(f32[4,4,64,1024]{3,2,1,0:T(8,128)} %shard_map.91) | data formatting | bytes 8388608
  (15 shorter events, 0.2 us)
Async XLA Ops:
  0.0 9.9 %copy-start = (f32[64,64]{1,0:T(8,128)S(1)}, f32[64,64]{1,0:T(8,128)}, u32[]{:S(2)}) copy-start(f32[64,64]{1,0:T(8,128)} %param.17) | copy-start | bytes 49156
  0.0 10.7 %copy-start.5 = (f32[2,4,1024]{2,1,0:T(4,128)S(1)}, f32[2,4,1024]{2,1,0:T(4,128)}, u32[]{:S(2)}) copy-start(f32[2,4,1024]{2,1,0:T(4,128)} %param.13) | copy-start | bytes 98308
  0.0 10.7 %copy-start.4 = (f32[4,1024]{1,0:T(4,128)S(1)}, f32[4,1024]{1,0:T(4,128)}, u32[]{:S(2)}) copy-start(f32[4,1024]{1,0:T(4,128)} %scale_ref.1) | copy-start | bytes 49156
  0.0 10.7 %copy-start.6 = (f32[4,1024]{1,0:T(4,128)S(1)}, f32[4,1024]{1,0:T(4,128)}, u32[]{:S(2)}) copy-start(f32[4,1024]{1,0:T(4,128)} %param.14) | copy-start | bytes 49156
  1.5 13.2 %collective-permute-start.1 = (f32[4,4,64,1]{3,2,1,0:T(8,128)S(1)}, f32[4,4,64,1]{3,2,1,0:T(8,128)S(1)}, u32[]{:S(2)}, u32[]{:S(2)}) collective-permute-start(f32[4,4,64,1]{3,2,1,0:T(8,128)S(1)} %get-tuple-element.8), channel_id=1, source_target_pairs={{1,0},{2,1},{3,2},{5,4},{6,5},{7,6},{9,8},{10,9},{11,10},{13,12},{... | collective-permute-start | bytes 12296 | tf_op jit(solution)/shard_map/ppermute | solution.py:23
  2.8 25.0 %collective-permute-start = (f32[4,4,64,1]{3,2,1,0:T(8,128)S(1)}, f32[4,4,64,1]{3,2,1,0:T(8,128)S(1)}, u32[]{:S(2)}, u32[]{:S(2)}) collective-permute-start(f32[4,4,64,1]{3,2,1,0:T(8,128)S(1)} %get-tuple-element.7), channel_id=1, source_target_pairs={{0,1},{1,2},{2,3},{4,5},{5,6},{6,7},{8,9},{9,10},{10,11},{12,13},{... | collective-permute-start | bytes 12296 | tf_op jit(solution)/shard_map/ppermute | solution.py:20
  10.7 4.0 %copy-start.3 = (bf16[64,2304]{1,0:T(8,128)(2,1)}, bf16[64,2304]{1,0:T(8,128)(2,1)S(1)}, u32[]{:S(2)}) copy-start(bf16[64,2304]{1,0:T(8,128)(2,1)S(1)} %slice_dynamic-update-slice_fusion.tables_ref) | copy-start | bytes 884740
  11.4 3.3 copy-start.2
  18.0 9.8 %copy-start.1 = (f32[4,4,64,1024]{3,2,1,0:T(8,128)S(1)}, f32[4,4,64,1024]{3,2,1,0:T(8,128)}, u32[]{:S(2)}) copy-start(f32[4,4,64,1024]{3,2,1,0:T(8,128)} %param.10) | copy-start | bytes 12582916
  38.2 4.0 %copy-start.7 = (f32[4,4,64,1024]{3,2,1,0:T(8,128)S(1)}, f32[4,4,64,1024]{3,2,1,0:T(8,128)}, u32[]{:S(2)}) copy-start(f32[4,4,64,1024]{3,2,1,0:T(8,128)} %param.9) | copy-start | bytes 12582916

commit v14 on v13

--- a/solution.py
+++ b/solution.py
@@ -218,10 +218,12 @@
     )(start, types, coeff, denom, table)
 
 
-def both_kernel(length, width, lend, start_ref, faces_ref, coeff_ref, scale_ref, inverse_ref, tables_ref,
+def both_kernel(length, width, lend, start_ref, faces_ref, ratios_ref, scale_ref, tables_ref,
                 out_ref, part_ref, ext_start, ext_types, ext_small, ext_part, ext_out,
                 recv_f, send_f, recv_b, send_b, sems, lend_sems, back_sems):
     types_ref = faces_ref.at[0]
+    coeff_ref = ratios_ref.at[0]
+    inverse_ref = ratios_ref.at[1]
     half = tables_ref.shape[1] // 2
     up_ref = tables_ref.at[:, pl.ds(0, half)]
     down_ref = tables_ref.at[:, pl.ds(half, half)]
@@ -437,7 +439,7 @@
         lax.fori_loop(0, lent, drain_back, 0)
 
 
-def both_sweeps(width, start, types, coeff, scale, inverse, tables):
+def both_sweeps(width, start, types, ratios, scale, tables):
     rows, tracers, dof, columns = start.shape
     groups = columns // width
     lend = max(1, groups * 5 // 8)
@@ -449,7 +451,7 @@
     return pl.pallas_call(
         functools.partial(both_kernel, length, width, lend),
         out_shape=jax.ShapeDtypeStruct(start.shape, jnp.float32),
-        in_specs=[pl.BlockSpec(memory_space=vmem)] * 6,
+        in_specs=[pl.BlockSpec(memory_space=vmem)] * 5,
         out_specs=pl.BlockSpec(memory_space=vmem),
         scratch_shapes=[
             pltpu.VMEM(start.shape, jnp.float32),
@@ -469,7 +471,7 @@
         compiler_params=pltpu.CompilerParams(
             collective_id=0, has_side_effects=True, vmem_limit_bytes=60 * 1024 * 1024
         ),
-    )(start, types, coeff, scale, inverse, tables)
+    )(start, types, ratios, scale, tables)
 
 
 def per_device(
@@ -482,8 +484,7 @@
     span_terms = span_block(padded, face_types, span_scale, up_blocks, 0, columns)
     start = jnp.einsum("pq,nrqc->nrpc", diag_inverse, rhs - span_terms, precision=fast)
     start = start / denominator[:, None, None, :]
-    coeff = stream_scale / denominator
-    inverse = 1.0 / denominator
+    ratios = jnp.stack([stream_scale, jnp.ones_like(stream_scale)]) / denominator
     both = jnp.einsum("pq,tqs->tps", diag_inverse, jnp.concatenate([up_blocks, down_blocks]), precision=precise)
     kinds = up_blocks.shape[0]
     flat = jnp.transpose(both, (1, 0, 2)).reshape(dof, 2 * kinds * dof)
@@ -495,7 +496,7 @@
     for part in (slice(0, width), slice(width, 2 * width)):
         pieces += [high[:, part], low[:, part], high[:, part]]
     tables = jnp.concatenate(pieces, axis=1)
-    small = [face_types, coeff, stream_scale, inverse]
+    small = [face_types, ratios, stream_scale]
     return both_sweeps(LANES, start, *small, tables)
 
 

time: 342 us -> 342 us (level)
  no operation moved by 1% of the time
where the time goes in v14:
time: 342 us; the launch traced here: 340 us
  Pallas kernels  289 us (85%)
  matrix products  31 us (9%)
  local copies, waits for them, and re-layouts  13.1 us (4%)
  starting transfers between devices  4.35 us (1%)
    pallas_call x1, Pallas kernels, both_sweeps(): pl.pallas_call(functools.partial(both_kernel, length, width, lend), out_s...  289 us
    dot_general x8, matrix products, typed_product(): jnp.einsum('tpq,rqw->trpw', blocks_table, state_in, precision=fast)  26.1 us
    unnamed x24, local copies, waits for them, and re-layouts  9.59 us
  transfers between devices with their start and end apart: 2, of which 0 were waited for; matrix products, arithmetic and copies ran while one was open for 6% of the time, Pallas kernels for 0%

profile of v14, /device:TPU:0, one launch (start us, length us, event | category | flops | bytes accessed | tf_op | source)
XLA Modules:
  0.0 340.1 jit_solution(16383982460522538436)
XLA Ops:
  0.0 0.0 copy-start
  0.0 0.0 copy-start.5
  0.0 0.0 copy-start.4
  0.0 0.0 copy-start.6
  0.0 1.5 fusion.58
  1.5 1.3 collective-permute-start.1
  2.8 3.1 collective-permute-start
  5.8 1.0 fusion.59
  6.8 0.9 fusion.60
  7.8 1.0 copy.13
  8.9 1.0 copy.14
  9.9 0.0 copy-done
  9.9 0.5 fusion.28
  10.4 0.1 copy.25
  10.7 0.0 copy-done.5
  10.7 0.0 copy-done.4
  10.7 0.0 copy-done.6
  10.7 0.0 copy-start.3
  10.7 0.7 pad_divide_fusion.ratios_ref
  11.4 0.0 copy-start.2
  11.4 2.6 constant_dynamic-update-slice_fusion.1
  14.1 0.0 collective-permute-done.1
  14.1 0.0 copy-done.3
  14.1 0.0 copy-done.2
  14.1 3.2 fusion.4
  17.4 0.0 copy-start.1
  17.4 3.2 fusion.6
  20.7 3.2 fusion
  23.9 3.2 fusion.2
  27.2 0.0 collective-permute-done
  27.2 0.0 copy-done.1
  27.2 3.2 fusion.5
  30.4 3.2 fusion.7
  33.7 0.7 fusion.26
  34.4 3.2 fusion.1
  37.6 0.0 copy-start.7
  37.6 3.4 %fusion.3 = f32[4,64,1024]{2,1,0:T(8,128)S(1)} fusion(f32[6,1024]{1,0:T(8,128)S(1)} %fusion.47, f32[4,4,64,1024]{3,2,1,0:T(8,128)S(1)} %copy-done.1, f32[4,4,64,1]{3,2,1,0:T(8,128)S(1)} %collective-permute-done, f32[6,64,64]{2,1,0:T(8,128)S(1)} %copy-done.2), kind=kOutput, calls=%fused_computation.7 | convolution fusion | flops 607125504 | bytes 5369856 | tf_op jit(solution)/shard_map/tpq,rqw->trpw/dot_general | solution.py:29
  41.0 0.5 fusion.24
  41.6 0.0 copy-done.7
  41.6 4.4 %divide_bitcast_fusion.start_ref = f32[4,4,64,1024]{3,2,1,0:T(8,128)} fusion(f32[4,1024]{1,0:T(4,128)S(1)} %fusion.51, f32[4,4,64,1024]{3,2,1,0:T(8,128)S(1)} %copy-done.7, f32[1,4,64,1024]{3,2,1,0:T(8,128)S(1)} %get-tuple-element.25, f32[1,4,64,1024]{3,2,1,0:T(8,128)S(1)} %get-tuple-element.26, f32[1,4,64,1024]{3,2,1,0:T(8,128)S(1)} %get-tuple-element.27, ...), kind=kOutput, calls=%fused_computation.24 | convolution fusion | flops 407896064 | bytes 12615680 | tf_op jit(solution)/shard_map/pq,nrqc->nrpc/dot_general | solution.py:485
  46.0 289.2 %shard_map.91 = f32[4,4,64,1024]{3,2,1,0:T(8,128)} custom-call(f32[4,4,64,1024]{3,2,1,0:T(8,128)} %divide_bitcast_fusion.start_ref, s32[3,4,1024]{2,1,0:T(4,128)} %faces_ref.1, f32[2,4,1024]{2,1,0:T(4,128)} %pad_divide_fusion.ratios_ref, f32[4,1024]{1,0:T(4,128)} %scale_ref.1, bf16[64,2304]{1,0:T(8,128)(2,1)} %copy-done.3), custom_call_target="tpu_custom_call" | custom-call | tf_op jit(solution)/shard_map/pallas_call | solution.py:451
  335.3 4.8 %copy.32 = f32[4,4,64,1024]{3,2,1,0:T(8,128)} copy(f32[4,4,64,1024]{3,2,1,0:T(8,128)} %shard_map.91) | data formatting | bytes 8388608
  (16 shorter events, 0.2 us)
Async XLA Ops:
  0.0 9.9 %copy-start = (f32[64,64]{1,0:T(8,128)S(1)}, f32[64,64]{1,0:T(8,128)}, u32[]{:S(2)}) copy-start(f32[64,64]{1,0:T(8,128)} %param.17) | copy-start | bytes 49156
  0.0 10.7 %copy-start.5 = (f32[2,4,1024]{2,1,0:T(4,128)S(1)}, f32[2,4,1024]{2,1,0:T(4,128)}, u32[]{:S(2)}) copy-start(f32[2,4,1024]{2,1,0:T(4,128)} %param.13) | copy-start | bytes 98308
  0.0 10.7 %copy-start.4 = (f32[4,1024]{1,0:T(4,128)S(1)}, f32[4,1024]{1,0:T(4,128)}, u32[]{:S(2)}) copy-start(f32[4,1024]{1,0:T(4,128)} %scale_ref.1) | copy-start | bytes 49156
  0.0 10.7 %copy-start.6 = (f32[4,1024]{1,0:T(4,128)S(1)}, f32[4,1024]{1,0:T(4,128)}, u32[]{:S(2)}) copy-start(f32[4,1024]{1,0:T(4,128)} %param.14) | copy-start | bytes 49156
  1.5 12.6 %collective-permute-start.1 = (f32[4,4,64,1]{3,2,1,0:T(8,128)S(1)}, f32[4,4,64,1]{3,2,1,0:T(8,128)S(1)}, u32[]{:S(2)}, u32[]{:S(2)}) collective-permute-start(f32[4,4,64,1]{3,2,1,0:T(8,128)S(1)} %get-tuple-element.6), channel_id=1, source_target_pairs={{1,0},{2,1},{3,2},{5,4},{6,5},{7,6},{9,8},{10,9},{11,10},{13,12},{... | collective-permute-start | bytes 12296 | tf_op jit(solution)/shard_map/ppermute | solution.py:23
  2.8 24.4 %collective-permute-start = (f32[4,4,64,1]{3,2,1,0:T(8,128)S(1)}, f32[4,4,64,1]{3,2,1,0:T(8,128)S(1)}, u32[]{:S(2)}, u32[]{:S(2)}) collective-permute-start(f32[4,4,64,1]{3,2,1,0:T(8,128)S(1)} %get-tuple-element.5), channel_id=1, source_target_pairs={{0,1},{1,2},{2,3},{4,5},{5,6},{6,7},{8,9},{9,10},{10,11},{12,13},{... | collective-permute-start | bytes 12296 | tf_op jit(solution)/shard_map/ppermute | solution.py:20
  10.7 3.4 %copy-start.3 = (bf16[64,2304]{1,0:T(8,128)(2,1)}, bf16[64,2304]{1,0:T(8,128)(2,1)S(1)}, u32[]{:S(2)}) copy-start(bf16[64,2304]{1,0:T(8,128)(2,1)S(1)} %slice_dynamic-update-slice_fusion.tables_ref) | copy-start | bytes 884740
  11.4 2.7 copy-start.2
  17.4 9.8 %copy-start.1 = (f32[4,4,64,1024]{3,2,1,0:T(8,128)S(1)}, f32[4,4,64,1024]{3,2,1,0:T(8,128)}, u32[]{:S(2)}) copy-start(f32[4,4,64,1024]{3,2,1,0:T(8,128)} %param.10) | copy-start | bytes 12582916
  37.6 4.0 %copy-start.7 = (f32[4,4,64,1024]{3,2,1,0:T(8,128)S(1)}, f32[4,4,64,1024]{3,2,1,0:T(8,128)}, u32[]{:S(2)}) copy-start(f32[4,4,64,1024]{3,2,1,0:T(8,128)} %param.9) | copy-start | bytes 12582916
